TPU v7x, 32 devices: a whole 2x2x4 slice. The times are simulated.
32 devices in a mesh: img: 16 (over z, x, core), row: 2 (over y).
Axes of the slice: x: 2, y: 2, z: 4, core: 2. Of those that a mesh axis runs over, the one named last changes fastest.
Arguments:
- llm_hidden: bfloat16 [8192, 6656], P('img', 'row'), may hold values from -96 to 96
- slot_start: int32 [16], P('img'), may hold values from 0 to 448
- image_group: int32 [16], replicated, may hold values from 0 to 15, each once
- timesteps: int32 [16], P('img'), may hold values from 0 to 999
- latents: float32 [16, 4, 16, 128], P('img', None, 'row'), may hold values from -6 to 6
- noise: float32 [16, 4, 16, 128], P('img', None, 'row'), may hold values from -6 to 6
- kv_weight: bfloat16 [6656, 640], P('row'), may hold values from -0.078125 to 0.078125
- in_weight: bfloat16 [3, 3, 320, 4], replicated, may hold values from -1 to 1
- res_weight: bfloat16 [3, 3, 320, 320], replicated, may hold values from -0.109375 to 0.109375
- query_weight: bfloat16 [320, 320], replicated, may hold values from -0.3125 to 0.3125
- out_weight: bfloat16 [320, 320], replicated, may hold values from -0.3125 to 0.3125
- cotangent: bfloat16 [16, 320, 16, 128], P('img', None, 'row'), may hold values from -6 to 6
Outputs:
- block_out: bfloat16 [16, 320, 16, 128], P('img', None, 'row')
- grad_hidden: bfloat16 [8192, 6656], P('img', 'row')
- grad_kv_weight: bfloat16 [6656, 640], P('row')
- grad_res_weight: bfloat16 [3, 3, 320, 320], replicated
- grad_query_weight: bfloat16 [320, 320], replicated
- grad_out_weight: bfloat16 [320, 320], replicated
Inputs may be any that keep to these rules, and one draw needn't show every extreme that they name: `slot_start`: each image's 64 condition rows lie inside its own sequence of 512 tokens. `image_group`: every group denoises exactly one image.
All inputs are finite; a program needn't handle non-finite values.
Results may differ from a plain program's by a relative error of at most 0.035.
The roundings to bfloat16 on the way count: a program that leaves them out, or rounds other values in their place, can miss the bound.
Values may be sent and summed in bfloat16 or wider, within the bound.
No kernel may reach another device: no remote copies, remote signals or barrier semaphores. Data moves between devices by JAX's collectives and lax.ppermute only.
A program may use at most 128 MiB of HBM per device.

v0:
```python
import functools
import math

import jax
import jax.numpy as jnp
from jax import lax
from jax.experimental import pallas as pl
from jax.experimental.pallas import tpu as pltpu
from jax.sharding import PartitionSpec as P


HEAD_DIM = 64
SLOTS = 64
GRID = ("img", "row")
F32 = jnp.float32
BF16 = jnp.bfloat16
VMEM = pl.BlockSpec(memory_space=pltpu.VMEM)
SMEM = pl.BlockSpec(memory_space=pltpu.SMEM)


LIMIT = 30 * 2**20


def near_core(array):
    return pltpu.with_memory_space_constraint(array, pltpu.VMEM)


def call(kernel, outs, ins, scratch=(), flops=0, scalars=0, leave=()):
    outs = [jax.ShapeDtypeStruct(shape, kind) for shape, kind in outs]
    moved = sum(math.prod(x.shape) * x.dtype.itemsize for x in [*outs, *ins])
    ins = [x if k < scalars else near_core(x) for k, x in enumerate(ins)]
    return pl.pallas_call(
        kernel,
        out_shape=[x if k in leave else pltpu.VMEM(x.shape, x.dtype) for k, x in enumerate(outs)],
        in_specs=[SMEM] * scalars + [VMEM] * (len(ins) - scalars),
        out_specs=[VMEM] * len(outs),
        scratch_shapes=list(scratch),
        cost_estimate=pl.CostEstimate(flops=flops, bytes_accessed=moved, transcendentals=0),
        compiler_params=pltpu.CompilerParams(vmem_limit_bytes=LIMIT),
    )(*ins)


def product(left, right, sides):
    return lax.dot_general(left, right, ((sides[:1], sides[1:]), ((), ())), preferred_element_type=F32)


def time_shift(timestep, channel_total):
    half_count = channel_total // 2
    frequency = jnp.exp(-math.log(10000.0) * jnp.arange(half_count, dtype=jnp.float32) / half_count)
    angles = timestep.astype(jnp.float32) * frequency
    return jnp.concatenate([jnp.cos(angles), jnp.sin(angles)])


def swap(block, mask):
    total = lax.axis_size("img") * lax.axis_size("row")
    return lax.ppermute(block, GRID, [(i, i ^ mask) for i in range(total)])


def spots_of(rows):
    image, row = lax.axis_index("img"), lax.axis_index("row")
    return {
        "image": image,
        "core": image & 1,
        "row": row,
        "square": ((image >> 1) & 1) * rows + row,
        "line": image >> 2,
        "plane": image & 3,
    }


def noisy_kernel(rows, timestep, latents, noise, noisy, *edges):
    step = timestep[0]
    index = lax.broadcasted_iota(jnp.int32, (8, 128), 0) * 128 + lax.broadcasted_iota(
        jnp.int32, (8, 128), 1
    )
    low, high = 0.00085**0.5, 0.012**0.5
    beta = (low + index.astype(F32) * ((high - low) / 999.0)) ** 2
    logs = jnp.where(index <= step, jnp.log(1.0 - jnp.where(index < 1000, beta, 0.0)), 0.0)
    total = jnp.sum(jnp.sum(logs, axis=1, keepdims=True), axis=0, keepdims=True)
    level = jnp.exp(total)
    keep, mix = jnp.sqrt(level), jnp.sqrt(1.0 - level)
    height = latents.shape[2]
    for c in range(latents.shape[1]):
        value = (keep * latents[0, c] + mix * noise[0, c]).astype(BF16).astype(F32)
        noisy[c] = value
        head, tail = value[:2].astype(BF16), value[height - 2 :].astype(BF16)
        if rows == 2:
            edges[0][c] = jnp.where(spots_of(rows)["row"] == 0, tail, head)
        else:
            edges[0][c] = tail
            edges[1][c] = head


def condition_kernel(rows, start, hidden, weight, kept, *refs):
    sent, mine, away = refs[: rows - 1], refs[rows - 1], refs[rows]
    window, weights, cond, held, row_sem, sems = refs[rows + 1 :]
    here = spots_of(rows)
    pieces = sems.shape[0]
    depth = weight.shape[0] // pieces
    span = window.shape[0]
    base = jnp.minimum((start[0] >> 4) << 4, hidden.shape[0] - span)
    load = pltpu.make_async_copy(hidden.at[pl.ds(pl.multiple_of(base, 16), span), :], window, row_sem)
    load.start()
    loads = [
        pltpu.make_async_copy(
            weight.at[k * depth : (k + 1) * depth, :], weights.at[k * depth : (k + 1) * depth, :], sems.at[k]
        )
        for k in range(pieces)
    ]
    for one in loads:
        one.start()
    load.wait()
    slot = lax.broadcasted_iota(jnp.int32, (SLOTS, span), 0)
    token = lax.broadcasted_iota(jnp.int32, (SLOTS, span), 1)
    chosen = jnp.where(token == slot + (start[0] - base), 1.0, 0.0).astype(BF16)
    cond[...] = product(chosen, window[...], (1, 0)).astype(BF16)
    half = cond.shape[1] // 2
    left, right = cond[:, :half], cond[:, half:]
    mine[...] = jnp.where(here["core"] == 0, left, right)
    away[...] = jnp.where(here["core"] == 0, right, left)
    total = None
    for k in range(pieces):
        loads[k].wait()
        one = product(cond[:, k * depth : (k + 1) * depth], weights[k * depth : (k + 1) * depth, :], (1, 0))
        total = one if total is None else total + one
    height = SLOTS // rows
    for r in range(rows):
        held[r] = total[r * height : (r + 1) * height]
    kept[...] = held[here["row"]]
    for j in range(1, rows):
        sent[j - 1][...] = held[here["row"] ^ j]


def select_kernel(rows, group_of, *refs):
    lines = len(refs) - 4
    here = spots_of(rows)
    for k in range(4):
        target = here["line"] * 4 + (here["plane"] ^ k)
        chosen = jnp.zeros(refs[0].shape, F32)
        for j in range(lines):
            goes = group_of[(here["line"] ^ j) * 4 + here["plane"]] == target
            chosen = chosen + jnp.where(goes, refs[j][...].astype(F32), 0.0)
        refs[lines + k][...] = chosen.astype(BF16)


def front_kernel(rows_total, noisy, *refs):
    far = refs[:-8]
    shift, in_weight, res_weight, query_weight, acts, hid, query, patches = refs[-8:]
    rows, cols = noisy.shape[1:]
    cells = rows * cols
    row = lax.axis_index("row")
    inner, outer = row > 0, row < rows_total - 1
    above = jnp.where(inner, far[0][...].astype(F32), 0.0)
    below = jnp.where(outer, far[-1][...].astype(F32), 0.0)
    lane = lax.broadcasted_iota(jnp.int32, (noisy.shape[0], cols), 1)
    depth = noisy.shape[0]
    for r in range(rows + 4):
        if r < 2:
            line = above[:, r]
        elif r < rows + 2:
            line = noisy[:, r - 2]
        else:
            line = below[:, r - rows - 2]
        turned = [
            jnp.where(lane == 0, 0.0, pltpu.roll(line, 1, 1)),
            line,
            jnp.where(lane == cols - 1, 0.0, pltpu.roll(line, cols - 1, 1)),
        ]
        for a in range(3):
            if 0 <= r - a < rows + 2:
                for b in range(3):
                    k = 3 * a + b
                    patches[k * depth : (k + 1) * depth, (r - a) * cols : (r - a + 1) * cols] = turned[b]
    first = product(in_weight[...], patches[...].astype(BF16), (0, 0))
    act = jax.nn.silu(first + shift[...])
    lane = lax.broadcasted_iota(jnp.int32, (act.shape[0], cols), 1)
    for r in range(rows + 2):
        band = act[:, r * cols : (r + 1) * cols]
        if r == 0:
            band = jnp.where(inner, band, 0.0)
        if r == rows + 1:
            band = jnp.where(outer, band, 0.0)
        spot = slice(r * cols, (r + 1) * cols)
        acts[1, :, spot] = band.astype(BF16)
        acts[0, :, spot] = jnp.where(lane == 0, 0.0, pltpu.roll(band, 1, 1)).astype(BF16)
        acts[2, :, spot] = jnp.where(lane == cols - 1, 0.0, pltpu.roll(band, cols - 1, 1)).astype(BF16)
    total = first[:, cols : cols + cells]
    for a in range(3):
        for b in range(3):
            total = total + product(res_weight[3 * a + b], acts[b, :, a * cols : a * cols + cells], (1, 0))
    low = total.astype(BF16)
    hid[...] = low
    query[...] = product(query_weight[...], low, (1, 0)).astype(BF16)


def attention_kernel(rows, query, hid, upstream, query_weight, out_weight, *refs):
    bands = refs[:rows]
    block_out, kept, grad_hid, query_grad, out_grad = refs[rows : rows + 5]
    sent = refs[rows + 5 : 2 * rows + 4]
    grad_att, attended, grad_query, held, pairs, grad_pairs = refs[2 * rows + 4 :]
    channels = hid.shape[0]
    here = spots_of(rows)
    height = SLOTS // rows
    for j in range(rows):
        held[here["row"] ^ j] = bands[j][...]
    for r in range(rows):
        pairs[r * height : (r + 1) * height, :] = held[r]
    scale = HEAD_DIM**-0.5
    grad_att[...] = product(out_weight[...], upstream[...], (0, 0)).astype(BF16)
    for h in range(channels // HEAD_DIM):
        spot = slice(h * HEAD_DIM, (h + 1) * HEAD_DIM)
        keys = pairs[:, h * HEAD_DIM : (h + 1) * HEAD_DIM]
        vals = pairs[:, channels + h * HEAD_DIM : channels + (h + 1) * HEAD_DIM]
        one = query[spot, :]
        score = product(keys, one, (1, 0)) * scale
        grown = jnp.exp(score - jnp.max(score, axis=0, keepdims=True))
        probs = grown / jnp.sum(grown, axis=0, keepdims=True)
        low = probs.astype(BF16)
        attended[spot, :] = product(vals, low, (0, 0)).astype(BF16)
        back = grad_att[spot, :]
        grad_prob = product(vals, back, (1, 0))
        inner = jnp.sum(probs * grad_prob, axis=0, keepdims=True)
        grad_score = (scale * probs * (grad_prob - inner)).astype(BF16)
        grad_query[spot, :] = product(keys, grad_score, (0, 0)).astype(BF16)
        grad_pairs[:, h * HEAD_DIM : (h + 1) * HEAD_DIM] = product(grad_score, one, (1, 1))
        grad_pairs[:, channels + h * HEAD_DIM : channels + (h + 1) * HEAD_DIM] = product(low, back, (1, 1))
    kept[...] = grad_pairs[pl.ds(pl.multiple_of(here["row"] * height, 8), height), :]
    for j in range(1, rows):
        spot = pl.ds(pl.multiple_of((here["row"] ^ j) * height, 8), height)
        sent[j - 1][...] = grad_pairs[spot, :].astype(BF16)
    block_out[...] = (
        hid[...].astype(F32) + product(out_weight[...], attended[...], (1, 0))
    ).astype(BF16)
    grad_hid[...] = (
        upstream[...].astype(F32) + product(query_weight[...], grad_query[...], (0, 0))
    ).astype(BF16)
    query_grad[...] = product(grad_query[...], hid[...], (1, 1))
    out_grad[...] = product(upstream[...], attended[...], (1, 1))


def filter_kernel(rows, cols, grad_hid, acts, query_grad, out_grad, kept, sent, whole, pair, wide):
    channels, cells = grad_hid.shape
    for t in range(0, 9, 2):
        taps = [t, t + 1] if t < 8 else [t]
        for k, tap in enumerate(taps):
            a, b = tap // 3, tap % 3
            pair[k * channels : (k + 1) * channels, :] = acts[b, :, a * cols : a * cols + cells]
        span = len(taps) * channels
        whole[:, t * channels : t * channels + span] = product(grad_hid[...], pair[:span, :], (1, 1))
    edge = 9 * channels
    base = edge // 128 * 128
    lead = edge - base
    wide[:, :channels] = query_grad[...]
    turned = pltpu.roll(wide[...], lead, 1) if lead else wide[...]
    lane = lax.broadcasted_iota(jnp.int32, (channels, 128), 1)
    whole[:, base : base + 128] = jnp.where(lane < lead, whole[:, base : base + 128], turned[:, :128])
    whole[:, base + 128 : edge + channels] = turned[:, 128 : lead + channels]
    whole[:, edge + channels : edge + 2 * channels] = out_grad[...]
    rest = whole.shape[1] - edge - 2 * channels
    if rest:
        whole[:, edge + 2 * channels :] = jnp.zeros((channels, rest), F32)
    half = channels // 2
    core = spots_of(rows)["core"]
    pieces, height = kept.shape[:2]
    for q in range(pieces):
        if height % 8 == 0:
            kept[q] = whole[pl.ds(pl.multiple_of(core * half + q * height, 8), height), :]
            away = whole[pl.ds(pl.multiple_of((1 - core) * half + q * height, 8), height), :]
        else:
            low = whole[q * height : (q + 1) * height, :]
            high = whole[half + q * height : half + (q + 1) * height, :]
            kept[q] = jnp.where(core == 0, low, high)
            away = jnp.where(core == 0, high, low)
        sent[q] = away.astype(BF16)


def square_kernel(rows, kept, came, own, *outs):
    here = spots_of(rows)["square"]
    own[...] = kept[here] + came[here].astype(F32)
    for j in range(1, 2 * rows):
        outs[j - 1][...] = (kept[here ^ j] + came[here ^ j].astype(F32)).astype(BF16)


def line_kernel(rows, count, near, *refs):
    here = spots_of(rows)["line"]
    total = refs[0][...]
    for one in refs[1:near]:
        total = total + one[...].astype(F32)
    own, outs, held = refs[near], refs[near + 1 : near + count], refs[near + count]
    slot = total.shape[1] // count
    held[...] = total
    own[...] = held[:, pl.ds(pl.multiple_of(here * slot, 128), slot)]
    for j in range(1, count):
        spot = pl.ds(pl.multiple_of((here ^ j) * slot, 128), slot)
        outs[j - 1][...] = held[:, spot].astype(BF16)


def unpack_kernel(rows, lines, *refs):
    count = 2 * rows
    here = spots_of(rows)
    parts = refs[: 2 * count]
    res, query, out, whole, *spare = refs[2 * count :]
    height = parts[0].shape[0]
    slot = parts[0].shape[1] // lines
    for c in range(2):
        for j in range(count):
            piece = parts[c * count + j][...].astype(F32)
            spot = (here["core"] ^ c) * count + (here["square"] ^ j)
            for z in range(lines):
                lanes = pl.ds(pl.multiple_of((here["line"] ^ z) * slot, 128), slot)
                one = piece[:, z * slot : (z + 1) * slot]
                if spare:
                    spare[0][spot, :, lanes] = one
                else:
                    whole[pl.ds(pl.multiple_of(spot * height, 8), height), lanes] = one
    if spare:
        for q in range(2 * count):
            whole[q * height : (q + 1) * height, :] = spare[0][q]
    channels = query.shape[0]
    for t in range(11):
        start = t * channels
        base = start // 128 * 128
        lead = start - base
        if lead:
            span = -(-(lead + channels) // 128) * 128
            piece = pltpu.roll(whole[:, base : base + span], span - lead, 1)[:, :channels]
        else:
            piece = whole[:, start : start + channels]
        piece = piece.astype(BF16)
        if t < 9:
            res[t] = piece
        elif t == 9:
            query[...] = piece
        else:
            out[...] = piece


def line_mask(j, rows):
    return j * 4 * rows


def square_mask(j, rows):
    return j // rows * 2 * rows + j % rows


def filter_step(grad_hid, acts, query_grad, out_grad, cols, rows, lines):
    channels, cells = grad_hid.shape
    slot = -(-11 * channels // (128 * lines)) * 128
    width = slot * lines
    half = channels // 2
    return call(
        functools.partial(filter_kernel, rows, cols),
        [((2 * rows, half // rows // 2, width), F32), ((2 * rows, half // rows // 2, width), BF16)],
        [grad_hid, acts, query_grad, out_grad],
        [
            pltpu.VMEM((channels, width), F32),
            pltpu.VMEM((2 * channels, cells), BF16),
            pltpu.VMEM((channels, -(-channels // 128) * 128), F32),
        ],
        flops=18 * channels * channels * cells,
    )


def square_step(kept, came, rows):
    squares, height, width = kept.shape
    return call(
        functools.partial(square_kernel, rows),
        [((height, width), F32)] + [((height, width), BF16)] * (squares - 1),
        [kept, came],
    )


def line_step(own, near, rows, lines):
    height, width = own.shape
    slot = width // lines
    return call(
        functools.partial(line_kernel, rows, lines, len(near) + 1),
        [((height, slot), F32)] + [((height, slot), BF16)] * (lines - 1),
        [own, *near],
        [pltpu.VMEM((height, width), F32)],
    )


def unpack_step(mine, other, channels, rows, lines):
    height = mine[0].shape[0]
    res, query, out = call(
        functools.partial(unpack_kernel, rows, lines),
        [((9, channels, channels), BF16), ((channels, channels), BF16), ((channels, channels), BF16)],
        [*mine, *other],
        [pltpu.VMEM((channels, mine[0].shape[1]), F32)]
        + [pltpu.VMEM((channels // height, height, mine[0].shape[1]), F32)] * (height % 8 > 0),
        leave=(0, 1, 2),
    )
    return res.reshape(3, 3, channels, channels), query, out


def gather_kernel(rows, lines, group_of, *refs):
    count = 4 * rows
    parts = refs[:count]
    image_rows, all_rows, held = refs[count:]
    image, row = lax.axis_index("img"), lax.axis_index("row")
    for k in range(count):
        for z in range(lines):
            held[k * lines + z] = parts[k][z]

    def spot(source, r):
        v = group_of[source] ^ image
        return (((v & 1) * 2 + ((v >> 1) & 1)) * rows + (row ^ r)) * lines + (v >> 2)

    for r in range(rows):
        image_rows[r] = held[spot(image, r)]
    for x in range(2):
        for z in range(lines):
            for c in range(2):
                p = (x * lines + z) * 2 + c
                for r in range(rows):
                    all_rows[p * rows + r] = held[spot(image ^ (z * 4 + x * 2 + c), r)]


def place_kernel(start, rows, blank, out, window, sem):
    span = window.shape[0]
    base = jnp.minimum((start[0] >> 4) << 4, out.shape[0] - span)
    token = lax.broadcasted_iota(jnp.int32, (span, SLOTS), 0)
    slot = lax.broadcasted_iota(jnp.int32, (span, SLOTS), 1)
    chosen = jnp.where(token == slot + (start[0] - base), 1.0, 0.0).astype(BF16)
    window[...] = product(chosen, rows[...], (1, 0)).astype(BF16)
    store = pltpu.make_async_copy(window, out.at[pl.ds(pl.multiple_of(base, 16), span), :], sem)
    store.start()
    store.wait()


def join_kernel(own, came, out, sems):
    width = own.shape[0]
    core = lax.axis_index("img") & 1
    count = sems.shape[1]
    depth = width // count
    stores = []
    for k in range(count):
        for side, one in enumerate((own, came)):
            start = (core if side == 0 else 1 - core) * width + k * depth
            target = out.at[pl.ds(pl.multiple_of(start, 8), depth), :]
            stores.append(pltpu.make_async_copy(one.at[k * depth : (k + 1) * depth, :], target, sems.at[side, k]))
    for one in stores:
        one.start()
    for one in stores:
        one.wait()


def blank_kernel(out, zeros, sems):
    zeros[...] = jnp.zeros(zeros.shape, zeros.dtype)
    depth = zeros.shape[0]
    count = out.shape[0] // depth
    stores = [
        pltpu.make_async_copy(zeros, out.at[k * depth : (k + 1) * depth, :], sems.at[k]) for k in range(count)
    ]
    for one in stores:
        one.start()
    for one in stores:
        one.wait()


def shards(
    llm_hidden,
    slot_start,
    image_group,
    timesteps,
    latents,
    noise,
    kv_weight,
    in_weight,
    res_weight,
    query_weight,
    out_weight,
    cotangent,
):
    rows = lax.axis_size("row")
    images = lax.axis_size("img")
    lines = images // 4
    channels = in_weight.shape[2]
    row_count, col_count = latents.shape[2:]
    cells = row_count * col_count
    tokens, features = llm_hidden.shape
    pair_width = kv_weight.shape[1]
    height = SLOTS // rows
    half = features // 2

    depth = latents.shape[1]
    noisy, *edges = call(
        functools.partial(noisy_kernel, rows),
        [((depth, row_count, col_count), F32)] + [((depth, 2, col_count), BF16)] * (1 if rows == 2 else 2),
        [timesteps, latents, noise],
        scalars=1,
    )
    if rows == 2:
        far = [lax.ppermute(edges[0], "row", [(0, 1), (1, 0)])]
    else:
        far = [
            lax.ppermute(edges[0], "row", [(i, i + 1) for i in range(rows - 1)]),
            lax.ppermute(edges[1], "row", [(i + 1, i) for i in range(rows - 1)]),
        ]

    span = min(SLOTS + 16, tokens)
    pieces = 4 if features % 512 == 0 else 1
    kept, *rest = pl.pallas_call(
        functools.partial(condition_kernel, rows),
        out_shape=[jax.ShapeDtypeStruct((height, pair_width), F32)] * rows
        + [jax.ShapeDtypeStruct((SLOTS, half), BF16)] * 2,
        in_specs=[SMEM, pl.BlockSpec(memory_space=pl.ANY), pl.BlockSpec(memory_space=pl.ANY)],
        out_specs=[VMEM] * (rows + 2),
        scratch_shapes=[
            pltpu.VMEM((span, features), BF16),
            pltpu.VMEM((features, pair_width), BF16),
            pltpu.VMEM((SLOTS, features), BF16),
            pltpu.VMEM((rows, height, pair_width), F32),
            pltpu.SemaphoreType.DMA,
            pltpu.SemaphoreType.DMA((pieces,)),
        ],
        cost_estimate=pl.CostEstimate(
            flops=2 * SLOTS * features * pair_width,
            bytes_accessed=2 * features * (pair_width + 3 * SLOTS),
            transcendentals=0,
        ),
        name="condition",
    )(slot_start, llm_hidden, kv_weight)
    sent, mine, away = rest[: rows - 1], rest[rows - 1], rest[rows]

    band = kept
    for j in range(1, rows):
        band = band + swap(sent[j - 1], j)
    band = band.astype(BF16)
    column = [band] + [swap(band, line_mask(j, rows)) for j in range(1, lines)]
    upstream = cotangent[0].reshape(channels, cells)
    shift = time_shift(timesteps[0], channels)[:, None]
    in_flat = in_weight.transpose(0, 1, 3, 2).reshape(-1, channels)
    column[0], upstream, shift, in_flat = lax.optimization_barrier((column[0], upstream, shift, in_flat))
    plane = call(
        functools.partial(select_kernel, rows), [((height, pair_width), BF16)] * 4, [image_group, *column], scalars=1
    )
    band = plane[0].astype(F32)
    for k in range(1, 4):
        band = band + swap(plane[k], k * rows).astype(F32)
    band = band.astype(BF16)
    bands = [band] + [swap(band, j) for j in range(1, rows)]

    other = swap(away, rows)
    block = jnp.concatenate([mine, other])
    near = [block] + [swap(block, line_mask(j, rows)) for j in range(1, lines)]

    acts, hid, query = call(
        functools.partial(front_kernel, rows),
        [
            ((3, channels, cells + 2 * col_count), BF16),
            ((channels, cells), BF16),
            ((channels, cells), BF16),
        ],
        [
            noisy,
            *far,
            shift,
            in_flat,
            res_weight.reshape(9, channels, channels),
            query_weight,
        ],
        [pltpu.VMEM((9 * depth, cells + 2 * col_count), F32)],
        flops=20 * channels * channels * cells,
    )
    block_out, kept, grad_hid, query_grad, out_grad, *sent = call(
        functools.partial(attention_kernel, rows),
        [
            ((channels, cells), BF16),
            ((height, pair_width), F32),
            ((channels, cells), BF16),
            ((channels, channels), F32),
            ((channels, channels), F32),
        ]
        + [((height, pair_width), BF16)] * (rows - 1),
        [query, hid, upstream, query_weight, out_weight, *bands],
        [pltpu.VMEM((channels, cells), BF16)] * 3
        + [
            pltpu.VMEM((rows, height, pair_width), BF16),
            pltpu.VMEM((SLOTS, pair_width), BF16),
            pltpu.VMEM((SLOTS, pair_width), F32),
        ],
        flops=10 * channels * channels * cells + 12 * channels * SLOTS * cells,
    )
    grad_band = kept
    for j in range(1, rows):
        grad_band = grad_band + swap(sent[j - 1], j).astype(F32)
    grad_band = grad_band.astype(BF16)
    kept, sent = filter_step(grad_hid, acts, query_grad, out_grad, col_count, rows, lines)
    own, *outs = square_step(kept, swap(sent, rows), rows)
    blank = pl.pallas_call(
        blank_kernel,
        out_shape=jax.ShapeDtypeStruct((tokens, features), BF16),
        out_specs=pl.BlockSpec(memory_space=pl.ANY),
        scratch_shapes=[
            pltpu.VMEM((tokens // 8, features), BF16),
            pltpu.SemaphoreType.DMA((8,)),
        ],
        name="blank",
    )()
    block_out = block_out.reshape(1, channels, row_count, col_count)
    own, block_out = lax.optimization_barrier((own, block_out))
    squares = 2 * rows
    came = [swap(outs[j - 1], square_mask(j, rows)) for j in range(1, squares)]
    own, *outs = line_step(own, came, rows, lines)
    came = [swap(outs[j - 1], line_mask(j, rows)) for j in range(1, lines)]
    weight_scale = (images * rows * cells) ** (-0.5)
    for one in came:
        own = own + one.astype(F32)
    final = (own * weight_scale).astype(BF16)
    far = [swap(final, line_mask(j, rows)) for j in range(1, lines)]

    column = jnp.stack([grad_band] + [swap(grad_band, line_mask(j, rows)) for j in range(1, lines)])
    parts = [column] + [swap(column, square_mask(j, rows)) for j in range(1, squares)]
    parts = parts + [swap(one, rows) for one in parts]
    image_rows, all_rows = call(
        functools.partial(gather_kernel, rows, lines),
        [((rows, height, pair_width), BF16), ((images * rows, height, pair_width), BF16)],
        [image_group, *parts],
        [pltpu.VMEM((4 * rows * lines, height, pair_width), BF16)],
        scalars=1,
    )
    all_rows = all_rows.reshape(images * SLOTS, pair_width)
    grad_condition = product(image_rows.reshape(SLOTS, pair_width), kv_weight, (1, 1)).astype(BF16)
    grad_hidden = pl.pallas_call(
        place_kernel,
        out_shape=jax.ShapeDtypeStruct((tokens, features), BF16),
        in_specs=[SMEM, VMEM, pl.BlockSpec(memory_space=pl.ANY)],
        out_specs=pl.BlockSpec(memory_space=pl.ANY),
        scratch_shapes=[pltpu.VMEM((span, features), BF16), pltpu.SemaphoreType.DMA],
        input_output_aliases={2: 0},
        name="place",
    )(slot_start, grad_condition, blank)
    wide = jnp.concatenate([final, *far], axis=1)
    parts = [wide] + [swap(wide, square_mask(j, rows)) for j in range(1, squares)]

    near_half = images * SLOTS // 2
    across = [swap(near[j], 2 * rows) for j in range(lines)]
    total = product(jnp.concatenate(near), all_rows[:near_half], (0, 0))
    total = total + product(jnp.concatenate(across), all_rows[near_half:], (0, 0))
    weight_half = (total * (images * SLOTS) ** (-0.5)).astype(BF16)
    came = swap(weight_half, rows)
    grad_kv_weight = pl.pallas_call(
        join_kernel,
        out_shape=jax.ShapeDtypeStruct((features, pair_width), BF16),
        in_specs=[VMEM, VMEM],
        out_specs=pl.BlockSpec(memory_space=pl.ANY),
        scratch_shapes=[pltpu.SemaphoreType.DMA((2, 4 if half % 64 == 0 else 1))],
        compiler_params=pltpu.CompilerParams(vmem_limit_bytes=LIMIT),
        name="join",
    )(near_core(weight_half), near_core(came))
    others = [swap(one, rows) for one in parts]
    grad_res_weight, grad_query_weight, grad_out_weight = unpack_step(
        parts, others, channels, rows, lines
    )
    return (
        block_out,
        grad_hidden,
        grad_kv_weight,
        grad_res_weight,
        grad_query_weight,
        grad_out_weight,
    )


def solution(mesh):
    return jax.shard_map(
        shards,
        mesh=mesh,
        in_specs=(
            P("img", "row"),
            P("img"),
            P(),
            P("img"),
            P("img", None, "row", None),
            P("img", None, "row", None),
            P("row", None),
            P(),
            P(),
            P(),
            P(),
            P("img", None, "row", None),
        ),
        out_specs=(P("img", None, "row", None), P("img", "row"), P("row", None), P(), P(), P()),
        check_vma=False,
    )
```

profile of v0, /device:TPU:0, one launch (start us, length us, event | category | flops | bytes accessed | tf_op | source)
XLA Modules:
  0.0 178.1 jit_solution(4017230062432172060)
XLA Ops:
  1.3 4.1 %condition.1 = (f32[32,640]{1,0:T(8,128)}, f32[32,640]{1,0:T(8,128)}, bf16[64,1664]{1,0:T(8,128)(2,1)}, bf16[64,1664]{1,0:T(8,128)(2,1)}) custom-call(s32[1]{0:T(128)S(6)} %copy.30.start, bf16[512,3328]{1,0:T(8,128)(2,1)} %hidden.1, bf16[3328,640]{1,0:T(8,128)(2,1)} %weight.1), custom_call_target="tpu_custom_call" | custom-call | flops 272629760 | bytes 5537792 | tf_op jit(solution)/shard_map/condition/pallas_call | solution.py:504
  5.5 3.1 %collective-permute-start.1 = (f32[32,640]{1,0:T(8,128)}, f32[32,640]{1,0:T(8,128)S(1)}, u32[]{:S(2)}, u32[]{:S(2)}) collective-permute-start(f32[32,640]{1,0:T(8,128)} %get-tuple-element.49), channel_id=1, source_target_pairs={{0,1},{1,0},{2,3},{3,2},{4,5},{5,4},{6,7},{7,6},{8,9},{9,8},{10,11... | collective-permute-start | bytes 245768 | tf_op jit(solution)/shard_map/ppermute | solution.py:56
  9.3 1.9 %collective-permute-done.1 = f32[32,640]{1,0:T(8,128)S(1)} collective-permute-done((f32[32,640]{1,0:T(8,128)}, f32[32,640]{1,0:T(8,128)S(1)}, u32[]{:S(2)}, u32[]{:S(2)}) %collective-permute-start.1) | collective-permute-done | bytes 81952 | tf_op jit(solution)/shard_map/ppermute | solution.py:56
  12.1 2.1 %collective-permute-start.2 = (bf16[32,640]{1,0:T(8,128)(2,1)S(1)}, bf16[32,640]{1,0:T(8,128)(2,1)S(1)}, u32[]{:S(2)}, u32[]{:S(2)}) collective-permute-start(bf16[32,640]{1,0:T(8,128)(2,1)S(1)} %add_convert_fusion.2.refs_0_), channel_id=1, source_target_pairs={{0,8},{1,9},{2,10},{3,11},{4,12},{5,13},{6,14},{7,15},{8,0},{9,1},... | collective-permute-start | bytes 122888 | tf_op jit(solution)/shard_map/ppermute | solution.py:56
  14.2 2.6 %collective-permute-start.3 = (bf16[32,640]{1,0:T(8,128)(2,1)S(1)}, bf16[32,640]{1,0:T(8,128)(2,1)S(1)}, u32[]{:S(2)}, u32[]{:S(2)}) collective-permute-start(bf16[32,640]{1,0:T(8,128)(2,1)S(1)} %add_convert_fusion.2.refs_0_), channel_id=1, source_target_pairs={{0,16},{1,17},{2,18},{3,19},{4,20},{5,21},{6,22},{7,23},{8,24},{9,... | collective-permute-start | bytes 122888 | tf_op jit(solution)/shard_map/ppermute | solution.py:56
  18.2 1.8 %collective-permute-done.3.refs_2_ = bf16[32,640]{1,0:T(8,128)(2,1)S(1)} collective-permute-done((bf16[32,640]{1,0:T(8,128)(2,1)S(1)}, bf16[32,640]{1,0:T(8,128)(2,1)S(1)}, u32[]{:S(2)}, u32[]{:S(2)}) %collective-permute-start.3) | collective-permute-done | bytes 40992 | tf_op jit(solution)/shard_map/ppermute | solution.py:56
  20.0 2.6 %collective-permute-done.4.refs_3_ = bf16[32,640]{1,0:T(8,128)(2,1)S(1)} collective-permute-done((bf16[32,640]{1,0:T(8,128)(2,1)S(1)}, bf16[32,640]{1,0:T(8,128)(2,1)S(1)}, u32[]{:S(2)}, u32[]{:S(2)}) %collective-permute-start.4) | collective-permute-done | bytes 40992 | tf_op jit(solution)/shard_map/ppermute | solution.py:56
  30.4 4.2 %shard_map.164 = (bf16[3,320,1280]{2,1,0:T(8,128)(2,1)S(1)}, bf16[320,1024]{1,0:T(8,128)(2,1)S(1)}, bf16[320,1024]{1,0:T(8,128)(2,1)S(1)}) custom-call(f32[4,8,128]{2,1,0:T(8,128)S(1)} %get-tuple-element.46.noisy, bf16[4,2,128]{2,1,0:T(2,128)(2,1)S(1)} %collective-permute-done.refs_0_, f32[320,1]{1,0:T(8,128)S(1)} %copy.19.refs_1_, ...), custom_call_target="tpu_custom_call" | custom-call | flops 2097152000 | bytes 5859072 | tf_op jit(solution)/shard_map/pallas_call | solution.py:32
  34.6 4.7 %shard_map.166 = (bf16[320,1024]{1,0:T(8,128)(2,1)S(1)}, f32[32,640]{1,0:T(8,128)S(1)}, bf16[320,1024]{1,0:T(8,128)(2,1)S(1)}, f32[320,320]{1,0:T(8,128)S(1)}, f...) custom-call(bf16[320,1024]{1,0:T(8,128)(2,1)S(1)} %get-tuple-element.52.query, ...), custom_call_target="tpu_custom_call" | custom-call | flops 1300234240 | bytes 4710400 | tf_op jit(solution)/shard_map/pallas_call | solution.py:32
  39.9 3.5 %collective-permute-done.10 = bf16[32,640]{1,0:T(8,128)(2,1)S(1)} collective-permute-done((bf16[32,640]{1,0:T(8,128)(2,1)S(1)}, bf16[32,640]{1,0:T(8,128)(2,1)S(1)}, u32[]{:S(2)}, u32[]{:S(2)}) %collective-permute-start.10) | collective-permute-done | bytes 40992 | tf_op jit(solution)/shard_map/ppermute | solution.py:56
  43.9 3.9 %collective-permute-start.11 = (bf16[32,640]{1,0:T(8,128)(2,1)S(1)}, bf16[32,640]{1,0:T(8,128)(2,1)S(1)}, u32[]{:S(2)}, u32[]{:S(2)}) collective-permute-start(bf16[32,640]{1,0:T(8,128)(2,1)S(1)} %add_convert_fusion), channel_id=1, source_target_pairs={{0,8},{1,9},{2,10},{3,11},{4,12},{5,13},{6,14},{7,15},{8,0},{9,1},... | collective-permute-start | bytes 122888 | tf_op jit(solution)/shard_map/ppermute | solution.py:56
  53.4 2.1 %collective-permute-start.22 = (bf16[128,1664]{1,0:T(8,128)(2,1)S(1)}, bf16[128,1664]{1,0:T(8,128)(2,1)S(1)}, u32[]{:S(2)}, u32[]{:S(2)}) collective-permute-start(bf16[128,1664]{1,0:T(8,128)(2,1)S(1)} %get-tuple-element.88), channel_id=1, source_target_pairs={{0,8},{1,9},{2,10},{3,11},{4,12},{5,13},{6,14},{7,15},{8,0},{9,1},... | collective-permute-start | bytes 1277960 | tf_op jit(solution)/shard_map/ppermute | solution.py:56
  59.0 3.4 %shard_map.167 = (f32[4,40,3584]{2,1,0:T(8,128)S(1)}, bf16[4,40,3584]{2,1,0:T(8,128)(2,1)S(1)}) custom-call(bf16[320,1024]{1,0:T(8,128)(2,1)S(1)} %get-tuple-element.60.grad_hid, bf16[3,320,1280]{2,1,0:T(8,128)(2,1)S(1)} %get-tuple-element.61.acts, f32[320,320]{1,0:T(8,128)S(1)} %get-tuple-element.62.query_grad, f32[320,320]{1,0:T(8,128)S(1)} %get-tuple-element.63.out_grad), custom_call_target="tpu_custom_call" | custom-call | flops 1887436800 | bytes 7372800 | tf_op jit(solution)/shard_map/pallas_call | solution.py:32
  62.5 2.9 %collective-permute-start.24 = (bf16[128,1664]{1,0:T(8,128)(2,1)S(1)}, bf16[128,1664]{1,0:T(8,128)(2,1)S(1)}, u32[]{:S(2)}, u32[]{:S(2)}) collective-permute-start(bf16[128,1664]{1,0:T(8,128)(2,1)S(1)} %get-tuple-element.88), channel_id=1, source_target_pairs={{0,24},{1,25},{2,26},{3,27},{4,28},{5,29},{6,30},{7,31},{8,16},{9,... | collective-permute-start | bytes 1277960 | tf_op jit(solution)/shard_map/ppermute | solution.py:56
  67.4 20.9 %collective-permute-done.23 = bf16[128,1664]{1,0:T(8,128)(2,1)S(1)} collective-permute-done((bf16[128,1664]{1,0:T(8,128)(2,1)S(1)}, bf16[128,1664]{1,0:T(8,128)(2,1)S(1)}, u32[]{:S(2)}, u32[]{:S(2)}) %collective-permute-start.23) | collective-permute-done | bytes 426016 | tf_op jit(solution)/shard_map/ppermute | solution.py:56
  93.2 22.0 %collective-permute-done.28 = bf16[128,1664]{1,0:T(8,128)(2,1)S(1)} collective-permute-done((bf16[128,1664]{1,0:T(8,128)(2,1)S(1)}, bf16[128,1664]{1,0:T(8,128)(2,1)S(1)}, u32[]{:S(2)}, u32[]{:S(2)}) %collective-permute-start.28) | collective-permute-done | bytes 426016 | tf_op jit(solution)/shard_map/ppermute | solution.py:56
  117.6 1.7 collective-permute-start.31
  121.6 4.8 %collective-permute-done.30.refs_1_ = bf16[40,3584]{1,0:T(8,128)(2,1)S(1)} collective-permute-done((bf16[40,3584]{1,0:T(8,128)(2,1)S(1)}, bf16[40,3584]{1,0:T(8,128)(2,1)S(1)}, u32[]{:S(2)}, u32[]{:S(2)}) %collective-permute-start.30) | collective-permute-done | bytes 286752 | tf_op jit(solution)/shard_map/ppermute | solution.py:56
  127.3 6.4 %collective-permute-done.32.refs_3_ = bf16[40,3584]{1,0:T(8,128)(2,1)S(1)} collective-permute-done((bf16[40,3584]{1,0:T(8,128)(2,1)S(1)}, bf16[40,3584]{1,0:T(8,128)(2,1)S(1)}, u32[]{:S(2)}, u32[]{:S(2)}) %collective-permute-start.32) | collective-permute-done | bytes 286752 | tf_op jit(solution)/shard_map/ppermute | solution.py:56
  134.1 4.3 %collective-permute-start.33 = (bf16[40,896]{1,0:T(8,128)(2,1)S(1)}, bf16[40,896]{1,0:T(8,128)(2,1)S(1)}, u32[]{:S(2)}, u32[]{:S(2)}) collective-permute-start(bf16[40,896]{1,0:T(8,128)(2,1)S(1)} %get-tuple-element.80), channel_id=1, source_target_pairs={{0,8},{1,9},{2,10},{3,11},{4,12},{5,13},{6,14},{7,15},{8,0},{9,1},... | collective-permute-start | bytes 215048 | tf_op jit(solution)/shard_map/ppermute | solution.py:56
  138.4 2.4 %collective-permute-done.35 = bf16[40,896]{1,0:T(8,128)(2,1)S(1)} collective-permute-done((bf16[40,896]{1,0:T(8,128)(2,1)S(1)}, bf16[40,896]{1,0:T(8,128)(2,1)S(1)}, u32[]{:S(2)}, u32[]{:S(2)}) %collective-permute-start.35) | collective-permute-done | bytes 71712 | tf_op jit(solution)/shard_map/ppermute | solution.py:56
  141.6 2.1 %collective-permute-start.38 = (bf16[40,896]{1,0:T(8,128)(2,1)S(1)}, bf16[40,896]{1,0:T(8,128)(2,1)S(1)}, u32[]{:S(2)}, u32[]{:S(2)}) collective-permute-start(bf16[40,896]{1,0:T(8,128)(2,1)S(1)} %multiply_convert_fusion.1), channel_id=1, source_target_pairs={{0,24},{1,25},{2,26},{3,27},{4,28},{5,29},{6,30},{7,31},{8,16},{9,... | collective-permute-start | bytes 215048 | tf_op jit(solution)/shard_map/ppermute | solution.py:56
  144.3 1.8 collective-permute-start.36
  146.1 2.3 %collective-permute-done.38 = bf16[40,896]{1,0:T(8,128)(2,1)S(1)} collective-permute-done((bf16[40,896]{1,0:T(8,128)(2,1)S(1)}, bf16[40,896]{1,0:T(8,128)(2,1)S(1)}, u32[]{:S(2)}, u32[]{:S(2)}) %collective-permute-start.38) | collective-permute-done | bytes 71712 | tf_op jit(solution)/shard_map/ppermute | solution.py:56
  150.4 1.6 collective-permute-start.40
  153.4 1.8 %blank.1 = bf16[512,3328]{1,0:T(8,128)(2,1)} custom-call(), custom_call_target="tpu_custom_call" | custom-call | tf_op jit(solution)/shard_map/blank/pallas_call | solution.py:592
  155.3 3.4 %collective-permute-done.39.refs_1_ = bf16[40,3584]{1,0:T(8,128)(2,1)S(1)} collective-permute-done((bf16[40,3584]{1,0:T(8,128)(2,1)S(1)}, bf16[40,3584]{1,0:T(8,128)(2,1)S(1)}, u32[]{:S(2)}, u32[]{:S(2)}) %collective-permute-start.39) | collective-permute-done | bytes 286752 | tf_op jit(solution)/shard_map/ppermute | solution.py:56
  160.1 4.1 %collective-permute-done.41.refs_3_ = bf16[40,3584]{1,0:T(8,128)(2,1)S(1)} collective-permute-done((bf16[40,3584]{1,0:T(8,128)(2,1)S(1)}, bf16[40,3584]{1,0:T(8,128)(2,1)S(1)}, u32[]{:S(2)}, u32[]{:S(2)}) %collective-permute-start.41) | collective-permute-done | bytes 286752 | tf_op jit(solution)/shard_map/ppermute | solution.py:56
  164.2 4.3 %convolution_convert_fusion.rows = bf16[64,3328]{1,0:T(8,128)(2,1)} fusion(bf16[64,640]{1,0:T(8,128)(2,1)S(1)} %bitcast.26, bf16[3328,640]{1,0:T(8,128)(2,1)} %weight.1), kind=kOutput, calls=%fused_computation | convolution fusion | flops 272842752 | bytes 4767744 | tf_op jit(solution)/shard_map/dot_general | solution.py:44
  168.6 2.1 %place.1 = bf16[512,3328]{1,0:T(8,128)(2,1)} custom-call(s32[1]{0:T(128)S(6)} %copy.30.start, bf16[64,3328]{1,0:T(8,128)(2,1)} %convolution_convert_fusion.rows, bf16[512,3328]{1,0:T(8,128)(2,1)} %blank.1), custom_call_target="tpu_custom_call", output_to_operand_aliasing={{}: (2, {})} | custom-call | tf_op jit(solution)/shard_map/place/pallas_call | solution.py:626
  170.7 3.5 %shard_map.171 = (bf16[9,320,320]{2,1,0:T(8,128)(2,1)}, bf16[320,320]{1,0:T(8,128)(2,1)}, bf16[320,320]{1,0:T(8,128)(2,1)}) custom-call(bf16[40,3584]{1,0:T(8,128)(2,1)S(1)} %pad_maximum_fusion.refs_0_, bf16[40,3584]{1,0:T(8,128)(2,1)S(1)} %collective-permute-done.39.refs_1_, bf16[40,3584]{1,0:T(8,128)(2,1)S(1)} %collective-permute-done.40.refs_2_, ...), custom_call_target="tpu_custom_call" | custom-call | bytes 4546560 | tf_op jit(solution)/shard_map/pallas_call | solution.py:32
  174.3 3.7 %join.1 = bf16[3328,640]{1,0:T(8,128)(2,1)} custom-call(bf16[1664,640]{1,0:T(8,128)(2,1)S(1)} %multiply_convert_fusion.own, bf16[1664,640]{1,0:T(8,128)(2,1)} %collective-permute-done.29.came), custom_call_target="tpu_custom_call" | custom-call | tf_op jit(solution)/shard_map/join/pallas_call | solution.py:644
  (113 shorter events, 39.4 us)
Async XLA Ops:
  12.1 6.0 %collective-permute-start.2 = (bf16[32,640]{1,0:T(8,128)(2,1)S(1)}, bf16[32,640]{1,0:T(8,128)(2,1)S(1)}, u32[]{:S(2)}, u32[]{:S(2)}) collective-permute-start(bf16[32,640]{1,0:T(8,128)(2,1)S(1)} %add_convert_fusion.2.refs_0_), channel_id=1, source_target_pairs={{0,8},{1,9},{2,10},{3,11},{4,12},{5,13},{6,14},{7,15},{8,0},{9,1},... | collective-permute-start | bytes 122888 | tf_op jit(solution)/shard_map/ppermute | solution.py:56
  39.9 13.5 %collective-permute-start.21 = (bf16[64,1664]{1,0:T(8,128)(2,1)S(1)}, bf16[64,1664]{1,0:T(8,128)(2,1)S(1)}, u32[]{:S(2)}, u32[]{:S(2)}) collective-permute-start(bf16[64,1664]{1,0:T(8,128)(2,1)S(1)} %copy-done.8), channel_id=1, source_target_pairs={{0,2},{1,3},{2,0},{3,1},{4,6},{5,7},{6,4},{7,5},{8,10},{9,11},{10,... | collective-permute-start | bytes 638984 | tf_op jit(solution)/shard_map/ppermute | solution.py:56
  43.4 5.9 %collective-permute-start.13 = (bf16[32,640]{1,0:T(8,128)(2,1)S(1)}, bf16[32,640]{1,0:T(8,128)(2,1)S(1)}, u32[]{:S(2)}, u32[]{:S(2)}) collective-permute-start(bf16[32,640]{1,0:T(8,128)(2,1)S(1)} %add_convert_fusion), channel_id=1, source_target_pairs={{0,24},{1,25},{2,26},{3,27},{4,28},{5,29},{6,30},{7,31},{8,16},{9,... | collective-permute-start | bytes 122888 | tf_op jit(solution)/shard_map/ppermute | solution.py:56
  43.9 5.9 %collective-permute-start.11 = (bf16[32,640]{1,0:T(8,128)(2,1)S(1)}, bf16[32,640]{1,0:T(8,128)(2,1)S(1)}, u32[]{:S(2)}, u32[]{:S(2)}) collective-permute-start(bf16[32,640]{1,0:T(8,128)(2,1)S(1)} %add_convert_fusion), channel_id=1, source_target_pairs={{0,8},{1,9},{2,10},{3,11},{4,12},{5,13},{6,14},{7,15},{8,0},{9,1},... | collective-permute-start | bytes 122888 | tf_op jit(solution)/shard_map/ppermute | solution.py:56
  49.8 6.6 %collective-permute-start.14 = (bf16[4,32,640]{2,1,0:T(8,128)(2,1)S(1)}, bf16[4,32,640]{2,1,0:T(8,128)(2,1)S(1)}, u32[]{:S(2)}, u32[]{:S(2)}) collective-permute-start(bf16[4,32,640]{2,1,0:T(8,128)(2,1)S(1)} %pad_maximum_fusion.1.refs_0_), channel_id=1, source_target_pairs={{0,1},{1,0},{2,3},{3,2},{4,5},{5,4},{6,7},{7,6},{8,9},{9,8},{10,11... | collective-permute-start | bytes 491528 | tf_op jit(solution)/shard_map/ppermute | solution.py:56
  50.4 7.0 %collective-permute-start.15 = (bf16[4,32,640]{2,1,0:T(8,128)(2,1)S(1)}, bf16[4,32,640]{2,1,0:T(8,128)(2,1)S(1)}, u32[]{:S(2)}, u32[]{:S(2)}) collective-permute-start(bf16[4,32,640]{2,1,0:T(8,128)(2,1)S(1)} %pad_maximum_fusion.1.refs_0_), channel_id=1, source_target_pairs={{0,4},{1,5},{2,6},{3,7},{4,0},{5,1},{6,2},{7,3},{8,12},{9,13},{10,... | collective-permute-start | bytes 491528 | tf_op jit(solution)/shard_map/ppermute | solution.py:56
  51.8 6.6 %collective-permute-start.16 = (bf16[4,32,640]{2,1,0:T(8,128)(2,1)S(1)}, bf16[4,32,640]{2,1,0:T(8,128)(2,1)S(1)}, u32[]{:S(2)}, u32[]{:S(2)}) collective-permute-start(bf16[4,32,640]{2,1,0:T(8,128)(2,1)S(1)} %pad_maximum_fusion.1.refs_0_), channel_id=1, source_target_pairs={{0,5},{1,4},{2,7},{3,6},{4,1},{5,0},{6,3},{7,2},{8,13},{9,12},{10,... | collective-permute-start | bytes 491528 | tf_op jit(solution)/shard_map/ppermute | solution.py:56
  53.4 35.9 %collective-permute-start.22 = (bf16[128,1664]{1,0:T(8,128)(2,1)S(1)}, bf16[128,1664]{1,0:T(8,128)(2,1)S(1)}, u32[]{:S(2)}, u32[]{:S(2)}) collective-permute-start(bf16[128,1664]{1,0:T(8,128)(2,1)S(1)} %get-tuple-element.88), channel_id=1, source_target_pairs={{0,8},{1,9},{2,10},{3,11},{4,12},{5,13},{6,14},{7,15},{8,0},{9,1},... | collective-permute-start | bytes 1277960 | tf_op jit(solution)/shard_map/ppermute | solution.py:56
  56.4 31.8 %collective-permute-start.23 = (bf16[128,1664]{1,0:T(8,128)(2,1)S(1)}, bf16[128,1664]{1,0:T(8,128)(2,1)S(1)}, u32[]{:S(2)}, u32[]{:S(2)}) collective-permute-start(bf16[128,1664]{1,0:T(8,128)(2,1)S(1)} %get-tuple-element.88), channel_id=1, source_target_pairs={{0,16},{1,17},{2,18},{3,19},{4,20},{5,21},{6,22},{7,23},{8,24},{9,... | collective-permute-start | bytes 1277960 | tf_op jit(solution)/shard_map/ppermute | solution.py:56
  58.5 6.9 %collective-permute-start.20 = (bf16[4,32,640]{2,1,0:T(8,128)(2,1)S(1)}, bf16[4,32,640]{2,1,0:T(8,128)(2,1)S(1)}, u32[]{:S(2)}, u32[]{:S(2)}) collective-permute-start(bf16[4,32,640]{2,1,0:T(8,128)(2,1)S(1)} %collective-permute-done.16.refs_3_), channel_id=1, source_target_pairs={{0,2},{1,3},{2,0},{3,1},{4,6},{5,7},{6,4},{7,5},{8,10},{9,11},{10,... | collective-permute-start | bytes 491528 | tf_op jit(solution)/shard_map/ppermute | solution.py:56
  62.4 54.5 %collective-permute-start.9 = (bf16[4,40,3584]{2,1,0:T(8,128)(2,1)S(1)}, bf16[4,40,3584]{2,1,0:T(8,128)(2,1)S(1)}, u32[]{:S(2)}, u32[]{:S(2)}) collective-permute-start(bf16[4,40,3584]{2,1,0:T(8,128)(2,1)S(1)} %get-tuple-element.65), channel_id=1, source_target_pairs={{0,2},{1,3},{2,0},{3,1},{4,6},{5,7},{6,4},{7,5},{8,10},{9,11},{10,... | collective-permute-start | bytes 3440648 | tf_op jit(solution)/shard_map/ppermute | solution.py:56
  62.5 27.9 %collective-permute-start.24 = (bf16[128,1664]{1,0:T(8,128)(2,1)S(1)}, bf16[128,1664]{1,0:T(8,128)(2,1)S(1)}, u32[]{:S(2)}, u32[]{:S(2)}) collective-permute-start(bf16[128,1664]{1,0:T(8,128)(2,1)S(1)} %get-tuple-element.88), channel_id=1, source_target_pairs={{0,24},{1,25},{2,26},{3,27},{4,28},{5,29},{6,30},{7,31},{8,16},{9,... | collective-permute-start | bytes 1277960 | tf_op jit(solution)/shard_map/ppermute | solution.py:56
  65.4 27.8 %collective-permute-start.25 = (bf16[128,1664]{1,0:T(8,128)(2,1)S(1)}, bf16[128,1664]{1,0:T(8,128)(2,1)S(1)}, u32[]{:S(2)}, u32[]{:S(2)}) collective-permute-start(bf16[128,1664]{1,0:T(8,128)(2,1)S(1)} %get-tuple-element.88), channel_id=1, source_target_pairs={{0,4},{1,5},{2,6},{3,7},{4,0},{5,1},{6,2},{7,3},{8,12},{9,13},{10,... | collective-permute-start | bytes 1277960 | tf_op jit(solution)/shard_map/ppermute | solution.py:56
  88.3 27.0 %collective-permute-start.27 = (bf16[128,1664]{1,0:T(8,128)(2,1)S(1)}, bf16[128,1664]{1,0:T(8,128)(2,1)S(1)}, u32[]{:S(2)}, u32[]{:S(2)}) collective-permute-start(bf16[128,1664]{1,0:T(8,128)(2,1)S(1)} %collective-permute-done.23), channel_id=1, source_target_pairs={{0,4},{1,5},{2,6},{3,7},{4,0},{5,1},{6,2},{7,3},{8,12},{9,13},{10,... | collective-permute-start | bytes 1277960 | tf_op jit(solution)/shard_map/ppermute | solution.py:56
  89.4 25.8 %collective-permute-start.26 = (bf16[128,1664]{1,0:T(8,128)(2,1)S(1)}, bf16[128,1664]{1,0:T(8,128)(2,1)S(1)}, u32[]{:S(2)}, u32[]{:S(2)}) collective-permute-start(bf16[128,1664]{1,0:T(8,128)(2,1)S(1)} %collective-permute-done.22), channel_id=1, source_target_pairs={{0,4},{1,5},{2,6},{3,7},{4,0},{5,1},{6,2},{7,3},{8,12},{9,13},{10,... | collective-permute-start | bytes 1277960 | tf_op jit(solution)/shard_map/ppermute | solution.py:56
  90.4 24.8 %collective-permute-start.28 = (bf16[128,1664]{1,0:T(8,128)(2,1)S(1)}, bf16[128,1664]{1,0:T(8,128)(2,1)S(1)}, u32[]{:S(2)}, u32[]{:S(2)}) collective-permute-start(bf16[128,1664]{1,0:T(8,128)(2,1)S(1)} %collective-permute-done.24), channel_id=1, source_target_pairs={{0,4},{1,5},{2,6},{3,7},{4,0},{5,1},{6,2},{7,3},{8,12},{9,13},{10,... | collective-permute-start | bytes 1277960 | tf_op jit(solution)/shard_map/ppermute | solution.py:56
  116.8 57.5 %collective-permute-start.29 = (bf16[1664,640]{1,0:T(8,128)(2,1)S(1)}, bf16[1664,640]{1,0:T(8,128)(2,1)}, u32[]{:S(2)}, u32[]{:S(2)}) collective-permute-start(bf16[1664,640]{1,0:T(8,128)(2,1)S(1)} %multiply_convert_fusion.own), channel_id=1, source_target_pairs={{0,2},{1,3},{2,0},{3,1},{4,6},{5,7},{6,4},{7,5},{8,10},{9,11},{10,... | collective-permute-start | bytes 6389768 | tf_op jit(solution)/shard_map/ppermute | solution.py:56
  117.1 9.3 %collective-permute-start.30 = (bf16[40,3584]{1,0:T(8,128)(2,1)S(1)}, bf16[40,3584]{1,0:T(8,128)(2,1)S(1)}, u32[]{:S(2)}, u32[]{:S(2)}) collective-permute-start(bf16[40,3584]{1,0:T(8,128)(2,1)S(1)} %get-tuple-element.76), channel_id=1, source_target_pairs={{0,1},{1,0},{2,3},{3,2},{4,5},{5,4},{6,7},{7,6},{8,9},{9,8},{10,11... | collective-permute-start | bytes 860168 | tf_op jit(solution)/shard_map/ppermute | solution.py:56
  117.6 9.7 %collective-permute-start.31 = (bf16[40,3584]{1,0:T(8,128)(2,1)S(1)}, bf16[40,3584]{1,0:T(8,128)(2,1)S(1)}, u32[]{:S(2)}, u32[]{:S(2)}) collective-permute-start(bf16[40,3584]{1,0:T(8,128)(2,1)S(1)} %get-tuple-element.77), channel_id=1, source_target_pairs={{0,4},{1,5},{2,6},{3,7},{4,0},{5,1},{6,2},{7,3},{8,12},{9,13},{10,... | collective-permute-start | bytes 860168 | tf_op jit(solution)/shard_map/ppermute | solution.py:56
  119.3 14.4 %collective-permute-start.32 = (bf16[40,3584]{1,0:T(8,128)(2,1)S(1)}, bf16[40,3584]{1,0:T(8,128)(2,1)S(1)}, u32[]{:S(2)}, u32[]{:S(2)}) collective-permute-start(bf16[40,3584]{1,0:T(8,128)(2,1)S(1)} %get-tuple-element.78), channel_id=1, source_target_pairs={{0,5},{1,4},{2,7},{3,6},{4,1},{5,0},{6,3},{7,2},{8,13},{9,12},{10,... | collective-permute-start | bytes 860168 | tf_op jit(solution)/shard_map/ppermute | solution.py:56
  133.9 6.9 %collective-permute-start.35 = (bf16[40,896]{1,0:T(8,128)(2,1)S(1)}, bf16[40,896]{1,0:T(8,128)(2,1)S(1)}, u32[]{:S(2)}, u32[]{:S(2)}) collective-permute-start(bf16[40,896]{1,0:T(8,128)(2,1)S(1)} %get-tuple-element.82), channel_id=1, source_target_pairs={{0,24},{1,25},{2,26},{3,27},{4,28},{5,29},{6,30},{7,31},{8,16},{9,... | collective-permute-start | bytes 215048 | tf_op jit(solution)/shard_map/ppermute | solution.py:56
  134.0 6.8 %collective-permute-start.34 = (bf16[40,896]{1,0:T(8,128)(2,1)S(1)}, bf16[40,896]{1,0:T(8,128)(2,1)S(1)}, u32[]{:S(2)}, u32[]{:S(2)}) collective-permute-start(bf16[40,896]{1,0:T(8,128)(2,1)S(1)} %get-tuple-element.81), channel_id=1, source_target_pairs={{0,16},{1,17},{2,18},{3,19},{4,20},{5,21},{6,22},{7,23},{8,24},{9,... | collective-permute-start | bytes 215048 | tf_op jit(solution)/shard_map/ppermute | solution.py:56
  134.1 7.5 %collective-permute-start.33 = (bf16[40,896]{1,0:T(8,128)(2,1)S(1)}, bf16[40,896]{1,0:T(8,128)(2,1)S(1)}, u32[]{:S(2)}, u32[]{:S(2)}) collective-permute-start(bf16[40,896]{1,0:T(8,128)(2,1)S(1)} %get-tuple-element.80), channel_id=1, source_target_pairs={{0,8},{1,9},{2,10},{3,11},{4,12},{5,13},{6,14},{7,15},{8,0},{9,1},... | collective-permute-start | bytes 215048 | tf_op jit(solution)/shard_map/ppermute | solution.py:56
  141.6 6.7 %collective-permute-start.38 = (bf16[40,896]{1,0:T(8,128)(2,1)S(1)}, bf16[40,896]{1,0:T(8,128)(2,1)S(1)}, u32[]{:S(2)}, u32[]{:S(2)}) collective-permute-start(bf16[40,896]{1,0:T(8,128)(2,1)S(1)} %multiply_convert_fusion.1), channel_id=1, source_target_pairs={{0,24},{1,25},{2,26},{3,27},{4,28},{5,29},{6,30},{7,31},{8,16},{9,... | collective-permute-start | bytes 215048 | tf_op jit(solution)/shard_map/ppermute | solution.py:56
  143.7 6.1 %collective-permute-start.37 = (bf16[40,896]{1,0:T(8,128)(2,1)S(1)}, bf16[40,896]{1,0:T(8,128)(2,1)S(1)}, u32[]{:S(2)}, u32[]{:S(2)}) collective-permute-start(bf16[40,896]{1,0:T(8,128)(2,1)S(1)} %multiply_convert_fusion.1), channel_id=1, source_target_pairs={{0,16},{1,17},{2,18},{3,19},{4,20},{5,21},{6,22},{7,23},{8,24},{9,... | collective-permute-start | bytes 215048 | tf_op jit(solution)/shard_map/ppermute | solution.py:56
  149.8 8.9 %collective-permute-start.39 = (bf16[40,3584]{1,0:T(8,128)(2,1)S(1)}, bf16[40,3584]{1,0:T(8,128)(2,1)S(1)}, u32[]{:S(2)}, u32[]{:S(2)}) collective-permute-start(bf16[40,3584]{1,0:T(8,128)(2,1)S(1)} %pad_maximum_fusion.refs_0_), channel_id=1, source_target_pairs={{0,1},{1,0},{2,3},{3,2},{4,5},{5,4},{6,7},{7,6},{8,9},{9,8},{10,11... | collective-permute-start | bytes 860168 | tf_op jit(solution)/shard_map/ppermute | solution.py:56
  150.4 9.7 %collective-permute-start.40 = (bf16[40,3584]{1,0:T(8,128)(2,1)S(1)}, bf16[40,3584]{1,0:T(8,128)(2,1)S(1)}, u32[]{:S(2)}, u32[]{:S(2)}) collective-permute-start(bf16[40,3584]{1,0:T(8,128)(2,1)S(1)} %pad_maximum_fusion.refs_0_), channel_id=1, source_target_pairs={{0,4},{1,5},{2,6},{3,7},{4,0},{5,1},{6,2},{7,3},{8,12},{9,13},{10,... | collective-permute-start | bytes 860168 | tf_op jit(solution)/shard_map/ppermute | solution.py:56
  152.0 12.2 %collective-permute-start.41 = (bf16[40,3584]{1,0:T(8,128)(2,1)S(1)}, bf16[40,3584]{1,0:T(8,128)(2,1)S(1)}, u32[]{:S(2)}, u32[]{:S(2)}) collective-permute-start(bf16[40,3584]{1,0:T(8,128)(2,1)S(1)} %pad_maximum_fusion.refs_0_), channel_id=1, source_target_pairs={{0,5},{1,4},{2,7},{3,6},{4,1},{5,0},{6,3},{7,2},{8,13},{9,12},{10,... | collective-permute-start | bytes 860168 | tf_op jit(solution)/shard_map/ppermute | solution.py:56
  155.2 15.4 %collective-permute-start.42 = (bf16[40,3584]{1,0:T(8,128)(2,1)S(1)}, bf16[40,3584]{1,0:T(8,128)(2,1)}, u32[]{:S(2)}, u32[]{:S(2)}) collective-permute-start(bf16[40,3584]{1,0:T(8,128)(2,1)S(1)} %pad_maximum_fusion.refs_0_), channel_id=1, source_target_pairs={{0,2},{1,3},{2,0},{3,1},{4,6},{5,7},{6,4},{7,5},{8,10},{9,11},{10,... | collective-permute-start | bytes 860168 | tf_op jit(solution)/shard_map/ppermute | solution.py:56
  158.7 12.0 %collective-permute-start.43 = (bf16[40,3584]{1,0:T(8,128)(2,1)S(1)}, bf16[40,3584]{1,0:T(8,128)(2,1)}, u32[]{:S(2)}, u32[]{:S(2)}) collective-permute-start(bf16[40,3584]{1,0:T(8,128)(2,1)S(1)} %collective-permute-done.39.refs_1_), channel_id=1, source_target_pairs={{0,2},{1,3},{2,0},{3,1},{4,6},{5,7},{6,4},{7,5},{8,10},{9,11},{10,... | collective-permute-start | bytes 860168 | tf_op jit(solution)/shard_map/ppermute | solution.py:56
  160.1 10.6 %collective-permute-start.44 = (bf16[40,3584]{1,0:T(8,128)(2,1)S(1)}, bf16[40,3584]{1,0:T(8,128)(2,1)}, u32[]{:S(2)}, u32[]{:S(2)}) collective-permute-start(bf16[40,3584]{1,0:T(8,128)(2,1)S(1)} %collective-permute-done.40.refs_2_), channel_id=1, source_target_pairs={{0,2},{1,3},{2,0},{3,1},{4,6},{5,7},{6,4},{7,5},{8,10},{9,11},{10,... | collective-permute-start | bytes 860168 | tf_op jit(solution)/shard_map/ppermute | solution.py:56
  164.2 6.5 %collective-permute-start.45 = (bf16[40,3584]{1,0:T(8,128)(2,1)S(1)}, bf16[40,3584]{1,0:T(8,128)(2,1)}, u32[]{:S(2)}, u32[]{:S(2)}) collective-permute-start(bf16[40,3584]{1,0:T(8,128)(2,1)S(1)} %collective-permute-done.41.refs_3_), channel_id=1, source_target_pairs={{0,2},{1,3},{2,0},{3,1},{4,6},{5,7},{6,4},{7,5},{8,10},{9,11},{10,... | collective-permute-start | bytes 860168 | tf_op jit(solution)/shard_map/ppermute | solution.py:56
  (23 other events, 231.2 us)
where the time goes:
time: 179 us; the launch traced here: 178 us
  waiting for transfers between devices  85.4 us (48%)
  starting transfers between devices  48.5 us (27%)
  Pallas kernels  29.7 us (17%)
  matrix products  7.41 us (4%)
  local copies, waits for them, and re-layouts  2.67 us (1%)
  between operations  2.5 us (1%)
  other arithmetic  1.98 us (1%)
    ppermute x45, waiting for transfers between devices, swap(): return lax.ppermute(block, GRID, [(i, i ^ mask) for i in range(total)])  85.4 us
    ppermute x45, starting transfers between devices, swap(): return lax.ppermute(block, GRID, [(i, i ^ mask) for i in range(total)])  46.9 us
    pallas_call x9, Pallas kernels, call(): pl.pallas_call(kernel, out_shape=[x if k in leave else pltpu.VMEM(x.shape...  17.9 us
    dot_general x3, matrix products, product(): lax.dot_general(left, right, ((sides[:1], sides[1:]), ((), ())), preferre...  7.41 us
    pallas_call x1, Pallas kernels, shards(): pl.pallas_call(functools.partial(condition_kernel, rows), out_shape=[jax....  4.14 us
    pallas_call x1, Pallas kernels, shards(): pl.pallas_call(join_kernel, out_shape=jax.ShapeDtypeStruct((features, pai...  3.69 us
  transfers between devices with their start and end apart: 46, of which 22 were waited for; matrix products, arithmetic and copies ran while one was open for 6% of the time, Pallas kernels for 9%

commit v1 on v0

--- a/solution.py
+++ b/solution.py
@@ -18,7 +18,7 @@
 SMEM = pl.BlockSpec(memory_space=pltpu.SMEM)
 
 
-LIMIT = 30 * 2**20
+LIMIT = 20 * 2**20
 
 
 def near_core(array):
@@ -417,33 +417,47 @@
                     all_rows[p * rows + r] = held[spot(image ^ (z * 4 + x * 2 + c), r)]
 
 
-def place_kernel(start, rows, blank, out, window, sem):
+def place_kernel(start, image, weight, blank, out, window, sem):
     span = window.shape[0]
     base = jnp.minimum((start[0] >> 4) << 4, out.shape[0] - span)
     token = lax.broadcasted_iota(jnp.int32, (span, SLOTS), 0)
     slot = lax.broadcasted_iota(jnp.int32, (span, SLOTS), 1)
     chosen = jnp.where(token == slot + (start[0] - base), 1.0, 0.0).astype(BF16)
-    window[...] = product(chosen, rows[...], (1, 0)).astype(BF16)
+    rows = product(image[...], weight[...], (1, 1)).astype(BF16)
+    window[...] = product(chosen, rows, (1, 0)).astype(BF16)
     store = pltpu.make_async_copy(window, out.at[pl.ds(pl.multiple_of(base, 16), span), :], sem)
     store.start()
     store.wait()
 
 
-def join_kernel(own, came, out, sems):
-    width = own.shape[0]
-    core = lax.axis_index("img") & 1
-    count = sems.shape[1]
+def join_kernel(flip, part, *refs):
+    out, sems = refs[-2:]
+    width = part.shape[0]
+    core = (lax.axis_index("img") & 1) ^ flip
+    count = sems.shape[0]
     depth = width // count
     stores = []
     for k in range(count):
-        for side, one in enumerate((own, came)):
-            start = (core if side == 0 else 1 - core) * width + k * depth
-            target = out.at[pl.ds(pl.multiple_of(start, 8), depth), :]
-            stores.append(pltpu.make_async_copy(one.at[k * depth : (k + 1) * depth, :], target, sems.at[side, k]))
+        target = out.at[pl.ds(pl.multiple_of(core * width + k * depth, 8), depth), :]
+        stores.append(pltpu.make_async_copy(part.at[k * depth : (k + 1) * depth, :], target, sems.at[k]))
     for one in stores:
         one.start()
     for one in stores:
         one.wait()
+
+
+def join_step(flip, part, base):
+    width, pair_width = part.shape
+    spare = pl.BlockSpec(memory_space=pl.ANY)
+    return pl.pallas_call(
+        functools.partial(join_kernel, flip),
+        out_shape=jax.ShapeDtypeStruct((2 * width, pair_width), BF16),
+        in_specs=[VMEM] + [spare] * len(base),
+        out_specs=spare,
+        scratch_shapes=[pltpu.SemaphoreType.DMA((4 if width % 64 == 0 else 1,))],
+        input_output_aliases={1: 0} if base else {},
+        compiler_params=pltpu.CompilerParams(vmem_limit_bytes=LIMIT),
+    )(near_core(part), *base)
 
 
 def blank_kernel(out, zeros, sems):
@@ -622,34 +636,32 @@
         scalars=1,
     )
     all_rows = all_rows.reshape(images * SLOTS, pair_width)
-    grad_condition = product(image_rows.reshape(SLOTS, pair_width), kv_weight, (1, 1)).astype(BF16)
     grad_hidden = pl.pallas_call(
         place_kernel,
         out_shape=jax.ShapeDtypeStruct((tokens, features), BF16),
-        in_specs=[SMEM, VMEM, pl.BlockSpec(memory_space=pl.ANY)],
+        in_specs=[SMEM, VMEM, VMEM, pl.BlockSpec(memory_space=pl.ANY)],
         out_specs=pl.BlockSpec(memory_space=pl.ANY),
         scratch_shapes=[pltpu.VMEM((span, features), BF16), pltpu.SemaphoreType.DMA],
-        input_output_aliases={2: 0},
+        input_output_aliases={3: 0},
+        compiler_params=pltpu.CompilerParams(vmem_limit_bytes=LIMIT),
         name="place",
-    )(slot_start, grad_condition, blank)
+    )(slot_start, near_core(image_rows.reshape(SLOTS, pair_width)), near_core(kv_weight), blank)
     wide = jnp.concatenate([final, *far], axis=1)
     parts = [wide] + [swap(wide, square_mask(j, rows)) for j in range(1, squares)]
 
     near_half = images * SLOTS // 2
-    across = [swap(near[j], 2 * rows) for j in range(lines)]
+    across = []
+    for j in range(lines):
+        if j % 2 and j > 1:
+            across.append(swap(across[j - 1], line_mask(1, rows)))
+        else:
+            across.append(swap(near[j], 2 * rows))
     total = product(jnp.concatenate(near), all_rows[:near_half], (0, 0))
     total = total + product(jnp.concatenate(across), all_rows[near_half:], (0, 0))
     weight_half = (total * (images * SLOTS) ** (-0.5)).astype(BF16)
     came = swap(weight_half, rows)
-    grad_kv_weight = pl.pallas_call(
-        join_kernel,
-        out_shape=jax.ShapeDtypeStruct((features, pair_width), BF16),
-        in_specs=[VMEM, VMEM],
-        out_specs=pl.BlockSpec(memory_space=pl.ANY),
-        scratch_shapes=[pltpu.SemaphoreType.DMA((2, 4 if half % 64 == 0 else 1))],
-        compiler_params=pltpu.CompilerParams(vmem_limit_bytes=LIMIT),
-        name="join",
-    )(near_core(weight_half), near_core(came))
+    grad_kv_weight = join_step(0, weight_half, [])
+    grad_kv_weight = join_step(1, came, [grad_kv_weight])
     others = [swap(one, rows) for one in parts]
     grad_res_weight, grad_query_weight, grad_out_weight = unpack_step(
         parts, others, channels, rows, lines

time: 179 us -> 171 us (0.955)
  waiting for transfers between devices: 85.4 us -> 79.8 us
  matrix products: 7.41 us -> 3.06 us
  local copies, waits for them, and re-layouts: 2.67 us -> 4.88 us
    ppermute x45, waiting for transfers between devices: 85.4 us -> 79.8 us  [swap(): return lax.ppermute(block, GRID, [(i, i ^ mask) for i in range(total)])]
    dot_general x3 -> x2, matrix products: 7.41 us -> 3.06 us  [product(): lax.dot_general(left, right, ((sides[:1], sides[1:]), ((), ())), preferre...]
    unnamed x23 -> x25, local copies, waits for them, and re-layouts: 2.32 us -> 4.52 us
    pallas_call x1 -> x2, Pallas kernels: 3.69 us -> 4.32 us  [join_step(): pl.pallas_call(functools.partial(join_kernel, flip), out_shape=jax.ShapeD...]
  transfers between devices with their start and end apart: 46 -> 46, of which waited for: 22 -> 23; matrix products, arithmetic and copies ran while one was open for 6% -> 4% of each run, Pallas kernels for 9% -> 11%
where the time goes in v1:
time: 171 us; the launch traced here: 170 us
  waiting for transfers between devices  79.8 us (47%)
  starting transfers between devices  47.3 us (28%)
  Pallas kernels  30.6 us (18%)
  local copies, waits for them, and re-layouts  4.88 us (3%)
  matrix products  3.06 us (2%)
  between operations  2.5 us (1%)
  other arithmetic  1.98 us (1%)
    ppermute x45, waiting for transfers between devices, swap(): return lax.ppermute(block, GRID, [(i, i ^ mask) for i in range(total)])  79.8 us
    ppermute x45, starting transfers between devices, swap(): return lax.ppermute(block, GRID, [(i, i ^ mask) for i in range(total)])  45.7 us
    pallas_call x9, Pallas kernels, call(): pl.pallas_call(kernel, out_shape=[x if k in leave else pltpu.VMEM(x.shape...  17.9 us
    unnamed x25, local copies, waits for them, and re-layouts  4.52 us
    pallas_call x2, Pallas kernels, join_step(): pl.pallas_call(functools.partial(join_kernel, flip), out_shape=jax.ShapeD...  4.32 us
    pallas_call x1, Pallas kernels, shards(): pl.pallas_call(functools.partial(condition_kernel, rows), out_shape=[jax....  4.15 us
  transfers between devices with their start and end apart: 46, of which 23 were waited for; matrix products, arithmetic and copies ran while one was open for 4% of the time, Pallas kernels for 11%

profile of v1, /device:TPU:0, one launch (start us, length us, event | category | flops | bytes accessed | tf_op | source)
XLA Modules:
  0.0 170.1 jit_solution(13101028848301097074)
XLA Ops:
  1.3 4.1 %condition.1 = (f32[32,640]{1,0:T(8,128)}, f32[32,640]{1,0:T(8,128)}, bf16[64,1664]{1,0:T(8,128)(2,1)}, bf16[64,1664]{1,0:T(8,128)(2,1)}) custom-call(s32[1]{0:T(128)S(6)} %copy.32.start, bf16[512,3328]{1,0:T(8,128)(2,1)} %hidden.1, bf16[3328,640]{1,0:T(8,128)(2,1)} %weight.3), custom_call_target="tpu_custom_call" | custom-call | flops 272629760 | bytes 5537792 | tf_op jit(solution)/shard_map/condition/pallas_call | solution.py:518
  5.5 3.1 %collective-permute-start.1 = (f32[32,640]{1,0:T(8,128)}, f32[32,640]{1,0:T(8,128)S(1)}, u32[]{:S(2)}, u32[]{:S(2)}) collective-permute-start(f32[32,640]{1,0:T(8,128)} %get-tuple-element.49), channel_id=1, source_target_pairs={{0,1},{1,0},{2,3},{3,2},{4,5},{5,4},{6,7},{7,6},{8,9},{9,8},{10,11... | collective-permute-start | bytes 245768 | tf_op jit(solution)/shard_map/ppermute | solution.py:56
  12.1 2.1 %collective-permute-start.2 = (bf16[32,640]{1,0:T(8,128)(2,1)S(1)}, bf16[32,640]{1,0:T(8,128)(2,1)S(1)}, u32[]{:S(2)}, u32[]{:S(2)}) collective-permute-start(bf16[32,640]{1,0:T(8,128)(2,1)S(1)} %add_convert_fusion.2.refs_0_), channel_id=1, source_target_pairs={{0,8},{1,9},{2,10},{3,11},{4,12},{5,13},{6,14},{7,15},{8,0},{9,1},... | collective-permute-start | bytes 122888 | tf_op jit(solution)/shard_map/ppermute | solution.py:56
  14.2 2.6 %collective-permute-start.3 = (bf16[32,640]{1,0:T(8,128)(2,1)S(1)}, bf16[32,640]{1,0:T(8,128)(2,1)S(1)}, u32[]{:S(2)}, u32[]{:S(2)}) collective-permute-start(bf16[32,640]{1,0:T(8,128)(2,1)S(1)} %add_convert_fusion.2.refs_0_), channel_id=1, source_target_pairs={{0,16},{1,17},{2,18},{3,19},{4,20},{5,21},{6,22},{7,23},{8,24},{9,... | collective-permute-start | bytes 122888 | tf_op jit(solution)/shard_map/ppermute | solution.py:56
  20.0 2.6 %collective-permute-done.4.refs_3_ = bf16[32,640]{1,0:T(8,128)(2,1)S(1)} collective-permute-done((bf16[32,640]{1,0:T(8,128)(2,1)S(1)}, bf16[32,640]{1,0:T(8,128)(2,1)S(1)}, u32[]{:S(2)}, u32[]{:S(2)}) %collective-permute-start.4) | collective-permute-done | bytes 40992 | tf_op jit(solution)/shard_map/ppermute | solution.py:56
  31.1 4.2 %shard_map.164 = (bf16[3,320,1280]{2,1,0:T(8,128)(2,1)S(1)}, bf16[320,1024]{1,0:T(8,128)(2,1)S(1)}, bf16[320,1024]{1,0:T(8,128)(2,1)S(1)}) custom-call(f32[4,8,128]{2,1,0:T(8,128)S(1)} %get-tuple-element.46.noisy, bf16[4,2,128]{2,1,0:T(2,128)(2,1)S(1)} %collective-permute-done.refs_0_, f32[320,1]{1,0:T(8,128)S(1)} %copy.20.refs_1_, ...), custom_call_target="tpu_custom_call" | custom-call | flops 2097152000 | bytes 5859072 | tf_op jit(solution)/shard_map/pallas_call | solution.py:32
  35.3 4.7 %shard_map.166 = (bf16[320,1024]{1,0:T(8,128)(2,1)S(1)}, f32[32,640]{1,0:T(8,128)S(1)}, bf16[320,1024]{1,0:T(8,128)(2,1)S(1)}, f32[320,320]{1,0:T(8,128)S(1)}, f...) custom-call(bf16[320,1024]{1,0:T(8,128)(2,1)S(1)} %get-tuple-element.52.query, ...), custom_call_target="tpu_custom_call" | custom-call | flops 1300234240 | bytes 4710400 | tf_op jit(solution)/shard_map/pallas_call | solution.py:32
  40.6 3.5 %collective-permute-done.10 = bf16[32,640]{1,0:T(8,128)(2,1)S(1)} collective-permute-done((bf16[32,640]{1,0:T(8,128)(2,1)S(1)}, bf16[32,640]{1,0:T(8,128)(2,1)S(1)}, u32[]{:S(2)}, u32[]{:S(2)}) %collective-permute-start.10) | collective-permute-done | bytes 40992 | tf_op jit(solution)/shard_map/ppermute | solution.py:56
  45.1 3.4 %collective-permute-start.13 = (bf16[32,640]{1,0:T(8,128)(2,1)S(1)}, bf16[32,640]{1,0:T(8,128)(2,1)S(1)}, u32[]{:S(2)}, u32[]{:S(2)}) collective-permute-start(bf16[32,640]{1,0:T(8,128)(2,1)S(1)} %add_convert_fusion), channel_id=1, source_target_pairs={{0,24},{1,25},{2,26},{3,27},{4,28},{5,29},{6,30},{7,31},{8,16},{9,... | collective-permute-start | bytes 122888 | tf_op jit(solution)/shard_map/ppermute | solution.py:56
  52.4 2.1 %collective-permute-start.16 = (bf16[4,32,640]{2,1,0:T(8,128)(2,1)S(1)}, bf16[4,32,640]{2,1,0:T(8,128)(2,1)S(1)}, u32[]{:S(2)}, u32[]{:S(2)}) collective-permute-start(bf16[4,32,640]{2,1,0:T(8,128)(2,1)S(1)} %pad_maximum_fusion.1.refs_0_), channel_id=1, source_target_pairs={{0,5},{1,4},{2,7},{3,6},{4,1},{5,0},{6,3},{7,2},{8,13},{9,12},{10,... | collective-permute-start | bytes 491528 | tf_op jit(solution)/shard_map/ppermute | solution.py:56
  54.8 2.7 %collective-permute-done.14.refs_1_ = bf16[4,32,640]{2,1,0:T(8,128)(2,1)S(1)} collective-permute-done((bf16[4,32,640]{2,1,0:T(8,128)(2,1)S(1)}, bf16[4,32,640]{2,1,0:T(8,128)(2,1)S(1)}, u32[]{:S(2)}, u32[]{:S(2)}) %collective-permute-start.14) | collective-permute-done | bytes 163872 | tf_op jit(solution)/shard_map/ppermute | solution.py:56
  60.1 3.4 %shard_map.167 = (f32[4,40,3584]{2,1,0:T(8,128)S(1)}, bf16[4,40,3584]{2,1,0:T(8,128)(2,1)S(1)}) custom-call(bf16[320,1024]{1,0:T(8,128)(2,1)S(1)} %get-tuple-element.60.grad_hid, bf16[3,320,1280]{2,1,0:T(8,128)(2,1)S(1)} %get-tuple-element.61.acts, f32[320,320]{1,0:T(8,128)S(1)} %get-tuple-element.62.query_grad, f32[320,320]{1,0:T(8,128)S(1)} %get-tuple-element.63.out_grad), custom_call_target="tpu_custom_call" | custom-call | flops 1887436800 | bytes 7372800 | tf_op jit(solution)/shard_map/pallas_call | solution.py:32
  63.6 3.4 %collective-permute-start.24 = (bf16[128,1664]{1,0:T(8,128)(2,1)S(1)}, bf16[128,1664]{1,0:T(8,128)(2,1)S(1)}, u32[]{:S(2)}, u32[]{:S(2)}) collective-permute-start(bf16[128,1664]{1,0:T(8,128)(2,1)S(1)} %get-tuple-element.88), channel_id=1, source_target_pairs={{0,24},{1,25},{2,26},{3,27},{4,28},{5,29},{6,30},{7,31},{8,16},{9,... | collective-permute-start | bytes 1277960 | tf_op jit(solution)/shard_map/ppermute | solution.py:56
  68.8 19.4 %collective-permute-done.23 = bf16[128,1664]{1,0:T(8,128)(2,1)S(1)} collective-permute-done((bf16[128,1664]{1,0:T(8,128)(2,1)S(1)}, bf16[128,1664]{1,0:T(8,128)(2,1)S(1)}, u32[]{:S(2)}, u32[]{:S(2)}) %collective-permute-start.23) | collective-permute-done | bytes 426016 | tf_op jit(solution)/shard_map/ppermute | solution.py:56
  90.4 6.0 %collective-permute-done.27 = bf16[128,1664]{1,0:T(8,128)(2,1)S(1)} collective-permute-done((bf16[128,1664]{1,0:T(8,128)(2,1)S(1)}, bf16[128,1664]{1,0:T(8,128)(2,1)S(1)}, u32[]{:S(2)}, u32[]{:S(2)}) %collective-permute-start.27) | collective-permute-done | bytes 426016 | tf_op jit(solution)/shard_map/ppermute | solution.py:56
  99.0 2.0 %collective-permute-done.26 = bf16[128,1664]{1,0:T(8,128)(2,1)S(1)} collective-permute-done((bf16[128,1664]{1,0:T(8,128)(2,1)S(1)}, bf16[128,1664]{1,0:T(8,128)(2,1)S(1)}, u32[]{:S(2)}, u32[]{:S(2)}) %collective-permute-start.26) | collective-permute-done | bytes 426016 | tf_op jit(solution)/shard_map/ppermute | solution.py:56
  101.0 3.6 %collective-permute-done.28 = bf16[128,1664]{1,0:T(8,128)(2,1)S(1)} collective-permute-done((bf16[128,1664]{1,0:T(8,128)(2,1)S(1)}, bf16[128,1664]{1,0:T(8,128)(2,1)S(1)}, u32[]{:S(2)}, u32[]{:S(2)}) %collective-permute-start.28) | collective-permute-done | bytes 426016 | tf_op jit(solution)/shard_map/ppermute | solution.py:56
  107.7 2.2 %collective-permute-start.32 = (bf16[40,3584]{1,0:T(8,128)(2,1)S(1)}, bf16[40,3584]{1,0:T(8,128)(2,1)S(1)}, u32[]{:S(2)}, u32[]{:S(2)}) collective-permute-start(bf16[40,3584]{1,0:T(8,128)(2,1)S(1)} %get-tuple-element.78), channel_id=1, source_target_pairs={{0,5},{1,4},{2,7},{3,6},{4,1},{5,0},{6,3},{7,2},{8,13},{9,12},{10,... | collective-permute-start | bytes 860168 | tf_op jit(solution)/shard_map/ppermute | solution.py:56
  110.9 4.8 %collective-permute-done.30.refs_1_ = bf16[40,3584]{1,0:T(8,128)(2,1)S(1)} collective-permute-done((bf16[40,3584]{1,0:T(8,128)(2,1)S(1)}, bf16[40,3584]{1,0:T(8,128)(2,1)S(1)}, u32[]{:S(2)}, u32[]{:S(2)}) %collective-permute-start.30) | collective-permute-done | bytes 286752 | tf_op jit(solution)/shard_map/ppermute | solution.py:56
  116.6 6.3 %collective-permute-done.32.refs_3_ = bf16[40,3584]{1,0:T(8,128)(2,1)S(1)} collective-permute-done((bf16[40,3584]{1,0:T(8,128)(2,1)S(1)}, bf16[40,3584]{1,0:T(8,128)(2,1)S(1)}, u32[]{:S(2)}, u32[]{:S(2)}) %collective-permute-start.32) | collective-permute-done | bytes 286752 | tf_op jit(solution)/shard_map/ppermute | solution.py:56
  124.3 3.4 %collective-permute-start.34 = (bf16[40,896]{1,0:T(8,128)(2,1)S(1)}, bf16[40,896]{1,0:T(8,128)(2,1)S(1)}, u32[]{:S(2)}, u32[]{:S(2)}) collective-permute-start(bf16[40,896]{1,0:T(8,128)(2,1)S(1)} %get-tuple-element.81), channel_id=1, source_target_pairs={{0,16},{1,17},{2,18},{3,19},{4,20},{5,21},{6,22},{7,23},{8,24},{9,... | collective-permute-start | bytes 215048 | tf_op jit(solution)/shard_map/ppermute | solution.py:56
  127.7 4.5 %collective-permute-done.34 = bf16[40,896]{1,0:T(8,128)(2,1)S(1)} collective-permute-done((bf16[40,896]{1,0:T(8,128)(2,1)S(1)}, bf16[40,896]{1,0:T(8,128)(2,1)S(1)}, u32[]{:S(2)}, u32[]{:S(2)}) %collective-permute-start.34) | collective-permute-done | bytes 71712 | tf_op jit(solution)/shard_map/ppermute | solution.py:56
  133.9 2.1 %collective-permute-start.37 = (bf16[40,896]{1,0:T(8,128)(2,1)S(1)}, bf16[40,896]{1,0:T(8,128)(2,1)S(1)}, u32[]{:S(2)}, u32[]{:S(2)}) collective-permute-start(bf16[40,896]{1,0:T(8,128)(2,1)S(1)} %multiply_convert_fusion.1), channel_id=1, source_target_pairs={{0,16},{1,17},{2,18},{3,19},{4,20},{5,21},{6,22},{7,23},{8,24},{9,... | collective-permute-start | bytes 215048 | tf_op jit(solution)/shard_map/ppermute | solution.py:56
  136.1 2.2 %collective-permute-start.38 = (bf16[40,896]{1,0:T(8,128)(2,1)S(1)}, bf16[40,896]{1,0:T(8,128)(2,1)S(1)}, u32[]{:S(2)}, u32[]{:S(2)}) collective-permute-start(bf16[40,896]{1,0:T(8,128)(2,1)S(1)} %multiply_convert_fusion.1), channel_id=1, source_target_pairs={{0,24},{1,25},{2,26},{3,27},{4,28},{5,29},{6,30},{7,31},{8,16},{9,... | collective-permute-start | bytes 215048 | tf_op jit(solution)/shard_map/ppermute | solution.py:56
  138.3 2.3 %collective-permute-done.37 = bf16[40,896]{1,0:T(8,128)(2,1)S(1)} collective-permute-done((bf16[40,896]{1,0:T(8,128)(2,1)S(1)}, bf16[40,896]{1,0:T(8,128)(2,1)S(1)}, u32[]{:S(2)}, u32[]{:S(2)}) %collective-permute-start.37) | collective-permute-done | bytes 71712 | tf_op jit(solution)/shard_map/ppermute | solution.py:56
  143.6 2.1 %collective-permute-start.41 = (bf16[40,3584]{1,0:T(8,128)(2,1)S(1)}, bf16[40,3584]{1,0:T(8,128)(2,1)S(1)}, u32[]{:S(2)}, u32[]{:S(2)}) collective-permute-start(bf16[40,3584]{1,0:T(8,128)(2,1)S(1)} %pad_maximum_fusion.refs_0_), channel_id=1, source_target_pairs={{0,5},{1,4},{2,7},{3,6},{4,1},{5,0},{6,3},{7,2},{8,13},{9,12},{10,... | collective-permute-start | bytes 860168 | tf_op jit(solution)/shard_map/ppermute | solution.py:56
  145.8 6.2 %collective-permute-done.39.refs_1_ = bf16[40,3584]{1,0:T(8,128)(2,1)S(1)} collective-permute-done((bf16[40,3584]{1,0:T(8,128)(2,1)S(1)}, bf16[40,3584]{1,0:T(8,128)(2,1)S(1)}, u32[]{:S(2)}, u32[]{:S(2)}) %collective-permute-start.39) | collective-permute-done | bytes 286752 | tf_op jit(solution)/shard_map/ppermute | solution.py:56
  152.5 3.0 %collective-permute-done.41.refs_3_ = bf16[40,3584]{1,0:T(8,128)(2,1)S(1)} collective-permute-done((bf16[40,3584]{1,0:T(8,128)(2,1)S(1)}, bf16[40,3584]{1,0:T(8,128)(2,1)S(1)}, u32[]{:S(2)}, u32[]{:S(2)}) %collective-permute-start.41) | collective-permute-done | bytes 286752 | tf_op jit(solution)/shard_map/ppermute | solution.py:56
  157.4 2.2 %copy-done = bf16[3328,640]{1,0:T(8,128)(2,1)S(1)} copy-done((bf16[3328,640]{1,0:T(8,128)(2,1)S(1)}, bf16[3328,640]{1,0:T(8,128)(2,1)}, u32[]{:S(2)}) %copy-start) | copy-done | bytes 4259864
  159.6 2.4 %place.1 = bf16[512,3328]{1,0:T(8,128)(2,1)} custom-call(s32[1]{0:T(128)S(6)} %copy.32.start, bf16[64,640]{1,0:T(8,128)(2,1)S(1)} %bitcast.24, bf16[3328,640]{1,0:T(8,128)(2,1)S(1)} %copy-done, bf16[512,3328]{1,0:T(8,128)(2,1)} %blank.1), custom_call_target="tpu_custom_call", output_to_operand_aliasing={{}: (3, {})} | custom-call | tf_op jit(solution)/shard_map/place/pallas_call | solution.py:639
  163.5 3.5 %shard_map.173 = (bf16[9,320,320]{2,1,0:T(8,128)(2,1)}, bf16[320,320]{1,0:T(8,128)(2,1)}, bf16[320,320]{1,0:T(8,128)(2,1)}) custom-call(bf16[40,3584]{1,0:T(8,128)(2,1)S(1)} %pad_maximum_fusion.refs_0_, bf16[40,3584]{1,0:T(8,128)(2,1)S(1)} %collective-permute-done.39.refs_1_, bf16[40,3584]{1,0:T(8,128)(2,1)S(1)} %collective-permute-done.40.refs_2_, ...), custom_call_target="tpu_custom_call" | custom-call | bytes 4546560 | tf_op jit(solution)/shard_map/pallas_call | solution.py:32
  167.0 3.0 %shard_map.171 = bf16[3328,640]{1,0:T(8,128)(2,1)} custom-call(bf16[1664,640]{1,0:T(8,128)(2,1)} %collective-permute-done.29.part, bf16[3328,640]{1,0:T(8,128)(2,1)} %shard_map.170.refs_0_), custom_call_target="tpu_custom_call", output_to_operand_aliasing={{}: (1, {})} | custom-call | tf_op jit(solution)/shard_map/pallas_call | solution.py:452
  (115 shorter events, 44.3 us)
Async XLA Ops:
  12.1 6.0 %collective-permute-start.2 = (bf16[32,640]{1,0:T(8,128)(2,1)S(1)}, bf16[32,640]{1,0:T(8,128)(2,1)S(1)}, u32[]{:S(2)}, u32[]{:S(2)}) collective-permute-start(bf16[32,640]{1,0:T(8,128)(2,1)S(1)} %add_convert_fusion.2.refs_0_), channel_id=1, source_target_pairs={{0,8},{1,9},{2,10},{3,11},{4,12},{5,13},{6,14},{7,15},{8,0},{9,1},... | collective-permute-start | bytes 122888 | tf_op jit(solution)/shard_map/ppermute | solution.py:56
  16.8 5.8 %collective-permute-start.4 = (bf16[32,640]{1,0:T(8,128)(2,1)S(1)}, bf16[32,640]{1,0:T(8,128)(2,1)S(1)}, u32[]{:S(2)}, u32[]{:S(2)}) collective-permute-start(bf16[32,640]{1,0:T(8,128)(2,1)S(1)} %add_convert_fusion.2.refs_0_), channel_id=1, source_target_pairs={{0,24},{1,25},{2,26},{3,27},{4,28},{5,29},{6,30},{7,31},{8,16},{9,... | collective-permute-start | bytes 122888 | tf_op jit(solution)/shard_map/ppermute | solution.py:56
  29.4 5.8 %collective-permute-start.8 = (bf16[32,640]{1,0:T(8,128)(2,1)S(1)}, bf16[32,640]{1,0:T(8,128)(2,1)S(1)}, u32[]{:S(2)}, u32[]{:S(2)}) collective-permute-start(bf16[32,640]{1,0:T(8,128)(2,1)S(1)} %add_convert_fusion.1.refs_0_), channel_id=1, source_target_pairs={{0,1},{1,0},{2,3},{3,2},{4,5},{5,4},{6,7},{7,6},{8,9},{9,8},{10,11... | collective-permute-start | bytes 122888 | tf_op jit(solution)/shard_map/ppermute | solution.py:56
  40.6 14.0 %collective-permute-start.21 = (bf16[64,1664]{1,0:T(8,128)(2,1)S(1)}, bf16[64,1664]{1,0:T(8,128)(2,1)S(1)}, u32[]{:S(2)}, u32[]{:S(2)}) collective-permute-start(bf16[64,1664]{1,0:T(8,128)(2,1)S(1)} %copy-done.9), channel_id=1, source_target_pairs={{0,2},{1,3},{2,0},{3,1},{4,6},{5,7},{6,4},{7,5},{8,10},{9,11},{10,... | collective-permute-start | bytes 638984 | tf_op jit(solution)/shard_map/ppermute | solution.py:56
  45.1 5.8 %collective-permute-start.13 = (bf16[32,640]{1,0:T(8,128)(2,1)S(1)}, bf16[32,640]{1,0:T(8,128)(2,1)S(1)}, u32[]{:S(2)}, u32[]{:S(2)}) collective-permute-start(bf16[32,640]{1,0:T(8,128)(2,1)S(1)} %add_convert_fusion), channel_id=1, source_target_pairs={{0,24},{1,25},{2,26},{3,27},{4,28},{5,29},{6,30},{7,31},{8,16},{9,... | collective-permute-start | bytes 122888 | tf_op jit(solution)/shard_map/ppermute | solution.py:56
  51.0 6.5 %collective-permute-start.14 = (bf16[4,32,640]{2,1,0:T(8,128)(2,1)S(1)}, bf16[4,32,640]{2,1,0:T(8,128)(2,1)S(1)}, u32[]{:S(2)}, u32[]{:S(2)}) collective-permute-start(bf16[4,32,640]{2,1,0:T(8,128)(2,1)S(1)} %pad_maximum_fusion.1.refs_0_), channel_id=1, source_target_pairs={{0,1},{1,0},{2,3},{3,2},{4,5},{5,4},{6,7},{7,6},{8,9},{9,8},{10,11... | collective-permute-start | bytes 491528 | tf_op jit(solution)/shard_map/ppermute | solution.py:56
  51.6 7.1 %collective-permute-start.15 = (bf16[4,32,640]{2,1,0:T(8,128)(2,1)S(1)}, bf16[4,32,640]{2,1,0:T(8,128)(2,1)S(1)}, u32[]{:S(2)}, u32[]{:S(2)}) collective-permute-start(bf16[4,32,640]{2,1,0:T(8,128)(2,1)S(1)} %pad_maximum_fusion.1.refs_0_), channel_id=1, source_target_pairs={{0,4},{1,5},{2,6},{3,7},{4,0},{5,1},{6,2},{7,3},{8,12},{9,13},{10,... | collective-permute-start | bytes 491528 | tf_op jit(solution)/shard_map/ppermute | solution.py:56
  52.4 7.2 %collective-permute-start.16 = (bf16[4,32,640]{2,1,0:T(8,128)(2,1)S(1)}, bf16[4,32,640]{2,1,0:T(8,128)(2,1)S(1)}, u32[]{:S(2)}, u32[]{:S(2)}) collective-permute-start(bf16[4,32,640]{2,1,0:T(8,128)(2,1)S(1)} %pad_maximum_fusion.1.refs_0_), channel_id=1, source_target_pairs={{0,5},{1,4},{2,7},{3,6},{4,1},{5,0},{6,3},{7,2},{8,13},{9,12},{10,... | collective-permute-start | bytes 491528 | tf_op jit(solution)/shard_map/ppermute | solution.py:56
  54.6 34.4 %collective-permute-start.22 = (bf16[128,1664]{1,0:T(8,128)(2,1)S(1)}, bf16[128,1664]{1,0:T(8,128)(2,1)S(1)}, u32[]{:S(2)}, u32[]{:S(2)}) collective-permute-start(bf16[128,1664]{1,0:T(8,128)(2,1)S(1)} %get-tuple-element.88), channel_id=1, source_target_pairs={{0,8},{1,9},{2,10},{3,11},{4,12},{5,13},{6,14},{7,15},{8,0},{9,1},... | collective-permute-start | bytes 1277960 | tf_op jit(solution)/shard_map/ppermute | solution.py:56
  57.5 30.8 %collective-permute-start.23 = (bf16[128,1664]{1,0:T(8,128)(2,1)S(1)}, bf16[128,1664]{1,0:T(8,128)(2,1)S(1)}, u32[]{:S(2)}, u32[]{:S(2)}) collective-permute-start(bf16[128,1664]{1,0:T(8,128)(2,1)S(1)} %get-tuple-element.88), channel_id=1, source_target_pairs={{0,16},{1,17},{2,18},{3,19},{4,20},{5,21},{6,22},{7,23},{8,24},{9,... | collective-permute-start | bytes 1277960 | tf_op jit(solution)/shard_map/ppermute | solution.py:56
  59.6 7.4 %collective-permute-start.20 = (bf16[4,32,640]{2,1,0:T(8,128)(2,1)S(1)}, bf16[4,32,640]{2,1,0:T(8,128)(2,1)S(1)}, u32[]{:S(2)}, u32[]{:S(2)}) collective-permute-start(bf16[4,32,640]{2,1,0:T(8,128)(2,1)S(1)} %collective-permute-done.16.refs_3_), channel_id=1, source_target_pairs={{0,2},{1,3},{2,0},{3,1},{4,6},{5,7},{6,4},{7,5},{8,10},{9,11},{10,... | collective-permute-start | bytes 491528 | tf_op jit(solution)/shard_map/ppermute | solution.py:56
  63.5 42.6 %collective-permute-start.9 = (bf16[4,40,3584]{2,1,0:T(8,128)(2,1)S(1)}, bf16[4,40,3584]{2,1,0:T(8,128)(2,1)S(1)}, u32[]{:S(2)}, u32[]{:S(2)}) collective-permute-start(bf16[4,40,3584]{2,1,0:T(8,128)(2,1)S(1)} %get-tuple-element.65), channel_id=1, source_target_pairs={{0,2},{1,3},{2,0},{3,1},{4,6},{5,7},{6,4},{7,5},{8,10},{9,11},{10,... | collective-permute-start | bytes 3440648 | tf_op jit(solution)/shard_map/ppermute | solution.py:56
  63.6 33.8 %collective-permute-start.24 = (bf16[128,1664]{1,0:T(8,128)(2,1)S(1)}, bf16[128,1664]{1,0:T(8,128)(2,1)S(1)}, u32[]{:S(2)}, u32[]{:S(2)}) collective-permute-start(bf16[128,1664]{1,0:T(8,128)(2,1)S(1)} %get-tuple-element.88), channel_id=1, source_target_pairs={{0,24},{1,25},{2,26},{3,27},{4,28},{5,29},{6,30},{7,31},{8,16},{9,... | collective-permute-start | bytes 1277960 | tf_op jit(solution)/shard_map/ppermute | solution.py:56
  67.0 31.9 %collective-permute-start.25 = (bf16[128,1664]{1,0:T(8,128)(2,1)S(1)}, bf16[128,1664]{1,0:T(8,128)(2,1)S(1)}, u32[]{:S(2)}, u32[]{:S(2)}) collective-permute-start(bf16[128,1664]{1,0:T(8,128)(2,1)S(1)} %get-tuple-element.88), channel_id=1, source_target_pairs={{0,4},{1,5},{2,6},{3,7},{4,0},{5,1},{6,2},{7,3},{8,12},{9,13},{10,... | collective-permute-start | bytes 1277960 | tf_op jit(solution)/shard_map/ppermute | solution.py:56
  88.3 8.1 %collective-permute-start.27 = (bf16[128,1664]{1,0:T(8,128)(2,1)S(1)}, bf16[128,1664]{1,0:T(8,128)(2,1)S(1)}, u32[]{:S(2)}, u32[]{:S(2)}) collective-permute-start(bf16[128,1664]{1,0:T(8,128)(2,1)S(1)} %collective-permute-done.23), channel_id=1, source_target_pairs={{0,4},{1,5},{2,6},{3,7},{4,0},{5,1},{6,2},{7,3},{8,12},{9,13},{10,... | collective-permute-start | bytes 1277960 | tf_op jit(solution)/shard_map/ppermute | solution.py:56
  89.0 11.9 %collective-permute-start.26 = (bf16[128,1664]{1,0:T(8,128)(2,1)S(1)}, bf16[128,1664]{1,0:T(8,128)(2,1)S(1)}, u32[]{:S(2)}, u32[]{:S(2)}) collective-permute-start(bf16[128,1664]{1,0:T(8,128)(2,1)S(1)} %collective-permute-done.22), channel_id=1, source_target_pairs={{0,4},{1,5},{2,6},{3,7},{4,0},{5,1},{6,2},{7,3},{8,12},{9,13},{10,... | collective-permute-start | bytes 1277960 | tf_op jit(solution)/shard_map/ppermute | solution.py:56
  96.4 8.1 %collective-permute-start.28 = (bf16[128,1664]{1,0:T(8,128)(2,1)S(1)}, bf16[128,1664]{1,0:T(8,128)(2,1)S(1)}, u32[]{:S(2)}, u32[]{:S(2)}) collective-permute-start(bf16[128,1664]{1,0:T(8,128)(2,1)S(1)} %collective-permute-done.27), channel_id=1, source_target_pairs={{0,8},{1,9},{2,10},{3,11},{4,12},{5,13},{6,14},{7,15},{8,0},{9,1},... | collective-permute-start | bytes 1277960 | tf_op jit(solution)/shard_map/ppermute | solution.py:56
  106.0 61.0 %collective-permute-start.29 = (bf16[1664,640]{1,0:T(8,128)(2,1)S(1)}, bf16[1664,640]{1,0:T(8,128)(2,1)}, u32[]{:S(2)}, u32[]{:S(2)}) collective-permute-start(bf16[1664,640]{1,0:T(8,128)(2,1)S(1)} %multiply_convert_fusion.part), channel_id=1, source_target_pairs={{0,2},{1,3},{2,0},{3,1},{4,6},{5,7},{6,4},{7,5},{8,10},{9,11},{10,... | collective-permute-start | bytes 6389768 | tf_op jit(solution)/shard_map/ppermute | solution.py:56
  106.4 9.3 %collective-permute-start.30 = (bf16[40,3584]{1,0:T(8,128)(2,1)S(1)}, bf16[40,3584]{1,0:T(8,128)(2,1)S(1)}, u32[]{:S(2)}, u32[]{:S(2)}) collective-permute-start(bf16[40,3584]{1,0:T(8,128)(2,1)S(1)} %get-tuple-element.76), channel_id=1, source_target_pairs={{0,1},{1,0},{2,3},{3,2},{4,5},{5,4},{6,7},{7,6},{8,9},{9,8},{10,11... | collective-permute-start | bytes 860168 | tf_op jit(solution)/shard_map/ppermute | solution.py:56
  106.9 9.7 %collective-permute-start.31 = (bf16[40,3584]{1,0:T(8,128)(2,1)S(1)}, bf16[40,3584]{1,0:T(8,128)(2,1)S(1)}, u32[]{:S(2)}, u32[]{:S(2)}) collective-permute-start(bf16[40,3584]{1,0:T(8,128)(2,1)S(1)} %get-tuple-element.77), channel_id=1, source_target_pairs={{0,4},{1,5},{2,6},{3,7},{4,0},{5,1},{6,2},{7,3},{8,12},{9,13},{10,... | collective-permute-start | bytes 860168 | tf_op jit(solution)/shard_map/ppermute | solution.py:56
  107.7 15.2 %collective-permute-start.32 = (bf16[40,3584]{1,0:T(8,128)(2,1)S(1)}, bf16[40,3584]{1,0:T(8,128)(2,1)S(1)}, u32[]{:S(2)}, u32[]{:S(2)}) collective-permute-start(bf16[40,3584]{1,0:T(8,128)(2,1)S(1)} %get-tuple-element.78), channel_id=1, source_target_pairs={{0,5},{1,4},{2,7},{3,6},{4,1},{5,0},{6,3},{7,2},{8,13},{9,12},{10,... | collective-permute-start | bytes 860168 | tf_op jit(solution)/shard_map/ppermute | solution.py:56
  124.3 7.9 %collective-permute-start.34 = (bf16[40,896]{1,0:T(8,128)(2,1)S(1)}, bf16[40,896]{1,0:T(8,128)(2,1)S(1)}, u32[]{:S(2)}, u32[]{:S(2)}) collective-permute-start(bf16[40,896]{1,0:T(8,128)(2,1)S(1)} %get-tuple-element.81), channel_id=1, source_target_pairs={{0,16},{1,17},{2,18},{3,19},{4,20},{5,21},{6,22},{7,23},{8,24},{9,... | collective-permute-start | bytes 215048 | tf_op jit(solution)/shard_map/ppermute | solution.py:56
  127.7 6.1 %collective-permute-start.35 = (bf16[40,896]{1,0:T(8,128)(2,1)S(1)}, bf16[40,896]{1,0:T(8,128)(2,1)S(1)}, u32[]{:S(2)}, u32[]{:S(2)}) collective-permute-start(bf16[40,896]{1,0:T(8,128)(2,1)S(1)} %get-tuple-element.82), channel_id=1, source_target_pairs={{0,24},{1,25},{2,26},{3,27},{4,28},{5,29},{6,30},{7,31},{8,16},{9,... | collective-permute-start | bytes 215048 | tf_op jit(solution)/shard_map/ppermute | solution.py:56
  133.9 6.7 %collective-permute-start.37 = (bf16[40,896]{1,0:T(8,128)(2,1)S(1)}, bf16[40,896]{1,0:T(8,128)(2,1)S(1)}, u32[]{:S(2)}, u32[]{:S(2)}) collective-permute-start(bf16[40,896]{1,0:T(8,128)(2,1)S(1)} %multiply_convert_fusion.1), channel_id=1, source_target_pairs={{0,16},{1,17},{2,18},{3,19},{4,20},{5,21},{6,22},{7,23},{8,24},{9,... | collective-permute-start | bytes 215048 | tf_op jit(solution)/shard_map/ppermute | solution.py:56
  136.1 6.1 %collective-permute-start.38 = (bf16[40,896]{1,0:T(8,128)(2,1)S(1)}, bf16[40,896]{1,0:T(8,128)(2,1)S(1)}, u32[]{:S(2)}, u32[]{:S(2)}) collective-permute-start(bf16[40,896]{1,0:T(8,128)(2,1)S(1)} %multiply_convert_fusion.1), channel_id=1, source_target_pairs={{0,24},{1,25},{2,26},{3,27},{4,28},{5,29},{6,30},{7,31},{8,16},{9,... | collective-permute-start | bytes 215048 | tf_op jit(solution)/shard_map/ppermute | solution.py:56
  142.2 9.8 %collective-permute-start.39 = (bf16[40,3584]{1,0:T(8,128)(2,1)S(1)}, bf16[40,3584]{1,0:T(8,128)(2,1)S(1)}, u32[]{:S(2)}, u32[]{:S(2)}) collective-permute-start(bf16[40,3584]{1,0:T(8,128)(2,1)S(1)} %pad_maximum_fusion.refs_0_), channel_id=1, source_target_pairs={{0,1},{1,0},{2,3},{3,2},{4,5},{5,4},{6,7},{7,6},{8,9},{9,8},{10,11... | collective-permute-start | bytes 860168 | tf_op jit(solution)/shard_map/ppermute | solution.py:56
  142.8 9.2 %collective-permute-start.40 = (bf16[40,3584]{1,0:T(8,128)(2,1)S(1)}, bf16[40,3584]{1,0:T(8,128)(2,1)S(1)}, u32[]{:S(2)}, u32[]{:S(2)}) collective-permute-start(bf16[40,3584]{1,0:T(8,128)(2,1)S(1)} %pad_maximum_fusion.refs_0_), channel_id=1, source_target_pairs={{0,4},{1,5},{2,6},{3,7},{4,0},{5,1},{6,2},{7,3},{8,12},{9,13},{10,... | collective-permute-start | bytes 860168 | tf_op jit(solution)/shard_map/ppermute | solution.py:56
  143.6 11.9 %collective-permute-start.41 = (bf16[40,3584]{1,0:T(8,128)(2,1)S(1)}, bf16[40,3584]{1,0:T(8,128)(2,1)S(1)}, u32[]{:S(2)}, u32[]{:S(2)}) collective-permute-start(bf16[40,3584]{1,0:T(8,128)(2,1)S(1)} %pad_maximum_fusion.refs_0_), channel_id=1, source_target_pairs={{0,5},{1,4},{2,7},{3,6},{4,1},{5,0},{6,3},{7,2},{8,13},{9,12},{10,... | collective-permute-start | bytes 860168 | tf_op jit(solution)/shard_map/ppermute | solution.py:56
  145.8 17.6 %collective-permute-start.42 = (bf16[40,3584]{1,0:T(8,128)(2,1)S(1)}, bf16[40,3584]{1,0:T(8,128)(2,1)}, u32[]{:S(2)}, u32[]{:S(2)}) collective-permute-start(bf16[40,3584]{1,0:T(8,128)(2,1)S(1)} %pad_maximum_fusion.refs_0_), channel_id=1, source_target_pairs={{0,2},{1,3},{2,0},{3,1},{4,6},{5,7},{6,4},{7,5},{8,10},{9,11},{10,... | collective-permute-start | bytes 860168 | tf_op jit(solution)/shard_map/ppermute | solution.py:56
  152.0 11.4 %collective-permute-start.43 = (bf16[40,3584]{1,0:T(8,128)(2,1)S(1)}, bf16[40,3584]{1,0:T(8,128)(2,1)}, u32[]{:S(2)}, u32[]{:S(2)}) collective-permute-start(bf16[40,3584]{1,0:T(8,128)(2,1)S(1)} %collective-permute-done.39.refs_1_), channel_id=1, source_target_pairs={{0,2},{1,3},{2,0},{3,1},{4,6},{5,7},{6,4},{7,5},{8,10},{9,11},{10,... | collective-permute-start | bytes 860168 | tf_op jit(solution)/shard_map/ppermute | solution.py:56
  152.0 11.4 %collective-permute-start.44 = (bf16[40,3584]{1,0:T(8,128)(2,1)S(1)}, bf16[40,3584]{1,0:T(8,128)(2,1)}, u32[]{:S(2)}, u32[]{:S(2)}) collective-permute-start(bf16[40,3584]{1,0:T(8,128)(2,1)S(1)} %collective-permute-done.40.refs_2_), channel_id=1, source_target_pairs={{0,2},{1,3},{2,0},{3,1},{4,6},{5,7},{6,4},{7,5},{8,10},{9,11},{10,... | collective-permute-start | bytes 860168 | tf_op jit(solution)/shard_map/ppermute | solution.py:56
  155.5 7.9 %collective-permute-start.45 = (bf16[40,3584]{1,0:T(8,128)(2,1)S(1)}, bf16[40,3584]{1,0:T(8,128)(2,1)}, u32[]{:S(2)}, u32[]{:S(2)}) collective-permute-start(bf16[40,3584]{1,0:T(8,128)(2,1)S(1)} %collective-permute-done.41.refs_3_), channel_id=1, source_target_pairs={{0,2},{1,3},{2,0},{3,1},{4,6},{5,7},{6,4},{7,5},{8,10},{9,11},{10,... | collective-permute-start | bytes 860168 | tf_op jit(solution)/shard_map/ppermute | solution.py:56
  (24 other events, 223.2 us)

commit v2 on v1

--- a/solution.py
+++ b/solution.py
@@ -25,14 +25,17 @@
     return pltpu.with_memory_space_constraint(array, pltpu.VMEM)
 
 
-def call(kernel, outs, ins, scratch=(), flops=0, scalars=0, leave=()):
+def call(kernel, outs, ins, scratch=(), flops=0, scalars=0, leave=(), remote=0):
     outs = [jax.ShapeDtypeStruct(shape, kind) for shape, kind in outs]
     moved = sum(math.prod(x.shape) * x.dtype.itemsize for x in [*outs, *ins])
-    ins = [x if k < scalars else near_core(x) for k, x in enumerate(ins)]
+    near = len(ins) - scalars - remote
+    ins = [near_core(x) if scalars <= k < scalars + near else x for k, x in enumerate(ins)]
+    if remote:
+        ins[-1] = pltpu.with_memory_space_constraint(ins[-1], pltpu.HBM)
     return pl.pallas_call(
         kernel,
         out_shape=[x if k in leave else pltpu.VMEM(x.shape, x.dtype) for k, x in enumerate(outs)],
-        in_specs=[SMEM] * scalars + [VMEM] * (len(ins) - scalars),
+        in_specs=[SMEM] * scalars + [VMEM] * near + [pl.BlockSpec(memory_space=pl.ANY)] * remote,
         out_specs=[VMEM] * len(outs),
         scratch_shapes=list(scratch),
         cost_estimate=pl.CostEstimate(flops=flops, bytes_accessed=moved, transcendentals=0),
@@ -144,8 +147,11 @@
 
 
 def front_kernel(rows_total, noisy, *refs):
-    far = refs[:-8]
-    shift, in_weight, res_weight, query_weight, acts, hid, query, patches = refs[-8:]
+    far = refs[:-12]
+    shift, in_weight, query_weight, source, acts, hid, query = refs[-12:-5]
+    patches, res_weight, ends, tails, sem = refs[-5:]
+    load = pltpu.make_async_copy(source, res_weight, sem)
+    load.start()
     rows, cols = noisy.shape[1:]
     cells = rows * cols
     row = lax.axis_index("row")
@@ -185,9 +191,18 @@
         acts[0, :, spot] = jnp.where(lane == 0, 0.0, pltpu.roll(band, 1, 1)).astype(BF16)
         acts[2, :, spot] = jnp.where(lane == cols - 1, 0.0, pltpu.roll(band, cols - 1, 1)).astype(BF16)
     total = first[:, cols : cols + cells]
-    for a in range(3):
-        for b in range(3):
-            total = total + product(res_weight[3 * a + b], acts[b, :, a * cols : a * cols + cells], (1, 0))
+    load.wait()
+    channels = act.shape[0]
+    main = channels // 256 * 256
+    left = channels - main
+    for k in range(9):
+        a, b = k // 3, k % 3
+        total = total + product(
+            res_weight[k, :, :main], acts[b, :main, a * cols : a * cols + cells], (1, 0)
+        )
+        ends[:, k * left : (k + 1) * left] = res_weight[k, :, main:]
+        tails[k * left : (k + 1) * left, :] = acts[b, main:, a * cols : a * cols + cells]
+    total = total + product(ends[...], tails[...], (1, 0))
     low = total.astype(BF16)
     hid[...] = low
     query[...] = product(query_weight[...], low, (1, 0)).astype(BF16)
@@ -197,7 +212,9 @@
     bands = refs[:rows]
     block_out, kept, grad_hid, query_grad, out_grad = refs[rows : rows + 5]
     sent = refs[rows + 5 : 2 * rows + 4]
-    grad_att, attended, grad_query, held, pairs, grad_pairs = refs[2 * rows + 4 :]
+    grad_att, attended, grad_query, held, pairs, grad_pairs, lows, grads = refs[2 * rows + 4 :]
+    cells = hid.shape[1]
+    chunk = 256 if cells % 256 == 0 else cells
     channels = hid.shape[0]
     here = spots_of(rows)
     height = SLOTS // rows
@@ -211,19 +228,23 @@
         spot = slice(h * HEAD_DIM, (h + 1) * HEAD_DIM)
         keys = pairs[:, h * HEAD_DIM : (h + 1) * HEAD_DIM]
         vals = pairs[:, channels + h * HEAD_DIM : channels + (h + 1) * HEAD_DIM]
-        one = query[spot, :]
-        score = product(keys, one, (1, 0)) * scale
-        grown = jnp.exp(score - jnp.max(score, axis=0, keepdims=True))
-        probs = grown / jnp.sum(grown, axis=0, keepdims=True)
-        low = probs.astype(BF16)
-        attended[spot, :] = product(vals, low, (0, 0)).astype(BF16)
-        back = grad_att[spot, :]
-        grad_prob = product(vals, back, (1, 0))
-        inner = jnp.sum(probs * grad_prob, axis=0, keepdims=True)
-        grad_score = (scale * probs * (grad_prob - inner)).astype(BF16)
-        grad_query[spot, :] = product(keys, grad_score, (0, 0)).astype(BF16)
-        grad_pairs[:, h * HEAD_DIM : (h + 1) * HEAD_DIM] = product(grad_score, one, (1, 1))
-        grad_pairs[:, channels + h * HEAD_DIM : channels + (h + 1) * HEAD_DIM] = product(low, back, (1, 1))
+        for k in range(0, cells, chunk):
+            lanes = slice(k, k + chunk)
+            score = product(keys, query[spot, lanes], (1, 0)) * scale
+            grown = jnp.exp(score - jnp.max(score, axis=0, keepdims=True))
+            probs = grown / jnp.sum(grown, axis=0, keepdims=True)
+            low = probs.astype(BF16)
+            lows[:, lanes] = low
+            attended[spot, lanes] = product(vals, low, (0, 0)).astype(BF16)
+            grad_prob = product(vals, grad_att[spot, lanes], (1, 0))
+            inner = jnp.sum(probs * grad_prob, axis=0, keepdims=True)
+            grad_score = (scale * probs * (grad_prob - inner)).astype(BF16)
+            grads[:, lanes] = grad_score
+            grad_query[spot, lanes] = product(keys, grad_score, (0, 0)).astype(BF16)
+        grad_pairs[:, h * HEAD_DIM : (h + 1) * HEAD_DIM] = product(grads[...], query[spot, :], (1, 1))
+        grad_pairs[:, channels + h * HEAD_DIM : channels + (h + 1) * HEAD_DIM] = product(
+            lows[...], grad_att[spot, :], (1, 1)
+        )
     kept[...] = grad_pairs[pl.ds(pl.multiple_of(here["row"] * height, 8), height), :]
     for j in range(1, rows):
         spot = pl.ds(pl.multiple_of((here["row"] ^ j) * height, 8), height)
@@ -572,10 +593,17 @@
             *far,
             shift,
             in_flat,
+            query_weight,
             res_weight.reshape(9, channels, channels),
-            query_weight,
         ],
-        [pltpu.VMEM((9 * depth, cells + 2 * col_count), F32)],
+        [
+            pltpu.VMEM((9 * depth, cells + 2 * col_count), F32),
+            pltpu.VMEM((9, channels, channels), BF16),
+            pltpu.VMEM((channels, 9 * (channels % 256)), BF16),
+            pltpu.VMEM((9 * (channels % 256), cells), BF16),
+            pltpu.SemaphoreType.DMA,
+        ],
+        remote=1,
         flops=20 * channels * channels * cells,
     )
     block_out, kept, grad_hid, query_grad, out_grad, *sent = call(
@@ -594,6 +622,8 @@
             pltpu.VMEM((rows, height, pair_width), BF16),
             pltpu.VMEM((SLOTS, pair_width), BF16),
             pltpu.VMEM((SLOTS, pair_width), F32),
+            pltpu.VMEM((SLOTS, cells), BF16),
+            pltpu.VMEM((SLOTS, cells), BF16),
         ],
         flops=10 * channels * channels * cells + 12 * channels * SLOTS * cells,
     )

time: 171 us -> 169 us (0.988)
  transfers between devices with their start and end apart: 46 -> 46, of which waited for: 23 -> 23; matrix products, arithmetic and copies ran while one was open for 4% -> 3% of each run, Pallas kernels for 11% -> 11%
where the time goes in v2:
time: 169 us; the launch traced here: 168 us
  waiting for transfers between devices  80.9 us (48%)
  starting transfers between devices  47.2 us (28%)
  Pallas kernels  29.7 us (18%)
  local copies, waits for them, and re-layouts  3.79 us (2%)
  matrix products  3.06 us (2%)
  between operations  2.5 us (1%)
    ppermute x45, waiting for transfers between devices, swap(): return lax.ppermute(block, GRID, [(i, i ^ mask) for i in range(total)])  80.9 us
    ppermute x45, starting transfers between devices, swap(): return lax.ppermute(block, GRID, [(i, i ^ mask) for i in range(total)])  45.6 us
    pallas_call x9, Pallas kernels, call(): pl.pallas_call(kernel, out_shape=[x if k in leave else pltpu.VMEM(x.shape...  17 us
    pallas_call x2, Pallas kernels, join_step(): pl.pallas_call(functools.partial(join_kernel, flip), out_shape=jax.ShapeD...  4.32 us
    pallas_call x1, Pallas kernels, shards(): pl.pallas_call(functools.partial(condition_kernel, rows), out_shape=[jax....  4.06 us
    unnamed x25, local copies, waits for them, and re-layouts  3.44 us
  transfers between devices with their start and end apart: 46, of which 23 were waited for; matrix products, arithmetic and copies ran while one was open for 3% of the time, Pallas kernels for 11%

profile of v2, /device:TPU:0, one launch (start us, length us, event | category | flops | bytes accessed | tf_op | source)
XLA Modules:
  0.0 168.3 jit_solution(2904091878460800218)
XLA Ops:
  1.3 4.1 %condition.1 = (f32[32,640]{1,0:T(8,128)}, f32[32,640]{1,0:T(8,128)}, bf16[64,1664]{1,0:T(8,128)(2,1)}, bf16[64,1664]{1,0:T(8,128)(2,1)}) custom-call(s32[1]{0:T(128)S(6)} %copy.32.start, bf16[512,3328]{1,0:T(8,128)(2,1)} %hidden.1, bf16[3328,640]{1,0:T(8,128)(2,1)} %weight.3), custom_call_target="tpu_custom_call" | custom-call | flops 272629760 | bytes 5537792 | tf_op jit(solution)/shard_map/condition/pallas_call | solution.py:539
  5.4 3.1 %collective-permute-start.1 = (f32[32,640]{1,0:T(8,128)}, f32[32,640]{1,0:T(8,128)S(1)}, u32[]{:S(2)}, u32[]{:S(2)}) collective-permute-start(f32[32,640]{1,0:T(8,128)} %get-tuple-element.49), channel_id=1, source_target_pairs={{0,1},{1,0},{2,3},{3,2},{4,5},{5,4},{6,7},{7,6},{8,9},{9,8},{10,11... | collective-permute-start | bytes 245768 | tf_op jit(solution)/shard_map/ppermute | solution.py:59
  9.2 1.9 %collective-permute-done.1 = f32[32,640]{1,0:T(8,128)S(1)} collective-permute-done((f32[32,640]{1,0:T(8,128)}, f32[32,640]{1,0:T(8,128)S(1)}, u32[]{:S(2)}, u32[]{:S(2)}) %collective-permute-start.1) | collective-permute-done | bytes 81952 | tf_op jit(solution)/shard_map/ppermute | solution.py:59
  12.0 2.1 %collective-permute-start.2 = (bf16[32,640]{1,0:T(8,128)(2,1)S(1)}, bf16[32,640]{1,0:T(8,128)(2,1)S(1)}, u32[]{:S(2)}, u32[]{:S(2)}) collective-permute-start(bf16[32,640]{1,0:T(8,128)(2,1)S(1)} %add_convert_fusion.2.refs_0_), channel_id=1, source_target_pairs={{0,8},{1,9},{2,10},{3,11},{4,12},{5,13},{6,14},{7,15},{8,0},{9,1},... | collective-permute-start | bytes 122888 | tf_op jit(solution)/shard_map/ppermute | solution.py:59
  14.1 2.6 %collective-permute-start.3 = (bf16[32,640]{1,0:T(8,128)(2,1)S(1)}, bf16[32,640]{1,0:T(8,128)(2,1)S(1)}, u32[]{:S(2)}, u32[]{:S(2)}) collective-permute-start(bf16[32,640]{1,0:T(8,128)(2,1)S(1)} %add_convert_fusion.2.refs_0_), channel_id=1, source_target_pairs={{0,16},{1,17},{2,18},{3,19},{4,20},{5,21},{6,22},{7,23},{8,24},{9,... | collective-permute-start | bytes 122888 | tf_op jit(solution)/shard_map/ppermute | solution.py:59
  17.0 2.9 %collective-permute-done.3.refs_2_ = bf16[32,640]{1,0:T(8,128)(2,1)S(1)} collective-permute-done((bf16[32,640]{1,0:T(8,128)(2,1)S(1)}, bf16[32,640]{1,0:T(8,128)(2,1)S(1)}, u32[]{:S(2)}, u32[]{:S(2)}) %collective-permute-start.3) | collective-permute-done | bytes 40992 | tf_op jit(solution)/shard_map/ppermute | solution.py:59
  19.9 2.6 %collective-permute-done.4.refs_3_ = bf16[32,640]{1,0:T(8,128)(2,1)S(1)} collective-permute-done((bf16[32,640]{1,0:T(8,128)(2,1)S(1)}, bf16[32,640]{1,0:T(8,128)(2,1)S(1)}, u32[]{:S(2)}, u32[]{:S(2)}) %collective-permute-start.4) | collective-permute-done | bytes 40992 | tf_op jit(solution)/shard_map/ppermute | solution.py:59
  30.0 4.2 %shard_map.164 = (bf16[3,320,1280]{2,1,0:T(8,128)(2,1)S(1)}, bf16[320,1024]{1,0:T(8,128)(2,1)S(1)}, bf16[320,1024]{1,0:T(8,128)(2,1)S(1)}) custom-call(f32[4,8,128]{2,1,0:T(8,128)S(1)} %get-tuple-element.46.noisy, bf16[4,2,128]{2,1,0:T(2,128)(2,1)S(1)} %collective-permute-done.refs_0_, f32[320,1]{1,0:T(8,128)S(1)} %copy.20.refs_1_, ...), custom_call_target="tpu_custom_call" | custom-call | flops 2097152000 | bytes 5859072 | tf_op jit(solution)/shard_map/pallas_call | solution.py:35
  34.3 3.8 %shard_map.166 = (bf16[320,1024]{1,0:T(8,128)(2,1)S(1)}, f32[32,640]{1,0:T(8,128)S(1)}, bf16[320,1024]{1,0:T(8,128)(2,1)S(1)}, f32[320,320]{1,0:T(8,128)S(1)}, f...) custom-call(bf16[320,1024]{1,0:T(8,128)(2,1)S(1)} %get-tuple-element.52.query, ...), custom_call_target="tpu_custom_call" | custom-call | flops 1300234240 | bytes 4710400 | tf_op jit(solution)/shard_map/pallas_call | solution.py:35
  38.7 3.5 %collective-permute-done.10 = bf16[32,640]{1,0:T(8,128)(2,1)S(1)} collective-permute-done((bf16[32,640]{1,0:T(8,128)(2,1)S(1)}, bf16[32,640]{1,0:T(8,128)(2,1)S(1)}, u32[]{:S(2)}, u32[]{:S(2)}) %collective-permute-start.10) | collective-permute-done | bytes 40992 | tf_op jit(solution)/shard_map/ppermute | solution.py:59
  43.2 3.4 %collective-permute-start.13 = (bf16[32,640]{1,0:T(8,128)(2,1)S(1)}, bf16[32,640]{1,0:T(8,128)(2,1)S(1)}, u32[]{:S(2)}, u32[]{:S(2)}) collective-permute-start(bf16[32,640]{1,0:T(8,128)(2,1)S(1)} %add_convert_fusion), channel_id=1, source_target_pairs={{0,24},{1,25},{2,26},{3,27},{4,28},{5,29},{6,30},{7,31},{8,16},{9,... | collective-permute-start | bytes 122888 | tf_op jit(solution)/shard_map/ppermute | solution.py:59
  52.9 2.7 %collective-permute-done.14.refs_1_ = bf16[4,32,640]{2,1,0:T(8,128)(2,1)S(1)} collective-permute-done((bf16[4,32,640]{2,1,0:T(8,128)(2,1)S(1)}, bf16[4,32,640]{2,1,0:T(8,128)(2,1)S(1)}, u32[]{:S(2)}, u32[]{:S(2)}) %collective-permute-start.14) | collective-permute-done | bytes 163872 | tf_op jit(solution)/shard_map/ppermute | solution.py:59
  58.2 3.2 %shard_map.167 = (f32[4,40,3584]{2,1,0:T(8,128)S(1)}, bf16[4,40,3584]{2,1,0:T(8,128)(2,1)S(1)}) custom-call(bf16[320,1024]{1,0:T(8,128)(2,1)S(1)} %get-tuple-element.60.grad_hid, bf16[3,320,1280]{2,1,0:T(8,128)(2,1)S(1)} %get-tuple-element.61.acts, f32[320,320]{1,0:T(8,128)S(1)} %get-tuple-element.62.query_grad, f32[320,320]{1,0:T(8,128)S(1)} %get-tuple-element.63.out_grad), custom_call_target="tpu_custom_call" | custom-call | flops 1887436800 | bytes 7372800 | tf_op jit(solution)/shard_map/pallas_call | solution.py:35
  61.5 3.4 %collective-permute-start.24 = (bf16[128,1664]{1,0:T(8,128)(2,1)S(1)}, bf16[128,1664]{1,0:T(8,128)(2,1)S(1)}, u32[]{:S(2)}, u32[]{:S(2)}) collective-permute-start(bf16[128,1664]{1,0:T(8,128)(2,1)S(1)} %get-tuple-element.88), channel_id=1, source_target_pairs={{0,24},{1,25},{2,26},{3,27},{4,28},{5,29},{6,30},{7,31},{8,16},{9,... | collective-permute-start | bytes 1277960 | tf_op jit(solution)/shard_map/ppermute | solution.py:59
  66.9 19.5 %collective-permute-done.23 = bf16[128,1664]{1,0:T(8,128)(2,1)S(1)} collective-permute-done((bf16[128,1664]{1,0:T(8,128)(2,1)S(1)}, bf16[128,1664]{1,0:T(8,128)(2,1)S(1)}, u32[]{:S(2)}, u32[]{:S(2)}) %collective-permute-start.23) | collective-permute-done | bytes 426016 | tf_op jit(solution)/shard_map/ppermute | solution.py:59
  88.6 6.0 %collective-permute-done.27 = bf16[128,1664]{1,0:T(8,128)(2,1)S(1)} collective-permute-done((bf16[128,1664]{1,0:T(8,128)(2,1)S(1)}, bf16[128,1664]{1,0:T(8,128)(2,1)S(1)}, u32[]{:S(2)}, u32[]{:S(2)}) %collective-permute-start.27) | collective-permute-done | bytes 426016 | tf_op jit(solution)/shard_map/ppermute | solution.py:59
  97.2 2.0 %collective-permute-done.26 = bf16[128,1664]{1,0:T(8,128)(2,1)S(1)} collective-permute-done((bf16[128,1664]{1,0:T(8,128)(2,1)S(1)}, bf16[128,1664]{1,0:T(8,128)(2,1)S(1)}, u32[]{:S(2)}, u32[]{:S(2)}) %collective-permute-start.26) | collective-permute-done | bytes 426016 | tf_op jit(solution)/shard_map/ppermute | solution.py:59
  99.2 3.6 %collective-permute-done.28 = bf16[128,1664]{1,0:T(8,128)(2,1)S(1)} collective-permute-done((bf16[128,1664]{1,0:T(8,128)(2,1)S(1)}, bf16[128,1664]{1,0:T(8,128)(2,1)S(1)}, u32[]{:S(2)}, u32[]{:S(2)}) %collective-permute-start.28) | collective-permute-done | bytes 426016 | tf_op jit(solution)/shard_map/ppermute | solution.py:59
  109.1 4.8 %collective-permute-done.30.refs_1_ = bf16[40,3584]{1,0:T(8,128)(2,1)S(1)} collective-permute-done((bf16[40,3584]{1,0:T(8,128)(2,1)S(1)}, bf16[40,3584]{1,0:T(8,128)(2,1)S(1)}, u32[]{:S(2)}, u32[]{:S(2)}) %collective-permute-start.30) | collective-permute-done | bytes 286752 | tf_op jit(solution)/shard_map/ppermute | solution.py:59
  114.9 6.3 %collective-permute-done.32.refs_3_ = bf16[40,3584]{1,0:T(8,128)(2,1)S(1)} collective-permute-done((bf16[40,3584]{1,0:T(8,128)(2,1)S(1)}, bf16[40,3584]{1,0:T(8,128)(2,1)S(1)}, u32[]{:S(2)}, u32[]{:S(2)}) %collective-permute-start.32) | collective-permute-done | bytes 286752 | tf_op jit(solution)/shard_map/ppermute | solution.py:59
  122.5 3.4 %collective-permute-start.34 = (bf16[40,896]{1,0:T(8,128)(2,1)S(1)}, bf16[40,896]{1,0:T(8,128)(2,1)S(1)}, u32[]{:S(2)}, u32[]{:S(2)}) collective-permute-start(bf16[40,896]{1,0:T(8,128)(2,1)S(1)} %get-tuple-element.81), channel_id=1, source_target_pairs={{0,16},{1,17},{2,18},{3,19},{4,20},{5,21},{6,22},{7,23},{8,24},{9,... | collective-permute-start | bytes 215048 | tf_op jit(solution)/shard_map/ppermute | solution.py:59
  125.9 4.4 %collective-permute-done.34 = bf16[40,896]{1,0:T(8,128)(2,1)S(1)} collective-permute-done((bf16[40,896]{1,0:T(8,128)(2,1)S(1)}, bf16[40,896]{1,0:T(8,128)(2,1)S(1)}, u32[]{:S(2)}, u32[]{:S(2)}) %collective-permute-start.34) | collective-permute-done | bytes 71712 | tf_op jit(solution)/shard_map/ppermute | solution.py:59
  132.1 2.1 %collective-permute-start.37 = (bf16[40,896]{1,0:T(8,128)(2,1)S(1)}, bf16[40,896]{1,0:T(8,128)(2,1)S(1)}, u32[]{:S(2)}, u32[]{:S(2)}) collective-permute-start(bf16[40,896]{1,0:T(8,128)(2,1)S(1)} %multiply_convert_fusion.1), channel_id=1, source_target_pairs={{0,16},{1,17},{2,18},{3,19},{4,20},{5,21},{6,22},{7,23},{8,24},{9,... | collective-permute-start | bytes 215048 | tf_op jit(solution)/shard_map/ppermute | solution.py:59
  134.2 2.2 %collective-permute-start.38 = (bf16[40,896]{1,0:T(8,128)(2,1)S(1)}, bf16[40,896]{1,0:T(8,128)(2,1)S(1)}, u32[]{:S(2)}, u32[]{:S(2)}) collective-permute-start(bf16[40,896]{1,0:T(8,128)(2,1)S(1)} %multiply_convert_fusion.1), channel_id=1, source_target_pairs={{0,24},{1,25},{2,26},{3,27},{4,28},{5,29},{6,30},{7,31},{8,16},{9,... | collective-permute-start | bytes 215048 | tf_op jit(solution)/shard_map/ppermute | solution.py:59
  136.5 2.3 %collective-permute-done.37 = bf16[40,896]{1,0:T(8,128)(2,1)S(1)} collective-permute-done((bf16[40,896]{1,0:T(8,128)(2,1)S(1)}, bf16[40,896]{1,0:T(8,128)(2,1)S(1)}, u32[]{:S(2)}, u32[]{:S(2)}) %collective-permute-start.37) | collective-permute-done | bytes 71712 | tf_op jit(solution)/shard_map/ppermute | solution.py:59
  144.0 6.2 %collective-permute-done.39.refs_1_ = bf16[40,3584]{1,0:T(8,128)(2,1)S(1)} collective-permute-done((bf16[40,3584]{1,0:T(8,128)(2,1)S(1)}, bf16[40,3584]{1,0:T(8,128)(2,1)S(1)}, u32[]{:S(2)}, u32[]{:S(2)}) %collective-permute-start.39) | collective-permute-done | bytes 286752 | tf_op jit(solution)/shard_map/ppermute | solution.py:59
  150.7 3.0 %collective-permute-done.41.refs_3_ = bf16[40,3584]{1,0:T(8,128)(2,1)S(1)} collective-permute-done((bf16[40,3584]{1,0:T(8,128)(2,1)S(1)}, bf16[40,3584]{1,0:T(8,128)(2,1)S(1)}, u32[]{:S(2)}, u32[]{:S(2)}) %collective-permute-start.41) | collective-permute-done | bytes 286752 | tf_op jit(solution)/shard_map/ppermute | solution.py:59
  153.7 1.8 %blank.1 = bf16[512,3328]{1,0:T(8,128)(2,1)} custom-call(), custom_call_target="tpu_custom_call" | custom-call | tf_op jit(solution)/shard_map/blank/pallas_call | solution.py:636
  155.6 2.2 %copy-done = bf16[3328,640]{1,0:T(8,128)(2,1)S(1)} copy-done((bf16[3328,640]{1,0:T(8,128)(2,1)S(1)}, bf16[3328,640]{1,0:T(8,128)(2,1)}, u32[]{:S(2)}) %copy-start) | copy-done | bytes 4259864
  157.8 2.4 %place.1 = bf16[512,3328]{1,0:T(8,128)(2,1)} custom-call(s32[1]{0:T(128)S(6)} %copy.32.start, bf16[64,640]{1,0:T(8,128)(2,1)S(1)} %bitcast.24, bf16[3328,640]{1,0:T(8,128)(2,1)S(1)} %copy-done, bf16[512,3328]{1,0:T(8,128)(2,1)} %blank.1), custom_call_target="tpu_custom_call", output_to_operand_aliasing={{}: (3, {})} | custom-call | tf_op jit(solution)/shard_map/place/pallas_call | solution.py:669
  161.6 3.5 %shard_map.173 = (bf16[9,320,320]{2,1,0:T(8,128)(2,1)}, bf16[320,320]{1,0:T(8,128)(2,1)}, bf16[320,320]{1,0:T(8,128)(2,1)}) custom-call(bf16[40,3584]{1,0:T(8,128)(2,1)S(1)} %pad_maximum_fusion.refs_0_, bf16[40,3584]{1,0:T(8,128)(2,1)S(1)} %collective-permute-done.39.refs_1_, bf16[40,3584]{1,0:T(8,128)(2,1)S(1)} %collective-permute-done.40.refs_2_, ...), custom_call_target="tpu_custom_call" | custom-call | bytes 4546560 | tf_op jit(solution)/shard_map/pallas_call | solution.py:35
  165.2 3.0 %shard_map.171 = bf16[3328,640]{1,0:T(8,128)(2,1)} custom-call(bf16[1664,640]{1,0:T(8,128)(2,1)} %collective-permute-done.29.part, bf16[3328,640]{1,0:T(8,128)(2,1)} %shard_map.170.refs_0_), custom_call_target="tpu_custom_call", output_to_operand_aliasing={{}: (1, {})} | custom-call | tf_op jit(solution)/shard_map/pallas_call | solution.py:473
  (115 shorter events, 43.3 us)
Async XLA Ops:
  14.1 5.8 %collective-permute-start.3 = (bf16[32,640]{1,0:T(8,128)(2,1)S(1)}, bf16[32,640]{1,0:T(8,128)(2,1)S(1)}, u32[]{:S(2)}, u32[]{:S(2)}) collective-permute-start(bf16[32,640]{1,0:T(8,128)(2,1)S(1)} %add_convert_fusion.2.refs_0_), channel_id=1, source_target_pairs={{0,16},{1,17},{2,18},{3,19},{4,20},{5,21},{6,22},{7,23},{8,24},{9,... | collective-permute-start | bytes 122888 | tf_op jit(solution)/shard_map/ppermute | solution.py:59
  16.7 5.8 %collective-permute-start.4 = (bf16[32,640]{1,0:T(8,128)(2,1)S(1)}, bf16[32,640]{1,0:T(8,128)(2,1)S(1)}, u32[]{:S(2)}, u32[]{:S(2)}) collective-permute-start(bf16[32,640]{1,0:T(8,128)(2,1)S(1)} %add_convert_fusion.2.refs_0_), channel_id=1, source_target_pairs={{0,24},{1,25},{2,26},{3,27},{4,28},{5,29},{6,30},{7,31},{8,16},{9,... | collective-permute-start | bytes 122888 | tf_op jit(solution)/shard_map/ppermute | solution.py:59
  28.4 5.8 %collective-permute-start.8 = (bf16[32,640]{1,0:T(8,128)(2,1)S(1)}, bf16[32,640]{1,0:T(8,128)(2,1)S(1)}, u32[]{:S(2)}, u32[]{:S(2)}) collective-permute-start(bf16[32,640]{1,0:T(8,128)(2,1)S(1)} %add_convert_fusion.1.refs_0_), channel_id=1, source_target_pairs={{0,1},{1,0},{2,3},{3,2},{4,5},{5,4},{6,7},{7,6},{8,9},{9,8},{10,11... | collective-permute-start | bytes 122888 | tf_op jit(solution)/shard_map/ppermute | solution.py:59
  38.7 14.0 %collective-permute-start.21 = (bf16[64,1664]{1,0:T(8,128)(2,1)S(1)}, bf16[64,1664]{1,0:T(8,128)(2,1)S(1)}, u32[]{:S(2)}, u32[]{:S(2)}) collective-permute-start(bf16[64,1664]{1,0:T(8,128)(2,1)S(1)} %copy-done.9), channel_id=1, source_target_pairs={{0,2},{1,3},{2,0},{3,1},{4,6},{5,7},{6,4},{7,5},{8,10},{9,11},{10,... | collective-permute-start | bytes 638984 | tf_op jit(solution)/shard_map/ppermute | solution.py:59
  43.2 5.8 %collective-permute-start.13 = (bf16[32,640]{1,0:T(8,128)(2,1)S(1)}, bf16[32,640]{1,0:T(8,128)(2,1)S(1)}, u32[]{:S(2)}, u32[]{:S(2)}) collective-permute-start(bf16[32,640]{1,0:T(8,128)(2,1)S(1)} %add_convert_fusion), channel_id=1, source_target_pairs={{0,24},{1,25},{2,26},{3,27},{4,28},{5,29},{6,30},{7,31},{8,16},{9,... | collective-permute-start | bytes 122888 | tf_op jit(solution)/shard_map/ppermute | solution.py:59
  49.1 6.5 %collective-permute-start.14 = (bf16[4,32,640]{2,1,0:T(8,128)(2,1)S(1)}, bf16[4,32,640]{2,1,0:T(8,128)(2,1)S(1)}, u32[]{:S(2)}, u32[]{:S(2)}) collective-permute-start(bf16[4,32,640]{2,1,0:T(8,128)(2,1)S(1)} %pad_maximum_fusion.1.refs_0_), channel_id=1, source_target_pairs={{0,1},{1,0},{2,3},{3,2},{4,5},{5,4},{6,7},{7,6},{8,9},{9,8},{10,11... | collective-permute-start | bytes 491528 | tf_op jit(solution)/shard_map/ppermute | solution.py:59
  49.7 7.0 %collective-permute-start.15 = (bf16[4,32,640]{2,1,0:T(8,128)(2,1)S(1)}, bf16[4,32,640]{2,1,0:T(8,128)(2,1)S(1)}, u32[]{:S(2)}, u32[]{:S(2)}) collective-permute-start(bf16[4,32,640]{2,1,0:T(8,128)(2,1)S(1)} %pad_maximum_fusion.1.refs_0_), channel_id=1, source_target_pairs={{0,4},{1,5},{2,6},{3,7},{4,0},{5,1},{6,2},{7,3},{8,12},{9,13},{10,... | collective-permute-start | bytes 491528 | tf_op jit(solution)/shard_map/ppermute | solution.py:59
  51.1 6.6 %collective-permute-start.16 = (bf16[4,32,640]{2,1,0:T(8,128)(2,1)S(1)}, bf16[4,32,640]{2,1,0:T(8,128)(2,1)S(1)}, u32[]{:S(2)}, u32[]{:S(2)}) collective-permute-start(bf16[4,32,640]{2,1,0:T(8,128)(2,1)S(1)} %pad_maximum_fusion.1.refs_0_), channel_id=1, source_target_pairs={{0,5},{1,4},{2,7},{3,6},{4,1},{5,0},{6,3},{7,2},{8,13},{9,12},{10,... | collective-permute-start | bytes 491528 | tf_op jit(solution)/shard_map/ppermute | solution.py:59
  52.7 34.6 %collective-permute-start.22 = (bf16[128,1664]{1,0:T(8,128)(2,1)S(1)}, bf16[128,1664]{1,0:T(8,128)(2,1)S(1)}, u32[]{:S(2)}, u32[]{:S(2)}) collective-permute-start(bf16[128,1664]{1,0:T(8,128)(2,1)S(1)} %get-tuple-element.88), channel_id=1, source_target_pairs={{0,8},{1,9},{2,10},{3,11},{4,12},{5,13},{6,14},{7,15},{8,0},{9,1},... | collective-permute-start | bytes 1277960 | tf_op jit(solution)/shard_map/ppermute | solution.py:59
  55.6 30.9 %collective-permute-start.23 = (bf16[128,1664]{1,0:T(8,128)(2,1)S(1)}, bf16[128,1664]{1,0:T(8,128)(2,1)S(1)}, u32[]{:S(2)}, u32[]{:S(2)}) collective-permute-start(bf16[128,1664]{1,0:T(8,128)(2,1)S(1)} %get-tuple-element.88), channel_id=1, source_target_pairs={{0,16},{1,17},{2,18},{3,19},{4,20},{5,21},{6,22},{7,23},{8,24},{9,... | collective-permute-start | bytes 1277960 | tf_op jit(solution)/shard_map/ppermute | solution.py:59
  57.7 7.3 %collective-permute-start.20 = (bf16[4,32,640]{2,1,0:T(8,128)(2,1)S(1)}, bf16[4,32,640]{2,1,0:T(8,128)(2,1)S(1)}, u32[]{:S(2)}, u32[]{:S(2)}) collective-permute-start(bf16[4,32,640]{2,1,0:T(8,128)(2,1)S(1)} %collective-permute-done.16.refs_3_), channel_id=1, source_target_pairs={{0,2},{1,3},{2,0},{3,1},{4,6},{5,7},{6,4},{7,5},{8,10},{9,11},{10,... | collective-permute-start | bytes 491528 | tf_op jit(solution)/shard_map/ppermute | solution.py:59
  61.4 42.9 %collective-permute-start.9 = (bf16[4,40,3584]{2,1,0:T(8,128)(2,1)S(1)}, bf16[4,40,3584]{2,1,0:T(8,128)(2,1)S(1)}, u32[]{:S(2)}, u32[]{:S(2)}) collective-permute-start(bf16[4,40,3584]{2,1,0:T(8,128)(2,1)S(1)} %get-tuple-element.65), channel_id=1, source_target_pairs={{0,2},{1,3},{2,0},{3,1},{4,6},{5,7},{6,4},{7,5},{8,10},{9,11},{10,... | collective-permute-start | bytes 3440648 | tf_op jit(solution)/shard_map/ppermute | solution.py:59
  61.5 34.0 %collective-permute-start.24 = (bf16[128,1664]{1,0:T(8,128)(2,1)S(1)}, bf16[128,1664]{1,0:T(8,128)(2,1)S(1)}, u32[]{:S(2)}, u32[]{:S(2)}) collective-permute-start(bf16[128,1664]{1,0:T(8,128)(2,1)S(1)} %get-tuple-element.88), channel_id=1, source_target_pairs={{0,24},{1,25},{2,26},{3,27},{4,28},{5,29},{6,30},{7,31},{8,16},{9,... | collective-permute-start | bytes 1277960 | tf_op jit(solution)/shard_map/ppermute | solution.py:59
  65.0 32.2 %collective-permute-start.25 = (bf16[128,1664]{1,0:T(8,128)(2,1)S(1)}, bf16[128,1664]{1,0:T(8,128)(2,1)S(1)}, u32[]{:S(2)}, u32[]{:S(2)}) collective-permute-start(bf16[128,1664]{1,0:T(8,128)(2,1)S(1)} %get-tuple-element.88), channel_id=1, source_target_pairs={{0,4},{1,5},{2,6},{3,7},{4,0},{5,1},{6,2},{7,3},{8,12},{9,13},{10,... | collective-permute-start | bytes 1277960 | tf_op jit(solution)/shard_map/ppermute | solution.py:59
  86.5 8.1 %collective-permute-start.27 = (bf16[128,1664]{1,0:T(8,128)(2,1)S(1)}, bf16[128,1664]{1,0:T(8,128)(2,1)S(1)}, u32[]{:S(2)}, u32[]{:S(2)}) collective-permute-start(bf16[128,1664]{1,0:T(8,128)(2,1)S(1)} %collective-permute-done.23), channel_id=1, source_target_pairs={{0,4},{1,5},{2,6},{3,7},{4,0},{5,1},{6,2},{7,3},{8,12},{9,13},{10,... | collective-permute-start | bytes 1277960 | tf_op jit(solution)/shard_map/ppermute | solution.py:59
  87.3 11.9 %collective-permute-start.26 = (bf16[128,1664]{1,0:T(8,128)(2,1)S(1)}, bf16[128,1664]{1,0:T(8,128)(2,1)S(1)}, u32[]{:S(2)}, u32[]{:S(2)}) collective-permute-start(bf16[128,1664]{1,0:T(8,128)(2,1)S(1)} %collective-permute-done.22), channel_id=1, source_target_pairs={{0,4},{1,5},{2,6},{3,7},{4,0},{5,1},{6,2},{7,3},{8,12},{9,13},{10,... | collective-permute-start | bytes 1277960 | tf_op jit(solution)/shard_map/ppermute | solution.py:59
  94.6 8.1 %collective-permute-start.28 = (bf16[128,1664]{1,0:T(8,128)(2,1)S(1)}, bf16[128,1664]{1,0:T(8,128)(2,1)S(1)}, u32[]{:S(2)}, u32[]{:S(2)}) collective-permute-start(bf16[128,1664]{1,0:T(8,128)(2,1)S(1)} %collective-permute-done.27), channel_id=1, source_target_pairs={{0,8},{1,9},{2,10},{3,11},{4,12},{5,13},{6,14},{7,15},{8,0},{9,1},... | collective-permute-start | bytes 1277960 | tf_op jit(solution)/shard_map/ppermute | solution.py:59
  104.3 60.9 %collective-permute-start.29 = (bf16[1664,640]{1,0:T(8,128)(2,1)S(1)}, bf16[1664,640]{1,0:T(8,128)(2,1)}, u32[]{:S(2)}, u32[]{:S(2)}) collective-permute-start(bf16[1664,640]{1,0:T(8,128)(2,1)S(1)} %multiply_convert_fusion.part), channel_id=1, source_target_pairs={{0,2},{1,3},{2,0},{3,1},{4,6},{5,7},{6,4},{7,5},{8,10},{9,11},{10,... | collective-permute-start | bytes 6389768 | tf_op jit(solution)/shard_map/ppermute | solution.py:59
  104.6 9.3 %collective-permute-start.30 = (bf16[40,3584]{1,0:T(8,128)(2,1)S(1)}, bf16[40,3584]{1,0:T(8,128)(2,1)S(1)}, u32[]{:S(2)}, u32[]{:S(2)}) collective-permute-start(bf16[40,3584]{1,0:T(8,128)(2,1)S(1)} %get-tuple-element.76), channel_id=1, source_target_pairs={{0,1},{1,0},{2,3},{3,2},{4,5},{5,4},{6,7},{7,6},{8,9},{9,8},{10,11... | collective-permute-start | bytes 860168 | tf_op jit(solution)/shard_map/ppermute | solution.py:59
  105.2 9.7 %collective-permute-start.31 = (bf16[40,3584]{1,0:T(8,128)(2,1)S(1)}, bf16[40,3584]{1,0:T(8,128)(2,1)S(1)}, u32[]{:S(2)}, u32[]{:S(2)}) collective-permute-start(bf16[40,3584]{1,0:T(8,128)(2,1)S(1)} %get-tuple-element.77), channel_id=1, source_target_pairs={{0,4},{1,5},{2,6},{3,7},{4,0},{5,1},{6,2},{7,3},{8,12},{9,13},{10,... | collective-permute-start | bytes 860168 | tf_op jit(solution)/shard_map/ppermute | solution.py:59
  106.8 14.4 %collective-permute-start.32 = (bf16[40,3584]{1,0:T(8,128)(2,1)S(1)}, bf16[40,3584]{1,0:T(8,128)(2,1)S(1)}, u32[]{:S(2)}, u32[]{:S(2)}) collective-permute-start(bf16[40,3584]{1,0:T(8,128)(2,1)S(1)} %get-tuple-element.78), channel_id=1, source_target_pairs={{0,5},{1,4},{2,7},{3,6},{4,1},{5,0},{6,3},{7,2},{8,13},{9,12},{10,... | collective-permute-start | bytes 860168 | tf_op jit(solution)/shard_map/ppermute | solution.py:59
  122.5 7.9 %collective-permute-start.34 = (bf16[40,896]{1,0:T(8,128)(2,1)S(1)}, bf16[40,896]{1,0:T(8,128)(2,1)S(1)}, u32[]{:S(2)}, u32[]{:S(2)}) collective-permute-start(bf16[40,896]{1,0:T(8,128)(2,1)S(1)} %get-tuple-element.81), channel_id=1, source_target_pairs={{0,16},{1,17},{2,18},{3,19},{4,20},{5,21},{6,22},{7,23},{8,24},{9,... | collective-permute-start | bytes 215048 | tf_op jit(solution)/shard_map/ppermute | solution.py:59
  125.8 6.1 %collective-permute-start.35 = (bf16[40,896]{1,0:T(8,128)(2,1)S(1)}, bf16[40,896]{1,0:T(8,128)(2,1)S(1)}, u32[]{:S(2)}, u32[]{:S(2)}) collective-permute-start(bf16[40,896]{1,0:T(8,128)(2,1)S(1)} %get-tuple-element.82), channel_id=1, source_target_pairs={{0,24},{1,25},{2,26},{3,27},{4,28},{5,29},{6,30},{7,31},{8,16},{9,... | collective-permute-start | bytes 215048 | tf_op jit(solution)/shard_map/ppermute | solution.py:59
  132.1 6.7 %collective-permute-start.37 = (bf16[40,896]{1,0:T(8,128)(2,1)S(1)}, bf16[40,896]{1,0:T(8,128)(2,1)S(1)}, u32[]{:S(2)}, u32[]{:S(2)}) collective-permute-start(bf16[40,896]{1,0:T(8,128)(2,1)S(1)} %multiply_convert_fusion.1), channel_id=1, source_target_pairs={{0,16},{1,17},{2,18},{3,19},{4,20},{5,21},{6,22},{7,23},{8,24},{9,... | collective-permute-start | bytes 215048 | tf_op jit(solution)/shard_map/ppermute | solution.py:59
  134.2 6.1 %collective-permute-start.38 = (bf16[40,896]{1,0:T(8,128)(2,1)S(1)}, bf16[40,896]{1,0:T(8,128)(2,1)S(1)}, u32[]{:S(2)}, u32[]{:S(2)}) collective-permute-start(bf16[40,896]{1,0:T(8,128)(2,1)S(1)} %multiply_convert_fusion.1), channel_id=1, source_target_pairs={{0,24},{1,25},{2,26},{3,27},{4,28},{5,29},{6,30},{7,31},{8,16},{9,... | collective-permute-start | bytes 215048 | tf_op jit(solution)/shard_map/ppermute | solution.py:59
  140.4 9.8 %collective-permute-start.39 = (bf16[40,3584]{1,0:T(8,128)(2,1)S(1)}, bf16[40,3584]{1,0:T(8,128)(2,1)S(1)}, u32[]{:S(2)}, u32[]{:S(2)}) collective-permute-start(bf16[40,3584]{1,0:T(8,128)(2,1)S(1)} %pad_maximum_fusion.refs_0_), channel_id=1, source_target_pairs={{0,1},{1,0},{2,3},{3,2},{4,5},{5,4},{6,7},{7,6},{8,9},{9,8},{10,11... | collective-permute-start | bytes 860168 | tf_op jit(solution)/shard_map/ppermute | solution.py:59
  141.0 9.2 %collective-permute-start.40 = (bf16[40,3584]{1,0:T(8,128)(2,1)S(1)}, bf16[40,3584]{1,0:T(8,128)(2,1)S(1)}, u32[]{:S(2)}, u32[]{:S(2)}) collective-permute-start(bf16[40,3584]{1,0:T(8,128)(2,1)S(1)} %pad_maximum_fusion.refs_0_), channel_id=1, source_target_pairs={{0,4},{1,5},{2,6},{3,7},{4,0},{5,1},{6,2},{7,3},{8,12},{9,13},{10,... | collective-permute-start | bytes 860168 | tf_op jit(solution)/shard_map/ppermute | solution.py:59
  142.5 11.2 %collective-permute-start.41 = (bf16[40,3584]{1,0:T(8,128)(2,1)S(1)}, bf16[40,3584]{1,0:T(8,128)(2,1)S(1)}, u32[]{:S(2)}, u32[]{:S(2)}) collective-permute-start(bf16[40,3584]{1,0:T(8,128)(2,1)S(1)} %pad_maximum_fusion.refs_0_), channel_id=1, source_target_pairs={{0,5},{1,4},{2,7},{3,6},{4,1},{5,0},{6,3},{7,2},{8,13},{9,12},{10,... | collective-permute-start | bytes 860168 | tf_op jit(solution)/shard_map/ppermute | solution.py:59
  143.9 17.6 %collective-permute-start.42 = (bf16[40,3584]{1,0:T(8,128)(2,1)S(1)}, bf16[40,3584]{1,0:T(8,128)(2,1)}, u32[]{:S(2)}, u32[]{:S(2)}) collective-permute-start(bf16[40,3584]{1,0:T(8,128)(2,1)S(1)} %pad_maximum_fusion.refs_0_), channel_id=1, source_target_pairs={{0,2},{1,3},{2,0},{3,1},{4,6},{5,7},{6,4},{7,5},{8,10},{9,11},{10,... | collective-permute-start | bytes 860168 | tf_op jit(solution)/shard_map/ppermute | solution.py:59
  150.2 11.4 %collective-permute-start.43 = (bf16[40,3584]{1,0:T(8,128)(2,1)S(1)}, bf16[40,3584]{1,0:T(8,128)(2,1)}, u32[]{:S(2)}, u32[]{:S(2)}) collective-permute-start(bf16[40,3584]{1,0:T(8,128)(2,1)S(1)} %collective-permute-done.39.refs_1_), channel_id=1, source_target_pairs={{0,2},{1,3},{2,0},{3,1},{4,6},{5,7},{6,4},{7,5},{8,10},{9,11},{10,... | collective-permute-start | bytes 860168 | tf_op jit(solution)/shard_map/ppermute | solution.py:59
  150.2 11.4 %collective-permute-start.44 = (bf16[40,3584]{1,0:T(8,128)(2,1)S(1)}, bf16[40,3584]{1,0:T(8,128)(2,1)}, u32[]{:S(2)}, u32[]{:S(2)}) collective-permute-start(bf16[40,3584]{1,0:T(8,128)(2,1)S(1)} %collective-permute-done.40.refs_2_), channel_id=1, source_target_pairs={{0,2},{1,3},{2,0},{3,1},{4,6},{5,7},{6,4},{7,5},{8,10},{9,11},{10,... | collective-permute-start | bytes 860168 | tf_op jit(solution)/shard_map/ppermute | solution.py:59
  153.7 7.9 %collective-permute-start.45 = (bf16[40,3584]{1,0:T(8,128)(2,1)S(1)}, bf16[40,3584]{1,0:T(8,128)(2,1)}, u32[]{:S(2)}, u32[]{:S(2)}) collective-permute-start(bf16[40,3584]{1,0:T(8,128)(2,1)S(1)} %collective-permute-done.41.refs_3_), channel_id=1, source_target_pairs={{0,2},{1,3},{2,0},{3,1},{4,6},{5,7},{6,4},{7,5},{8,10},{9,11},{10,... | collective-permute-start | bytes 860168 | tf_op jit(solution)/shard_map/ppermute | solution.py:59
  (24 other events, 202.7 us)

commit v3 on v2

--- a/solution.py
+++ b/solution.py
@@ -261,13 +261,12 @@
 
 def filter_kernel(rows, cols, grad_hid, acts, query_grad, out_grad, kept, sent, whole, pair, wide):
     channels, cells = grad_hid.shape
-    for t in range(0, 9, 2):
-        taps = [t, t + 1] if t < 8 else [t]
-        for k, tap in enumerate(taps):
-            a, b = tap // 3, tap % 3
-            pair[k * channels : (k + 1) * channels, :] = acts[b, :, a * cols : a * cols + cells]
-        span = len(taps) * channels
-        whole[:, t * channels : t * channels + span] = product(grad_hid[...], pair[:span, :], (1, 1))
+    for k in range(9):
+        a, b = k // 3, k % 3
+        pair[k * channels : (k + 1) * channels, :] = acts[b, :, a * cols : a * cols + cells]
+    for k in range(0, 9 * channels, 256):
+        ends = min(k + 256, 9 * channels)
+        whole[:, k:ends] = product(grad_hid[...], pair[k:ends, :], (1, 1))
     edge = 9 * channels
     base = edge // 128 * 128
     lead = edge - base
@@ -375,7 +374,7 @@
         [grad_hid, acts, query_grad, out_grad],
         [
             pltpu.VMEM((channels, width), F32),
-            pltpu.VMEM((2 * channels, cells), BF16),
+            pltpu.VMEM((9 * channels, cells), BF16),
             pltpu.VMEM((channels, -(-channels // 128) * 128), F32),
         ],
         flops=18 * channels * channels * cells,

time: 169 us -> 169 us (level)
  transfers between devices with their start and end apart: 46 -> 46, of which waited for: 23 -> 24; matrix products, arithmetic and copies ran while one was open for 3% -> 3% of each run, Pallas kernels for 11% -> 10%
where the time goes in v3:
time: 169 us; the launch traced here: 168 us
  waiting for transfers between devices  81.8 us (48%)
  starting transfers between devices  47 us (28%)
  Pallas kernels  29.2 us (17%)
  local copies, waits for them, and re-layouts  3.79 us (2%)
  matrix products  3.06 us (2%)
  between operations  2.52 us (1%)
    ppermute x45, waiting for transfers between devices, swap(): return lax.ppermute(block, GRID, [(i, i ^ mask) for i in range(total)])  81.8 us
    ppermute x45, starting transfers between devices, swap(): return lax.ppermute(block, GRID, [(i, i ^ mask) for i in range(total)])  45.4 us
    pallas_call x9, Pallas kernels, call(): pl.pallas_call(kernel, out_shape=[x if k in leave else pltpu.VMEM(x.shape...  16.5 us
    pallas_call x2, Pallas kernels, join_step(): pl.pallas_call(functools.partial(join_kernel, flip), out_shape=jax.ShapeD...  4.32 us
    pallas_call x1, Pallas kernels, shards(): pl.pallas_call(functools.partial(condition_kernel, rows), out_shape=[jax....  4.06 us
    unnamed x25, local copies, waits for them, and re-layouts  3.44 us
  transfers between devices with their start and end apart: 46, of which 24 were waited for; matrix products, arithmetic and copies ran while one was open for 3% of the time, Pallas kernels for 10%

profile of v3, /device:TPU:0, one launch (start us, length us, event | category | flops | bytes accessed | tf_op | source)
XLA Modules:
  0.0 168.5 jit_solution(14403951682640291741)
XLA Ops:
  1.3 4.1 %condition.1 = (f32[32,640]{1,0:T(8,128)}, f32[32,640]{1,0:T(8,128)}, bf16[64,1664]{1,0:T(8,128)(2,1)}, bf16[64,1664]{1,0:T(8,128)(2,1)}) custom-call(s32[1]{0:T(128)S(6)} %copy.32.start, bf16[512,3328]{1,0:T(8,128)(2,1)} %hidden.1, bf16[3328,640]{1,0:T(8,128)(2,1)} %weight.3), custom_call_target="tpu_custom_call" | custom-call | flops 272629760 | bytes 5537792 | tf_op jit(solution)/shard_map/condition/pallas_call | solution.py:538
  5.4 3.1 %collective-permute-start.1 = (f32[32,640]{1,0:T(8,128)}, f32[32,640]{1,0:T(8,128)S(1)}, u32[]{:S(2)}, u32[]{:S(2)}) collective-permute-start(f32[32,640]{1,0:T(8,128)} %get-tuple-element.49), channel_id=1, source_target_pairs={{0,1},{1,0},{2,3},{3,2},{4,5},{5,4},{6,7},{7,6},{8,9},{9,8},{10,11... | collective-permute-start | bytes 245768 | tf_op jit(solution)/shard_map/ppermute | solution.py:59
  9.2 1.9 %collective-permute-done.1 = f32[32,640]{1,0:T(8,128)S(1)} collective-permute-done((f32[32,640]{1,0:T(8,128)}, f32[32,640]{1,0:T(8,128)S(1)}, u32[]{:S(2)}, u32[]{:S(2)}) %collective-permute-start.1) | collective-permute-done | bytes 81952 | tf_op jit(solution)/shard_map/ppermute | solution.py:59
  12.0 2.1 %collective-permute-start.2 = (bf16[32,640]{1,0:T(8,128)(2,1)S(1)}, bf16[32,640]{1,0:T(8,128)(2,1)S(1)}, u32[]{:S(2)}, u32[]{:S(2)}) collective-permute-start(bf16[32,640]{1,0:T(8,128)(2,1)S(1)} %add_convert_fusion.2.refs_0_), channel_id=1, source_target_pairs={{0,8},{1,9},{2,10},{3,11},{4,12},{5,13},{6,14},{7,15},{8,0},{9,1},... | collective-permute-start | bytes 122888 | tf_op jit(solution)/shard_map/ppermute | solution.py:59
  14.1 2.6 %collective-permute-start.3 = (bf16[32,640]{1,0:T(8,128)(2,1)S(1)}, bf16[32,640]{1,0:T(8,128)(2,1)S(1)}, u32[]{:S(2)}, u32[]{:S(2)}) collective-permute-start(bf16[32,640]{1,0:T(8,128)(2,1)S(1)} %add_convert_fusion.2.refs_0_), channel_id=1, source_target_pairs={{0,16},{1,17},{2,18},{3,19},{4,20},{5,21},{6,22},{7,23},{8,24},{9,... | collective-permute-start | bytes 122888 | tf_op jit(solution)/shard_map/ppermute | solution.py:59
  17.0 2.9 %collective-permute-done.3.refs_2_ = bf16[32,640]{1,0:T(8,128)(2,1)S(1)} collective-permute-done((bf16[32,640]{1,0:T(8,128)(2,1)S(1)}, bf16[32,640]{1,0:T(8,128)(2,1)S(1)}, u32[]{:S(2)}, u32[]{:S(2)}) %collective-permute-start.3) | collective-permute-done | bytes 40992 | tf_op jit(solution)/shard_map/ppermute | solution.py:59
  19.9 2.6 %collective-permute-done.4.refs_3_ = bf16[32,640]{1,0:T(8,128)(2,1)S(1)} collective-permute-done((bf16[32,640]{1,0:T(8,128)(2,1)S(1)}, bf16[32,640]{1,0:T(8,128)(2,1)S(1)}, u32[]{:S(2)}, u32[]{:S(2)}) %collective-permute-start.4) | collective-permute-done | bytes 40992 | tf_op jit(solution)/shard_map/ppermute | solution.py:59
  30.0 4.2 %shard_map.164 = (bf16[3,320,1280]{2,1,0:T(8,128)(2,1)S(1)}, bf16[320,1024]{1,0:T(8,128)(2,1)S(1)}, bf16[320,1024]{1,0:T(8,128)(2,1)S(1)}) custom-call(f32[4,8,128]{2,1,0:T(8,128)S(1)} %get-tuple-element.46.noisy, bf16[4,2,128]{2,1,0:T(2,128)(2,1)S(1)} %collective-permute-done.refs_0_, f32[320,1]{1,0:T(8,128)S(1)} %copy.20.refs_1_, ...), custom_call_target="tpu_custom_call" | custom-call | flops 2097152000 | bytes 5859072 | tf_op jit(solution)/shard_map/pallas_call | solution.py:35
  34.3 3.8 %shard_map.166 = (bf16[320,1024]{1,0:T(8,128)(2,1)S(1)}, f32[32,640]{1,0:T(8,128)S(1)}, bf16[320,1024]{1,0:T(8,128)(2,1)S(1)}, f32[320,320]{1,0:T(8,128)S(1)}, f...) custom-call(bf16[320,1024]{1,0:T(8,128)(2,1)S(1)} %get-tuple-element.52.query, ...), custom_call_target="tpu_custom_call" | custom-call | flops 1300234240 | bytes 4710400 | tf_op jit(solution)/shard_map/pallas_call | solution.py:35
  38.7 3.5 %collective-permute-done.10 = bf16[32,640]{1,0:T(8,128)(2,1)S(1)} collective-permute-done((bf16[32,640]{1,0:T(8,128)(2,1)S(1)}, bf16[32,640]{1,0:T(8,128)(2,1)S(1)}, u32[]{:S(2)}, u32[]{:S(2)}) %collective-permute-start.10) | collective-permute-done | bytes 40992 | tf_op jit(solution)/shard_map/ppermute | solution.py:59
  43.2 3.4 %collective-permute-start.13 = (bf16[32,640]{1,0:T(8,128)(2,1)S(1)}, bf16[32,640]{1,0:T(8,128)(2,1)S(1)}, u32[]{:S(2)}, u32[]{:S(2)}) collective-permute-start(bf16[32,640]{1,0:T(8,128)(2,1)S(1)} %add_convert_fusion), channel_id=1, source_target_pairs={{0,24},{1,25},{2,26},{3,27},{4,28},{5,29},{6,30},{7,31},{8,16},{9,... | collective-permute-start | bytes 122888 | tf_op jit(solution)/shard_map/ppermute | solution.py:59
  52.9 2.7 %collective-permute-done.14.refs_1_ = bf16[4,32,640]{2,1,0:T(8,128)(2,1)S(1)} collective-permute-done((bf16[4,32,640]{2,1,0:T(8,128)(2,1)S(1)}, bf16[4,32,640]{2,1,0:T(8,128)(2,1)S(1)}, u32[]{:S(2)}, u32[]{:S(2)}) %collective-permute-start.14) | collective-permute-done | bytes 163872 | tf_op jit(solution)/shard_map/ppermute | solution.py:59
  58.2 2.9 %shard_map.167 = (f32[4,40,3584]{2,1,0:T(8,128)S(1)}, bf16[4,40,3584]{2,1,0:T(8,128)(2,1)S(1)}) custom-call(bf16[320,1024]{1,0:T(8,128)(2,1)S(1)} %get-tuple-element.60.grad_hid, bf16[3,320,1280]{2,1,0:T(8,128)(2,1)S(1)} %get-tuple-element.61.acts, f32[320,320]{1,0:T(8,128)S(1)} %get-tuple-element.62.query_grad, f32[320,320]{1,0:T(8,128)S(1)} %get-tuple-element.63.out_grad), custom_call_target="tpu_custom_call" | custom-call | flops 1887436800 | bytes 7372800 | tf_op jit(solution)/shard_map/pallas_call | solution.py:35
  61.2 3.4 %collective-permute-start.24 = (bf16[128,1664]{1,0:T(8,128)(2,1)S(1)}, bf16[128,1664]{1,0:T(8,128)(2,1)S(1)}, u32[]{:S(2)}, u32[]{:S(2)}) collective-permute-start(bf16[128,1664]{1,0:T(8,128)(2,1)S(1)} %get-tuple-element.88), channel_id=1, source_target_pairs={{0,24},{1,25},{2,26},{3,27},{4,28},{5,29},{6,30},{7,31},{8,16},{9,... | collective-permute-start | bytes 1277960 | tf_op jit(solution)/shard_map/ppermute | solution.py:59
  66.4 20.4 %collective-permute-done.23 = bf16[128,1664]{1,0:T(8,128)(2,1)S(1)} collective-permute-done((bf16[128,1664]{1,0:T(8,128)(2,1)S(1)}, bf16[128,1664]{1,0:T(8,128)(2,1)S(1)}, u32[]{:S(2)}, u32[]{:S(2)}) %collective-permute-start.23) | collective-permute-done | bytes 426016 | tf_op jit(solution)/shard_map/ppermute | solution.py:59
  89.0 6.0 %collective-permute-done.27 = bf16[128,1664]{1,0:T(8,128)(2,1)S(1)} collective-permute-done((bf16[128,1664]{1,0:T(8,128)(2,1)S(1)}, bf16[128,1664]{1,0:T(8,128)(2,1)S(1)}, u32[]{:S(2)}, u32[]{:S(2)}) %collective-permute-start.27) | collective-permute-done | bytes 426016 | tf_op jit(solution)/shard_map/ppermute | solution.py:59
  97.3 2.2 %collective-permute-done.26 = bf16[128,1664]{1,0:T(8,128)(2,1)S(1)} collective-permute-done((bf16[128,1664]{1,0:T(8,128)(2,1)S(1)}, bf16[128,1664]{1,0:T(8,128)(2,1)S(1)}, u32[]{:S(2)}, u32[]{:S(2)}) %collective-permute-start.26) | collective-permute-done | bytes 426016 | tf_op jit(solution)/shard_map/ppermute | solution.py:59
  99.5 3.6 %collective-permute-done.28 = bf16[128,1664]{1,0:T(8,128)(2,1)S(1)} collective-permute-done((bf16[128,1664]{1,0:T(8,128)(2,1)S(1)}, bf16[128,1664]{1,0:T(8,128)(2,1)S(1)}, u32[]{:S(2)}, u32[]{:S(2)}) %collective-permute-start.28) | collective-permute-done | bytes 426016 | tf_op jit(solution)/shard_map/ppermute | solution.py:59
  109.5 4.8 %collective-permute-done.30.refs_1_ = bf16[40,3584]{1,0:T(8,128)(2,1)S(1)} collective-permute-done((bf16[40,3584]{1,0:T(8,128)(2,1)S(1)}, bf16[40,3584]{1,0:T(8,128)(2,1)S(1)}, u32[]{:S(2)}, u32[]{:S(2)}) %collective-permute-start.30) | collective-permute-done | bytes 286752 | tf_op jit(solution)/shard_map/ppermute | solution.py:59
  115.3 6.3 %collective-permute-done.32.refs_3_ = bf16[40,3584]{1,0:T(8,128)(2,1)S(1)} collective-permute-done((bf16[40,3584]{1,0:T(8,128)(2,1)S(1)}, bf16[40,3584]{1,0:T(8,128)(2,1)S(1)}, u32[]{:S(2)}, u32[]{:S(2)}) %collective-permute-start.32) | collective-permute-done | bytes 286752 | tf_op jit(solution)/shard_map/ppermute | solution.py:59
  122.6 3.4 %collective-permute-start.34 = (bf16[40,896]{1,0:T(8,128)(2,1)S(1)}, bf16[40,896]{1,0:T(8,128)(2,1)S(1)}, u32[]{:S(2)}, u32[]{:S(2)}) collective-permute-start(bf16[40,896]{1,0:T(8,128)(2,1)S(1)} %get-tuple-element.81), channel_id=1, source_target_pairs={{0,16},{1,17},{2,18},{3,19},{4,20},{5,21},{6,22},{7,23},{8,24},{9,... | collective-permute-start | bytes 215048 | tf_op jit(solution)/shard_map/ppermute | solution.py:59
  126.8 3.8 %collective-permute-done.34 = bf16[40,896]{1,0:T(8,128)(2,1)S(1)} collective-permute-done((bf16[40,896]{1,0:T(8,128)(2,1)S(1)}, bf16[40,896]{1,0:T(8,128)(2,1)S(1)}, u32[]{:S(2)}, u32[]{:S(2)}) %collective-permute-start.34) | collective-permute-done | bytes 71712 | tf_op jit(solution)/shard_map/ppermute | solution.py:59
  132.3 2.1 %collective-permute-start.37 = (bf16[40,896]{1,0:T(8,128)(2,1)S(1)}, bf16[40,896]{1,0:T(8,128)(2,1)S(1)}, u32[]{:S(2)}, u32[]{:S(2)}) collective-permute-start(bf16[40,896]{1,0:T(8,128)(2,1)S(1)} %multiply_convert_fusion.1), channel_id=1, source_target_pairs={{0,16},{1,17},{2,18},{3,19},{4,20},{5,21},{6,22},{7,23},{8,24},{9,... | collective-permute-start | bytes 215048 | tf_op jit(solution)/shard_map/ppermute | solution.py:59
  134.4 2.2 %collective-permute-start.38 = (bf16[40,896]{1,0:T(8,128)(2,1)S(1)}, bf16[40,896]{1,0:T(8,128)(2,1)S(1)}, u32[]{:S(2)}, u32[]{:S(2)}) collective-permute-start(bf16[40,896]{1,0:T(8,128)(2,1)S(1)} %multiply_convert_fusion.1), channel_id=1, source_target_pairs={{0,24},{1,25},{2,26},{3,27},{4,28},{5,29},{6,30},{7,31},{8,16},{9,... | collective-permute-start | bytes 215048 | tf_op jit(solution)/shard_map/ppermute | solution.py:59
  136.7 2.3 %collective-permute-done.37 = bf16[40,896]{1,0:T(8,128)(2,1)S(1)} collective-permute-done((bf16[40,896]{1,0:T(8,128)(2,1)S(1)}, bf16[40,896]{1,0:T(8,128)(2,1)S(1)}, u32[]{:S(2)}, u32[]{:S(2)}) %collective-permute-start.37) | collective-permute-done | bytes 71712 | tf_op jit(solution)/shard_map/ppermute | solution.py:59
  144.1 6.2 %collective-permute-done.39.refs_1_ = bf16[40,3584]{1,0:T(8,128)(2,1)S(1)} collective-permute-done((bf16[40,3584]{1,0:T(8,128)(2,1)S(1)}, bf16[40,3584]{1,0:T(8,128)(2,1)S(1)}, u32[]{:S(2)}, u32[]{:S(2)}) %collective-permute-start.39) | collective-permute-done | bytes 286752 | tf_op jit(solution)/shard_map/ppermute | solution.py:59
  150.9 3.0 %collective-permute-done.41.refs_3_ = bf16[40,3584]{1,0:T(8,128)(2,1)S(1)} collective-permute-done((bf16[40,3584]{1,0:T(8,128)(2,1)S(1)}, bf16[40,3584]{1,0:T(8,128)(2,1)S(1)}, u32[]{:S(2)}, u32[]{:S(2)}) %collective-permute-start.41) | collective-permute-done | bytes 286752 | tf_op jit(solution)/shard_map/ppermute | solution.py:59
  153.9 1.8 %blank.1 = bf16[512,3328]{1,0:T(8,128)(2,1)} custom-call(), custom_call_target="tpu_custom_call" | custom-call | tf_op jit(solution)/shard_map/blank/pallas_call | solution.py:635
  155.8 2.2 %copy-done = bf16[3328,640]{1,0:T(8,128)(2,1)S(1)} copy-done((bf16[3328,640]{1,0:T(8,128)(2,1)S(1)}, bf16[3328,640]{1,0:T(8,128)(2,1)}, u32[]{:S(2)}) %copy-start) | copy-done | bytes 4259864
  158.0 2.4 %place.1 = bf16[512,3328]{1,0:T(8,128)(2,1)} custom-call(s32[1]{0:T(128)S(6)} %copy.32.start, bf16[64,640]{1,0:T(8,128)(2,1)S(1)} %bitcast.24, bf16[3328,640]{1,0:T(8,128)(2,1)S(1)} %copy-done, bf16[512,3328]{1,0:T(8,128)(2,1)} %blank.1), custom_call_target="tpu_custom_call", output_to_operand_aliasing={{}: (3, {})} | custom-call | tf_op jit(solution)/shard_map/place/pallas_call | solution.py:668
  161.8 3.5 %shard_map.173 = (bf16[9,320,320]{2,1,0:T(8,128)(2,1)}, bf16[320,320]{1,0:T(8,128)(2,1)}, bf16[320,320]{1,0:T(8,128)(2,1)}) custom-call(bf16[40,3584]{1,0:T(8,128)(2,1)S(1)} %pad_maximum_fusion.refs_0_, bf16[40,3584]{1,0:T(8,128)(2,1)S(1)} %collective-permute-done.39.refs_1_, bf16[40,3584]{1,0:T(8,128)(2,1)S(1)} %collective-permute-done.40.refs_2_, ...), custom_call_target="tpu_custom_call" | custom-call | bytes 4546560 | tf_op jit(solution)/shard_map/pallas_call | solution.py:35
  165.4 3.0 %shard_map.171 = bf16[3328,640]{1,0:T(8,128)(2,1)} custom-call(bf16[1664,640]{1,0:T(8,128)(2,1)} %collective-permute-done.29.part, bf16[3328,640]{1,0:T(8,128)(2,1)} %shard_map.170.refs_0_), custom_call_target="tpu_custom_call", output_to_operand_aliasing={{}: (1, {})} | custom-call | tf_op jit(solution)/shard_map/pallas_call | solution.py:472
  (115 shorter events, 43.4 us)
Async XLA Ops:
  14.1 5.8 %collective-permute-start.3 = (bf16[32,640]{1,0:T(8,128)(2,1)S(1)}, bf16[32,640]{1,0:T(8,128)(2,1)S(1)}, u32[]{:S(2)}, u32[]{:S(2)}) collective-permute-start(bf16[32,640]{1,0:T(8,128)(2,1)S(1)} %add_convert_fusion.2.refs_0_), channel_id=1, source_target_pairs={{0,16},{1,17},{2,18},{3,19},{4,20},{5,21},{6,22},{7,23},{8,24},{9,... | collective-permute-start | bytes 122888 | tf_op jit(solution)/shard_map/ppermute | solution.py:59
  16.7 5.8 %collective-permute-start.4 = (bf16[32,640]{1,0:T(8,128)(2,1)S(1)}, bf16[32,640]{1,0:T(8,128)(2,1)S(1)}, u32[]{:S(2)}, u32[]{:S(2)}) collective-permute-start(bf16[32,640]{1,0:T(8,128)(2,1)S(1)} %add_convert_fusion.2.refs_0_), channel_id=1, source_target_pairs={{0,24},{1,25},{2,26},{3,27},{4,28},{5,29},{6,30},{7,31},{8,16},{9,... | collective-permute-start | bytes 122888 | tf_op jit(solution)/shard_map/ppermute | solution.py:59
  28.4 5.8 %collective-permute-start.8 = (bf16[32,640]{1,0:T(8,128)(2,1)S(1)}, bf16[32,640]{1,0:T(8,128)(2,1)S(1)}, u32[]{:S(2)}, u32[]{:S(2)}) collective-permute-start(bf16[32,640]{1,0:T(8,128)(2,1)S(1)} %add_convert_fusion.1.refs_0_), channel_id=1, source_target_pairs={{0,1},{1,0},{2,3},{3,2},{4,5},{5,4},{6,7},{7,6},{8,9},{9,8},{10,11... | collective-permute-start | bytes 122888 | tf_op jit(solution)/shard_map/ppermute | solution.py:59
  38.7 14.0 %collective-permute-start.21 = (bf16[64,1664]{1,0:T(8,128)(2,1)S(1)}, bf16[64,1664]{1,0:T(8,128)(2,1)S(1)}, u32[]{:S(2)}, u32[]{:S(2)}) collective-permute-start(bf16[64,1664]{1,0:T(8,128)(2,1)S(1)} %copy-done.9), channel_id=1, source_target_pairs={{0,2},{1,3},{2,0},{3,1},{4,6},{5,7},{6,4},{7,5},{8,10},{9,11},{10,... | collective-permute-start | bytes 638984 | tf_op jit(solution)/shard_map/ppermute | solution.py:59
  43.2 5.8 %collective-permute-start.13 = (bf16[32,640]{1,0:T(8,128)(2,1)S(1)}, bf16[32,640]{1,0:T(8,128)(2,1)S(1)}, u32[]{:S(2)}, u32[]{:S(2)}) collective-permute-start(bf16[32,640]{1,0:T(8,128)(2,1)S(1)} %add_convert_fusion), channel_id=1, source_target_pairs={{0,24},{1,25},{2,26},{3,27},{4,28},{5,29},{6,30},{7,31},{8,16},{9,... | collective-permute-start | bytes 122888 | tf_op jit(solution)/shard_map/ppermute | solution.py:59
  49.1 6.5 %collective-permute-start.14 = (bf16[4,32,640]{2,1,0:T(8,128)(2,1)S(1)}, bf16[4,32,640]{2,1,0:T(8,128)(2,1)S(1)}, u32[]{:S(2)}, u32[]{:S(2)}) collective-permute-start(bf16[4,32,640]{2,1,0:T(8,128)(2,1)S(1)} %pad_maximum_fusion.1.refs_0_), channel_id=1, source_target_pairs={{0,1},{1,0},{2,3},{3,2},{4,5},{5,4},{6,7},{7,6},{8,9},{9,8},{10,11... | collective-permute-start | bytes 491528 | tf_op jit(solution)/shard_map/ppermute | solution.py:59
  49.7 7.0 %collective-permute-start.15 = (bf16[4,32,640]{2,1,0:T(8,128)(2,1)S(1)}, bf16[4,32,640]{2,1,0:T(8,128)(2,1)S(1)}, u32[]{:S(2)}, u32[]{:S(2)}) collective-permute-start(bf16[4,32,640]{2,1,0:T(8,128)(2,1)S(1)} %pad_maximum_fusion.1.refs_0_), channel_id=1, source_target_pairs={{0,4},{1,5},{2,6},{3,7},{4,0},{5,1},{6,2},{7,3},{8,12},{9,13},{10,... | collective-permute-start | bytes 491528 | tf_op jit(solution)/shard_map/ppermute | solution.py:59
  51.1 6.6 %collective-permute-start.16 = (bf16[4,32,640]{2,1,0:T(8,128)(2,1)S(1)}, bf16[4,32,640]{2,1,0:T(8,128)(2,1)S(1)}, u32[]{:S(2)}, u32[]{:S(2)}) collective-permute-start(bf16[4,32,640]{2,1,0:T(8,128)(2,1)S(1)} %pad_maximum_fusion.1.refs_0_), channel_id=1, source_target_pairs={{0,5},{1,4},{2,7},{3,6},{4,1},{5,0},{6,3},{7,2},{8,13},{9,12},{10,... | collective-permute-start | bytes 491528 | tf_op jit(solution)/shard_map/ppermute | solution.py:59
  52.7 35.0 %collective-permute-start.22 = (bf16[128,1664]{1,0:T(8,128)(2,1)S(1)}, bf16[128,1664]{1,0:T(8,128)(2,1)S(1)}, u32[]{:S(2)}, u32[]{:S(2)}) collective-permute-start(bf16[128,1664]{1,0:T(8,128)(2,1)S(1)} %get-tuple-element.88), channel_id=1, source_target_pairs={{0,8},{1,9},{2,10},{3,11},{4,12},{5,13},{6,14},{7,15},{8,0},{9,1},... | collective-permute-start | bytes 1277960 | tf_op jit(solution)/shard_map/ppermute | solution.py:59
  55.6 31.3 %collective-permute-start.23 = (bf16[128,1664]{1,0:T(8,128)(2,1)S(1)}, bf16[128,1664]{1,0:T(8,128)(2,1)S(1)}, u32[]{:S(2)}, u32[]{:S(2)}) collective-permute-start(bf16[128,1664]{1,0:T(8,128)(2,1)S(1)} %get-tuple-element.88), channel_id=1, source_target_pairs={{0,16},{1,17},{2,18},{3,19},{4,20},{5,21},{6,22},{7,23},{8,24},{9,... | collective-permute-start | bytes 1277960 | tf_op jit(solution)/shard_map/ppermute | solution.py:59
  57.7 7.0 %collective-permute-start.20 = (bf16[4,32,640]{2,1,0:T(8,128)(2,1)S(1)}, bf16[4,32,640]{2,1,0:T(8,128)(2,1)S(1)}, u32[]{:S(2)}, u32[]{:S(2)}) collective-permute-start(bf16[4,32,640]{2,1,0:T(8,128)(2,1)S(1)} %collective-permute-done.16.refs_3_), channel_id=1, source_target_pairs={{0,2},{1,3},{2,0},{3,1},{4,6},{5,7},{6,4},{7,5},{8,10},{9,11},{10,... | collective-permute-start | bytes 491528 | tf_op jit(solution)/shard_map/ppermute | solution.py:59
  61.1 43.6 %collective-permute-start.9 = (bf16[4,40,3584]{2,1,0:T(8,128)(2,1)S(1)}, bf16[4,40,3584]{2,1,0:T(8,128)(2,1)S(1)}, u32[]{:S(2)}, u32[]{:S(2)}) collective-permute-start(bf16[4,40,3584]{2,1,0:T(8,128)(2,1)S(1)} %get-tuple-element.65), channel_id=1, source_target_pairs={{0,2},{1,3},{2,0},{3,1},{4,6},{5,7},{6,4},{7,5},{8,10},{9,11},{10,... | collective-permute-start | bytes 3440648 | tf_op jit(solution)/shard_map/ppermute | solution.py:59
  61.2 34.5 %collective-permute-start.24 = (bf16[128,1664]{1,0:T(8,128)(2,1)S(1)}, bf16[128,1664]{1,0:T(8,128)(2,1)S(1)}, u32[]{:S(2)}, u32[]{:S(2)}) collective-permute-start(bf16[128,1664]{1,0:T(8,128)(2,1)S(1)} %get-tuple-element.88), channel_id=1, source_target_pairs={{0,24},{1,25},{2,26},{3,27},{4,28},{5,29},{6,30},{7,31},{8,16},{9,... | collective-permute-start | bytes 1277960 | tf_op jit(solution)/shard_map/ppermute | solution.py:59
  64.6 32.7 %collective-permute-start.25 = (bf16[128,1664]{1,0:T(8,128)(2,1)S(1)}, bf16[128,1664]{1,0:T(8,128)(2,1)S(1)}, u32[]{:S(2)}, u32[]{:S(2)}) collective-permute-start(bf16[128,1664]{1,0:T(8,128)(2,1)S(1)} %get-tuple-element.88), channel_id=1, source_target_pairs={{0,4},{1,5},{2,6},{3,7},{4,0},{5,1},{6,2},{7,3},{8,12},{9,13},{10,... | collective-permute-start | bytes 1277960 | tf_op jit(solution)/shard_map/ppermute | solution.py:59
  86.8 8.1 %collective-permute-start.27 = (bf16[128,1664]{1,0:T(8,128)(2,1)S(1)}, bf16[128,1664]{1,0:T(8,128)(2,1)S(1)}, u32[]{:S(2)}, u32[]{:S(2)}) collective-permute-start(bf16[128,1664]{1,0:T(8,128)(2,1)S(1)} %collective-permute-done.23), channel_id=1, source_target_pairs={{0,4},{1,5},{2,6},{3,7},{4,0},{5,1},{6,2},{7,3},{8,12},{9,13},{10,... | collective-permute-start | bytes 1277960 | tf_op jit(solution)/shard_map/ppermute | solution.py:59
  87.6 11.9 %collective-permute-start.26 = (bf16[128,1664]{1,0:T(8,128)(2,1)S(1)}, bf16[128,1664]{1,0:T(8,128)(2,1)S(1)}, u32[]{:S(2)}, u32[]{:S(2)}) collective-permute-start(bf16[128,1664]{1,0:T(8,128)(2,1)S(1)} %collective-permute-done.22), channel_id=1, source_target_pairs={{0,4},{1,5},{2,6},{3,7},{4,0},{5,1},{6,2},{7,3},{8,12},{9,13},{10,... | collective-permute-start | bytes 1277960 | tf_op jit(solution)/shard_map/ppermute | solution.py:59
  95.0 8.1 %collective-permute-start.28 = (bf16[128,1664]{1,0:T(8,128)(2,1)S(1)}, bf16[128,1664]{1,0:T(8,128)(2,1)S(1)}, u32[]{:S(2)}, u32[]{:S(2)}) collective-permute-start(bf16[128,1664]{1,0:T(8,128)(2,1)S(1)} %collective-permute-done.27), channel_id=1, source_target_pairs={{0,8},{1,9},{2,10},{3,11},{4,12},{5,13},{6,14},{7,15},{8,0},{9,1},... | collective-permute-start | bytes 1277960 | tf_op jit(solution)/shard_map/ppermute | solution.py:59
  104.6 60.7 %collective-permute-start.29 = (bf16[1664,640]{1,0:T(8,128)(2,1)S(1)}, bf16[1664,640]{1,0:T(8,128)(2,1)}, u32[]{:S(2)}, u32[]{:S(2)}) collective-permute-start(bf16[1664,640]{1,0:T(8,128)(2,1)S(1)} %multiply_convert_fusion.part), channel_id=1, source_target_pairs={{0,2},{1,3},{2,0},{3,1},{4,6},{5,7},{6,4},{7,5},{8,10},{9,11},{10,... | collective-permute-start | bytes 6389768 | tf_op jit(solution)/shard_map/ppermute | solution.py:59
  105.0 9.3 %collective-permute-start.30 = (bf16[40,3584]{1,0:T(8,128)(2,1)S(1)}, bf16[40,3584]{1,0:T(8,128)(2,1)S(1)}, u32[]{:S(2)}, u32[]{:S(2)}) collective-permute-start(bf16[40,3584]{1,0:T(8,128)(2,1)S(1)} %get-tuple-element.76), channel_id=1, source_target_pairs={{0,1},{1,0},{2,3},{3,2},{4,5},{5,4},{6,7},{7,6},{8,9},{9,8},{10,11... | collective-permute-start | bytes 860168 | tf_op jit(solution)/shard_map/ppermute | solution.py:59
  105.6 9.7 %collective-permute-start.31 = (bf16[40,3584]{1,0:T(8,128)(2,1)S(1)}, bf16[40,3584]{1,0:T(8,128)(2,1)S(1)}, u32[]{:S(2)}, u32[]{:S(2)}) collective-permute-start(bf16[40,3584]{1,0:T(8,128)(2,1)S(1)} %get-tuple-element.77), channel_id=1, source_target_pairs={{0,4},{1,5},{2,6},{3,7},{4,0},{5,1},{6,2},{7,3},{8,12},{9,13},{10,... | collective-permute-start | bytes 860168 | tf_op jit(solution)/shard_map/ppermute | solution.py:59
  107.1 14.5 %collective-permute-start.32 = (bf16[40,3584]{1,0:T(8,128)(2,1)S(1)}, bf16[40,3584]{1,0:T(8,128)(2,1)S(1)}, u32[]{:S(2)}, u32[]{:S(2)}) collective-permute-start(bf16[40,3584]{1,0:T(8,128)(2,1)S(1)} %get-tuple-element.78), channel_id=1, source_target_pairs={{0,5},{1,4},{2,7},{3,6},{4,1},{5,0},{6,3},{7,2},{8,13},{9,12},{10,... | collective-permute-start | bytes 860168 | tf_op jit(solution)/shard_map/ppermute | solution.py:59
  122.6 7.9 %collective-permute-start.34 = (bf16[40,896]{1,0:T(8,128)(2,1)S(1)}, bf16[40,896]{1,0:T(8,128)(2,1)S(1)}, u32[]{:S(2)}, u32[]{:S(2)}) collective-permute-start(bf16[40,896]{1,0:T(8,128)(2,1)S(1)} %get-tuple-element.81), channel_id=1, source_target_pairs={{0,16},{1,17},{2,18},{3,19},{4,20},{5,21},{6,22},{7,23},{8,24},{9,... | collective-permute-start | bytes 215048 | tf_op jit(solution)/shard_map/ppermute | solution.py:59
  126.0 6.1 %collective-permute-start.35 = (bf16[40,896]{1,0:T(8,128)(2,1)S(1)}, bf16[40,896]{1,0:T(8,128)(2,1)S(1)}, u32[]{:S(2)}, u32[]{:S(2)}) collective-permute-start(bf16[40,896]{1,0:T(8,128)(2,1)S(1)} %get-tuple-element.82), channel_id=1, source_target_pairs={{0,24},{1,25},{2,26},{3,27},{4,28},{5,29},{6,30},{7,31},{8,16},{9,... | collective-permute-start | bytes 215048 | tf_op jit(solution)/shard_map/ppermute | solution.py:59
  132.3 6.7 %collective-permute-start.37 = (bf16[40,896]{1,0:T(8,128)(2,1)S(1)}, bf16[40,896]{1,0:T(8,128)(2,1)S(1)}, u32[]{:S(2)}, u32[]{:S(2)}) collective-permute-start(bf16[40,896]{1,0:T(8,128)(2,1)S(1)} %multiply_convert_fusion.1), channel_id=1, source_target_pairs={{0,16},{1,17},{2,18},{3,19},{4,20},{5,21},{6,22},{7,23},{8,24},{9,... | collective-permute-start | bytes 215048 | tf_op jit(solution)/shard_map/ppermute | solution.py:59
  134.4 6.1 %collective-permute-start.38 = (bf16[40,896]{1,0:T(8,128)(2,1)S(1)}, bf16[40,896]{1,0:T(8,128)(2,1)S(1)}, u32[]{:S(2)}, u32[]{:S(2)}) collective-permute-start(bf16[40,896]{1,0:T(8,128)(2,1)S(1)} %multiply_convert_fusion.1), channel_id=1, source_target_pairs={{0,24},{1,25},{2,26},{3,27},{4,28},{5,29},{6,30},{7,31},{8,16},{9,... | collective-permute-start | bytes 215048 | tf_op jit(solution)/shard_map/ppermute | solution.py:59
  140.6 9.8 %collective-permute-start.39 = (bf16[40,3584]{1,0:T(8,128)(2,1)S(1)}, bf16[40,3584]{1,0:T(8,128)(2,1)S(1)}, u32[]{:S(2)}, u32[]{:S(2)}) collective-permute-start(bf16[40,3584]{1,0:T(8,128)(2,1)S(1)} %pad_maximum_fusion.refs_0_), channel_id=1, source_target_pairs={{0,1},{1,0},{2,3},{3,2},{4,5},{5,4},{6,7},{7,6},{8,9},{9,8},{10,11... | collective-permute-start | bytes 860168 | tf_op jit(solution)/shard_map/ppermute | solution.py:59
  141.2 9.2 %collective-permute-start.40 = (bf16[40,3584]{1,0:T(8,128)(2,1)S(1)}, bf16[40,3584]{1,0:T(8,128)(2,1)S(1)}, u32[]{:S(2)}, u32[]{:S(2)}) collective-permute-start(bf16[40,3584]{1,0:T(8,128)(2,1)S(1)} %pad_maximum_fusion.refs_0_), channel_id=1, source_target_pairs={{0,4},{1,5},{2,6},{3,7},{4,0},{5,1},{6,2},{7,3},{8,12},{9,13},{10,... | collective-permute-start | bytes 860168 | tf_op jit(solution)/shard_map/ppermute | solution.py:59
  142.5 11.4 %collective-permute-start.41 = (bf16[40,3584]{1,0:T(8,128)(2,1)S(1)}, bf16[40,3584]{1,0:T(8,128)(2,1)S(1)}, u32[]{:S(2)}, u32[]{:S(2)}) collective-permute-start(bf16[40,3584]{1,0:T(8,128)(2,1)S(1)} %pad_maximum_fusion.refs_0_), channel_id=1, source_target_pairs={{0,5},{1,4},{2,7},{3,6},{4,1},{5,0},{6,3},{7,2},{8,13},{9,12},{10,... | collective-permute-start | bytes 860168 | tf_op jit(solution)/shard_map/ppermute | solution.py:59
  144.1 17.6 %collective-permute-start.42 = (bf16[40,3584]{1,0:T(8,128)(2,1)S(1)}, bf16[40,3584]{1,0:T(8,128)(2,1)}, u32[]{:S(2)}, u32[]{:S(2)}) collective-permute-start(bf16[40,3584]{1,0:T(8,128)(2,1)S(1)} %pad_maximum_fusion.refs_0_), channel_id=1, source_target_pairs={{0,2},{1,3},{2,0},{3,1},{4,6},{5,7},{6,4},{7,5},{8,10},{9,11},{10,... | collective-permute-start | bytes 860168 | tf_op jit(solution)/shard_map/ppermute | solution.py:59
  150.4 11.4 %collective-permute-start.43 = (bf16[40,3584]{1,0:T(8,128)(2,1)S(1)}, bf16[40,3584]{1,0:T(8,128)(2,1)}, u32[]{:S(2)}, u32[]{:S(2)}) collective-permute-start(bf16[40,3584]{1,0:T(8,128)(2,1)S(1)} %collective-permute-done.39.refs_1_), channel_id=1, source_target_pairs={{0,2},{1,3},{2,0},{3,1},{4,6},{5,7},{6,4},{7,5},{8,10},{9,11},{10,... | collective-permute-start | bytes 860168 | tf_op jit(solution)/shard_map/ppermute | solution.py:59
  150.4 11.4 %collective-permute-start.44 = (bf16[40,3584]{1,0:T(8,128)(2,1)S(1)}, bf16[40,3584]{1,0:T(8,128)(2,1)}, u32[]{:S(2)}, u32[]{:S(2)}) collective-permute-start(bf16[40,3584]{1,0:T(8,128)(2,1)S(1)} %collective-permute-done.40.refs_2_), channel_id=1, source_target_pairs={{0,2},{1,3},{2,0},{3,1},{4,6},{5,7},{6,4},{7,5},{8,10},{9,11},{10,... | collective-permute-start | bytes 860168 | tf_op jit(solution)/shard_map/ppermute | solution.py:59
  153.9 7.9 %collective-permute-start.45 = (bf16[40,3584]{1,0:T(8,128)(2,1)S(1)}, bf16[40,3584]{1,0:T(8,128)(2,1)}, u32[]{:S(2)}, u32[]{:S(2)}) collective-permute-start(bf16[40,3584]{1,0:T(8,128)(2,1)S(1)} %collective-permute-done.41.refs_3_), channel_id=1, source_target_pairs={{0,2},{1,3},{2,0},{3,1},{4,6},{5,7},{6,4},{7,5},{8,10},{9,11},{10,... | collective-permute-start | bytes 860168 | tf_op jit(solution)/shard_map/ppermute | solution.py:59
  (24 other events, 202.6 us)
